TPU v7x, 32 devices: a whole 2x2x4 slice. The times are simulated.
32 devices in a mesh: fsdp: 4 (over y, core), ctx: 8 (over z, x).
Axes of the slice: x: 2, y: 2, z: 4, core: 2. Of those that a mesh axis runs over, the one named last changes fastest.
Arguments:
- stream_in: bfloat16 [8192, 767], P(('fsdp', 'ctx')), as said below
- gain_attn: bfloat16 [768], P('fsdp'), may hold values from 0.5 to 1.5
- w_qkv: bfloat16 [768, 2304], P('fsdp'), may hold values from -0.3125 to 0.3125
- bias_qv: bfloat16 [1536], P('fsdp'), may hold values from -4 to 4
- w_out: bfloat16 [768, 768], P('fsdp'), may hold values from -2 to 2
- bias_out: bfloat16 [768], P('fsdp'), may hold values from -4 to 4
- gain_mlp: bfloat16 [768], P('fsdp'), may hold values from 0.5 to 1.5
- w_up: bfloat16 [768, 3072], P('fsdp'), may hold values from -0.21875 to 0.21875
- bias_up: bfloat16 [3072], P('fsdp'), may hold values from -4 to 4
- w_down: bfloat16 [3072, 768], P('fsdp'), may hold values from -0.109375 to 0.109375
- bias_down: bfloat16 [768], P('fsdp'), may hold values from -4 to 4
- grad_out: bfloat16 [8192, 767], P(('fsdp', 'ctx')), may hold values from -6 to 6
Outputs:
- stream_out: bfloat16 [8192, 767], P(('fsdp', 'ctx'))
- grad_stream: float32 [8192, 767], P(('fsdp', 'ctx'))
- grad_gain_attn: float32 [768], P('fsdp')
- grad_w_qkv: float32 [768, 2304], P('fsdp')
- grad_bias_qv: float32 [1536], P('fsdp')
- grad_w_out: float32 [768, 768], P('fsdp')
- grad_bias_out: float32 [768], P('fsdp')
- grad_gain_mlp: float32 [768], P('fsdp')
- grad_w_up: float32 [768, 3072], P('fsdp')
- grad_bias_up: float32 [3072], P('fsdp')
- grad_w_down: float32 [3072, 768], P('fsdp')
- grad_bias_down: float32 [768], P('fsdp')
Inputs may be any that keep to these rules, and one draw needn't show every extreme that they name: `stream_in`: every row is the first 767 entries of a zero-mean row of 768 entries, given as differences of neighbouring entries of a random row.
All inputs are finite; a program needn't handle non-finite values.
Results may differ from a plain program's by a relative error of at most 0.018.
Values may be sent and summed in bfloat16 or wider, within the bound.
No kernel may reach another device: no remote copies, remote signals or barrier semaphores. Data moves between devices by JAX's collectives and lax.ppermute only.
A program may use at most 192 MiB of HBM per device.

v0:
```python
import jax
import jax.numpy as jnp
from jax import lax
from jax.experimental import pallas as pl
from jax.experimental.pallas import tpu as pltpu
from jax.sharding import PartitionSpec as P

D = 768
H = 12
HD = 64
HEAD_GROUPS = 4
GROUP_HEADS = H // HEAD_GROUPS
GROUP_COLS = GROUP_HEADS * HD
HEAD_SCALE = HD ** (-0.5)
NORM_EPS = 1e-05
NEG_BIG = -1e30
GELU_A = 0.7978845608028654
GELU_B = 0.044715
LANES = 128
PIECES = 8
EXTRA = 8
AXES = ("fsdp", "ctx")
VMEM_LIMIT = 120 << 19
UNROLL_BLOCKS = 8

f32 = jnp.float32
bf16 = jnp.bfloat16


def dot(left, right):
    return lax.dot_general(left, right, (((1,), (0,)), ((), ())), preferred_element_type=f32)


def dot_tn(left, right):
    return lax.dot_general(left, right, (((0,), (0,)), ((), ())), preferred_element_type=f32)


def dot_nt(left, right):
    return lax.dot_general(left, right, (((1,), (1,)), ((), ())), preferred_element_type=f32)


def centered(branch):
    return branch - jnp.mean(branch, axis=1, keepdims=True)


def inverse_rms(stream):
    return lax.rsqrt(jnp.mean(stream * stream, axis=1, keepdims=True) + NORM_EPS)


def norm_back(grad, unit, inverse):
    return inverse * (grad - unit * jnp.mean(grad * unit, axis=1, keepdims=True))


def slab_at(relative):
    return ((relative & 1) << 1) | (relative >> 1)


def loop(start, stop, body, carried):
    if isinstance(start, int) and isinstance(stop, int) and stop - start <= UNROLL_BLOCKS:
        for at in range(start, stop):
            carried = body(at, carried)
        return carried
    return lax.fori_loop(start, stop, body, carried)


def call(body, name, outs, args, flops=0, exps=0, scratch=(), **grid):
    moved = sum(x.size * x.dtype.itemsize for x in tuple(args) + tuple(outs))
    specs = dict(
        in_specs=[pl.BlockSpec(memory_space=pltpu.SMEM)]
        + [pl.BlockSpec(memory_space=pltpu.VMEM)] * (len(args) - 1),
        out_specs=tuple(pl.BlockSpec(memory_space=pltpu.VMEM) for _ in outs),
    )
    specs.update(grid)
    return pl.pallas_call(
        body,
        out_shape=tuple(outs),
        scratch_shapes=list(scratch),
        compiler_params=pltpu.CompilerParams(vmem_limit_bytes=VMEM_LIMIT),
        cost_estimate=pl.CostEstimate(flops=flops, bytes_accessed=moved, transcendentals=exps),
        name=name,
        **specs,
    )(*args)


def shape(dims, kind):
    return jax.ShapeDtypeStruct(tuple(dims), kind)


def norm_kernel(place, x_ref, resid_ref, unit_ref):
    x = x_ref[...].astype(f32)
    resid_ref[:, : D - 1] = x
    resid_ref[:, D - 1 :] = -jnp.sum(x, axis=1, keepdims=True)
    resid = resid_ref[...]
    unit_ref[0] = (resid * inverse_rms(resid)).astype(bf16)


def cut_kernel(place, qkv_ref, up_ref, heads_ref, *slabs):
    group = place[0] % HEAD_GROUPS
    for at in range(HEAD_GROUPS):

        @pl.when(group == at)
        def _():
            for kind in range(3):
                start = kind * D + at * GROUP_COLS
                heads_ref[:, kind * GROUP_COLS : (kind + 1) * GROUP_COLS] = qkv_ref[
                    :, start : start + GROUP_COLS
                ]

    hidden = slabs[0].shape[1]
    for distance, slab in enumerate(slabs):
        at = pl.multiple_of((distance ^ place[1]) * hidden, LANES)
        slab[...] = up_ref[:, pl.ds(at, hidden)]


def load_heads(place, slab_refs, wq, wkv):
    shard = slab_refs[0].shape[0]
    for distance, slab_ref in enumerate(slab_refs):
        at = pl.ds(pl.multiple_of((distance ^ place[1]) * shard, shard), shard)
        wq[at, :] = slab_ref[:, :GROUP_COLS]
        wkv[at, :] = slab_ref[:, GROUP_COLS:]


def project(place, normed_ref, slots, base, bias_ref, k_ref, v_ref, vt_ref, qt_ref, wq, wkv):
    rows, query_rows = normed_ref.shape[1], qt_ref.shape[2]
    own = pl.ds(pl.multiple_of(place[2] * query_rows, query_rows), query_rows)
    for start in range(0, slots, 2):
        pair = range(start, min(start + 2, slots))
        normed = jnp.concatenate([normed_ref[slot] for slot in pair], axis=0)
        both = dot(normed, wkv[...])
        keys, values = both[:, :GROUP_COLS], both[:, GROUP_COLS:] + bias_ref[1:2, :]
        mine = jnp.concatenate([normed_ref[slot, own, :] for slot in pair], axis=0)
        queries = (dot(mine, wq[...]) + bias_ref[0:1, :]) * HEAD_SCALE
        for at, slot in enumerate(pair):
            here = slice(at * rows, (at + 1) * rows)
            k_ref[slot] = keys[here].astype(bf16)
            v_ref[slot] = values[here].astype(bf16)
            vt_ref[:, slot * rows : (slot + 1) * rows] = values[here].T.astype(bf16)
            qt_ref[slot] = queries[at * query_rows : (at + 1) * query_rows].T.astype(bf16)


def project_kernel(place, *refs):
    slabs, (gain_ref, bias_ref) = refs[:4], refs[4:6]
    pieces = refs[6:-7]
    normed_ref, k_ref, v_ref, vt_ref, qt_ref, wq, wkv = refs[-7:]
    load_heads(place, slabs, wq, wkv)
    gain = gain_ref[...]
    slot = 0
    for ref in pieces:
        for at in range(ref.shape[0]):
            normed_ref[slot] = (ref[at].astype(f32) * gain).astype(bf16)
            slot += 1
    project(place, normed_ref, slot, 0, bias_ref, k_ref, v_ref, vt_ref, qt_ref, wq, wkv)


def project_block_kernel(place, *refs):
    slabs, bias_ref, normed_ref = refs[:4], refs[4], refs[5]
    k_ref, v_ref, vt_ref, qt_ref, wq, wkv = refs[6:]

    @pl.when(pl.program_id(0) == 0)
    def _():
        load_heads(place, slabs, wq, wkv)

    slots = normed_ref.shape[0]
    project(place, normed_ref, slots, 0, bias_ref, k_ref, v_ref, vt_ref, qt_ref, wq, wkv)


def collect_kernel(place, normed_ref, k_ref, normed_t_ref, query_t_ref, kt_ref):
    blocks, rows, _ = k_ref.shape
    query_rows = query_t_ref.shape[1] // blocks
    own = pl.ds(pl.multiple_of(place[2] * query_rows, query_rows), query_rows)
    for slot in range(blocks):
        tokens = slice(slot * rows, (slot + 1) * rows)
        normed_t_ref[:, tokens] = normed_ref[slot].T
        query_t_ref[:, slot * query_rows : (slot + 1) * query_rows] = normed_ref[slot, own, :].T
        kt_ref[:, tokens] = k_ref[slot].T


def by_head(value):
    head = lax.broadcasted_iota(jnp.int32, value.shape, 0) // HD
    zero = jnp.zeros_like(value)
    return jnp.concatenate([jnp.where(head == at, value, zero) for at in range(GROUP_HEADS)], axis=1)


def attend_kernel(place, qt_ref, k_ref, vt_ref, out_ref, log_ref):
    blocks, _, width = qt_ref.shape
    rows = k_ref.shape[1]
    member = place[0]

    def one_query_block(block, _):
        queries = by_head(qt_ref[block ^ member])

        def one_key_block(key_block, carried):
            top, total, accs = carried
            slot = key_block ^ member
            at = pl.multiple_of(slot * rows, rows)
            scores = dot(k_ref[slot], queries)
            new_top = jnp.maximum(top, jnp.max(scores, axis=0, keepdims=True))
            weights = jnp.exp(scores - new_top)
            fading = jnp.exp(top - new_top)
            total = total * fading + jnp.sum(weights, axis=0, keepdims=True)
            low = weights.astype(bf16)
            kept = []
            for head in range(GROUP_HEADS):
                lanes = slice(head * width, (head + 1) * width)
                values = vt_ref[head * HD : (head + 1) * HD, pl.ds(at, rows)]
                kept.append(accs[head] * fading[:, lanes] + dot(values, low[:, lanes]))
            return new_top, total, tuple(kept)

        start_state = (
            jnp.full((1, GROUP_HEADS * width), NEG_BIG, f32),
            jnp.zeros((1, GROUP_HEADS * width), f32),
            tuple(jnp.zeros((HD, width), f32) for _ in range(GROUP_HEADS)),
        )
        top, total, accs = loop(0, block + 1, one_key_block, start_state)
        for head in range(GROUP_HEADS):
            lanes = slice(head * width, (head + 1) * width)
            out_ref[block, head * HD : (head + 1) * HD, :] = (accs[head] / total[:, lanes]).astype(bf16)
        log_ref[block] = top + jnp.log(total)
        return 0

    loop(0, blocks, one_query_block, 0)


def attend_back_kernel(
    place, qt_ref, k_ref, v_ref, kt_ref, gt_ref, out_ref, log_ref, dq_ref, dkv_ref, sum_ref, dk_acc, dv_acc, dq_acc, delta_ref
):
    blocks, _, width = qt_ref.shape
    rows = k_ref.shape[1]
    member = place[0]

    def prepare(block, _):
        products = gt_ref[block].astype(f32) * out_ref[block].astype(f32)
        for head in range(GROUP_HEADS):
            delta_ref[block, :, head * width : (head + 1) * width] = jnp.sum(
                products[head * HD : (head + 1) * HD], axis=0, keepdims=True
            )
        return 0

    lax.fori_loop(0, blocks, prepare, 0)
    dq_acc[...] = jnp.zeros_like(dq_acc)
    sum_ref[...] = jnp.zeros_like(sum_ref)

    def one_key_block(key_block, _):
        slot = key_block ^ member
        at = pl.multiple_of(slot * rows, rows)
        dk_acc[...] = jnp.zeros_like(dk_acc)
        dv_acc[...] = jnp.zeros_like(dv_acc)

        def one_query_block(block, _):
            queries, grads = by_head(qt_ref[block ^ member]), by_head(gt_ref[block])
            prob = jnp.exp(dot(k_ref[slot], queries) - log_ref[block])
            grad_prob = dot(v_ref[slot], grads)
            grad_scores = (prob * (grad_prob - delta_ref[block])).astype(bf16)
            dv_acc[...] += dot_nt(prob.astype(bf16), grads)
            dk_acc[...] += dot_nt(grad_scores, queries)
            for head in range(GROUP_HEADS):
                part = slice(head * HD, (head + 1) * HD)
                lanes = slice(head * width, (head + 1) * width)
                dq_acc[block, part, :] += dot(kt_ref[part, pl.ds(at, rows)], grad_scores[:, lanes])
            return 0

        loop(key_block, blocks, one_query_block, 0)
        dkv_ref[slot] = jnp.concatenate([dk_acc[...], dv_acc[...]], axis=1).astype(bf16)
        sum_ref[1:2, :] += jnp.sum(dv_acc[...], axis=0, keepdims=True)
        return 0

    loop(0, blocks, one_key_block, 0)

    def write(block, _):
        grads = dq_acc[block].T * HEAD_SCALE
        dq_ref[block ^ member] = grads.astype(bf16)
        sum_ref[0:1, :] += jnp.sum(grads, axis=0, keepdims=True)
        return 0

    lax.fori_loop(0, blocks, write, 0)


def middle_kernel(
    place, att_ref, resid_ref, vec_ref, slab0, slab1, slab2, slab3, middle_ref, normed_ref, branch
):
    query_rows = att_ref.shape[2]
    for split in range(att_ref.shape[0] // HEAD_GROUPS):
        total = None
        for distance, slab_ref in enumerate((slab0, slab1, slab2, slab3)):
            part = dot_tn(att_ref[split * HEAD_GROUPS + (distance ^ place[1])], slab_ref[...])
            total = part if total is None else total + part
        branch[split * query_rows : (split + 1) * query_rows, :] = total
    middle = resid_ref[...] + centered(branch[...] + vec_ref[1:2, :])
    middle_ref[...] = middle
    normed_ref[...] = (middle * inverse_rms(middle) * vec_ref[2:3, :]).astype(bf16)


def mlp_kernel(place, *refs):
    normed, grads, slabs = refs[:4], refs[4:8], refs[8:12]
    down_ref, bias_ref = refs[12:14]
    branch_own, branch_far, branch_give, norm_own, norm_far, norm_give = refs[14:20]
    downs, ups, (bias_grad, weight, down_total, up_total) = refs[20:24], refs[24:28], refs[28:]
    rows = normed[0].shape[0]
    shard, wide = slabs[0].shape[0], down_ref.shape[0] // PIECES
    piece = shard // PIECES
    mine, low = place[1], place[3]
    for distance, slab in enumerate(slabs):
        at = pl.multiple_of((distance ^ mine) * shard, shard)
        weight[pl.ds(at, shard), :] = slab[...]
    for tile in range(2):
        blocks = (tile, 2 + tile)
        tokens = jnp.concatenate([normed[at][...] for at in blocks], axis=0)
        grad = jnp.concatenate([grads[at][...] for at in blocks], axis=0)
        hidden = dot(tokens, weight[...]) + bias_ref[...]
        square = hidden * hidden
        bent = jnp.tanh(GELU_A * hidden * (1.0 + GELU_B * square))
        half = 0.5 * (1.0 + bent)
        active = (hidden * half).astype(bf16)
        slope = half + 0.5 * hidden * (1.0 - bent * bent) * (GELU_A * (1.0 + 3.0 * GELU_B * square))
        grad_hidden = (dot_nt(grad, down_ref[...]) * slope).astype(bf16)
        norm, branch = dot_nt(grad_hidden, weight[...]), dot(active, down_ref[...])
        for at in range(2):
            here = slice(at * rows, (at + 1) * rows)
            if tile:
                norm_give[at], branch_give[at] = norm[here].astype(bf16), branch[here].astype(bf16)
            else:
                (norm_own, norm_far)[at][...] = norm[here]
                (branch_own, branch_far)[at][...] = branch[here]
        down, up = dot_tn(active, grad), dot_tn(tokens, grad_hidden)
        bias = jnp.sum(grad_hidden.astype(f32), axis=0, keepdims=True)
        if tile == 0:
            down_total[...], up_total[...], bias_grad[...] = down, up, bias
        else:
            down_total[...] += down
            up_total[...] += up
            bias_grad[...] += bias
    for near, (down_ref, up_ref) in enumerate(zip(downs, ups)):
        for side in range(2):
            at = (side << 2 | near) ^ low
            down_ref[side] = down_total[pl.ds(pl.multiple_of(at * wide, wide), wide), :].astype(bf16)
            for distance in range(4):
                here = pl.multiple_of((distance ^ mine) * shard + at * piece, piece)
                up_ref[side, distance] = up_total[pl.ds(here, piece), :].astype(bf16)


def branch_back_kernel(
    place,
    own_ref,
    core_ref,
    far_ref,
    middle_ref,
    top_ref,
    vec_ref,
    slab0,
    slab1,
    slab2,
    slab3,
    grad_middle_ref,
    grad_branch_ref,
    ga_ref,
    sum_ref,
):
    query_rows = ga_ref.shape[2]
    rows = top_ref.shape[0]
    grad = own_ref[...] + core_ref[0].astype(f32) + far_ref[...].astype(f32)
    middle = middle_ref[...]
    inverse = inverse_rms(middle)
    unit = middle * inverse
    sum_ref[0:1, :] = jnp.sum(grad * unit, axis=0, keepdims=True)
    grad_top = jnp.concatenate([top_ref[...].astype(f32), jnp.zeros((rows, 1), f32)], axis=1)
    grad_middle = grad_top + norm_back(grad * vec_ref[2:3, :], unit, inverse)
    grad_middle_ref[...] = grad_middle
    grad_branch = centered(grad_middle).astype(bf16)
    grad_branch_ref[...] = grad_branch
    for distance, slab_ref in enumerate((slab0, slab1, slab2, slab3)):
        product = dot_nt(slab_ref[...], grad_branch).astype(bf16)
        for split in range(ga_ref.shape[0] // HEAD_GROUPS):
            at = split * HEAD_GROUPS + (distance ^ place[1])
            ga_ref[at] = product[:, split * query_rows : (split + 1) * query_rows]
    sum_ref[1:2, :] = jnp.sum(grad_branch.astype(f32), axis=0, keepdims=True)
    sum_ref[2:3, :] = jnp.sum(centered(grad_top).astype(bf16).astype(f32), axis=0, keepdims=True)


def out_back_kernel(place, att_ref, grad_ref, sum_ref, bias_up_ref, near_ref, far_ref, grad_w):
    query_rows = att_ref.shape[2]
    groups, piece = HEAD_GROUPS, near_ref.shape[2] - EXTRA
    shard = D // groups
    mine, low = place[1], place[3]
    empty = jnp.zeros((1, D - 3 * shard), f32)
    for group in range(groups):
        weight = None
        for split in range(att_ref.shape[0] // groups):
            product = dot(
                att_ref[split * groups + group], grad_ref[split * query_rows : (split + 1) * query_rows, :]
            )
            weight = product if weight is None else weight + product
        lanes = slice(group * shard, (group + 1) * shard)
        grad_w[group * shard : (group + 1) * shard, :] = weight
        row = [sum_ref[at : at + 1, lanes] for at in (1, 0, 2)]
        grad_w[D + group : D + group + 1, :] = jnp.concatenate(row + [empty], axis=1)
    for distance in range(4):
        far, core = distance >> 1, distance & 1
        row = grad_w[pl.ds(D + (distance ^ mine), 1), :]
        up_row = jnp.zeros_like(row) if distance else bias_up_ref[...]
        extra = jnp.concatenate([row, up_row, jnp.zeros((EXTRA - 2, D), f32)], axis=0)
        for near in range(4):
            for side in range(2):
                at = (distance ^ mine) * shard + ((side << 2 | near) ^ low) * piece
                part = grad_w[pl.ds(pl.multiple_of(at, piece), piece), :]
                target = (near_ref, far_ref)[core]
                target[far, near * 2 + side] = jnp.concatenate([part, extra], axis=0).astype(bf16)


def sum_kernel(place, *refs):
    firsts, seconds, targets = refs[:4], refs[4:8], refs[8:]
    wide = firsts[0].shape[1]
    for side, target in enumerate(targets):
        target[:wide, :] = sum(ref[side].astype(f32) for ref in firsts).astype(bf16)
        target[wide:, :] = sum(ref[side].astype(f32) for ref in seconds).astype(bf16)


def arrange_heads(place, q_ref, kv_ref, sum_ref, near_ref, far_ref):
    mine, piece = place[1], near_ref.shape[2] - EXTRA
    shard = 2 * piece
    group = place[0] % HEAD_GROUPS
    for row in range(D // shard):
        relative = row ^ mine
        first = jnp.where(group // 2 == row, sum_ref[0:1, :], 0.0)
        second = jnp.where(2 + group // 2 == row, sum_ref[1:2, :], 0.0)
        extra = jnp.concatenate([first, second, jnp.zeros_like(first)], axis=1)
        extra = jnp.concatenate([extra, jnp.zeros((EXTRA - 1, extra.shape[1]), f32)], axis=0)
        for part in range(2):
            at_row = slice(row * shard + part * piece, row * shard + (part + 1) * piece)
            block = jnp.concatenate([q_ref[at_row, :], kv_ref[at_row, :]], axis=1)
            both = jnp.concatenate([block, extra], axis=0).astype(bf16)
            for core, target in enumerate((near_ref, far_ref)):

                @pl.when((relative & 1) == core)
                def _():
                    target[relative >> 1, part ^ ((place[3] >> 2) & 1)] = both


def project_back_kernel(
    place,
    normed_t_ref,
    query_t_ref,
    dq_ref,
    dkv_ref,
    sum_ref,
    slab0,
    slab1,
    slab2,
    slab3,
    keep_ref,
    give_ref,
    near_ref,
    far_ref,
    wq,
    wkv,
    aq,
    akv,
):
    load_heads(place, (slab0, slab1, slab2, slab3), wq, wkv)
    blocks, query_rows, _ = dq_ref.shape
    rows = dkv_ref.shape[1]
    half = keep_ref.shape[0]
    own = pl.ds(pl.multiple_of(place[2] * query_rows, query_rows), query_rows)
    aq[...] = jnp.zeros_like(aq)
    akv[...] = jnp.zeros_like(akv)
    chunk = min(blocks, max(4, LANES // query_rows))

    def one(at, _):
        start = at * chunk
        dkv = jnp.concatenate([dkv_ref[start + k] for k in range(chunk)], axis=0)
        dq = jnp.concatenate([dq_ref[start + k] for k in range(chunk)], axis=0)
        tokens = pl.ds(pl.multiple_of(start * rows, chunk * rows), chunk * rows)
        queries = pl.ds(pl.multiple_of(start * query_rows, chunk * query_rows), chunk * query_rows)
        akv[...] += dot(normed_t_ref[:, tokens], dkv)
        aq[...] += dot(query_t_ref[:, queries], dq)
        return 0

    loop(0, blocks // chunk, one, 0)
    arrange_heads(place, aq, akv, sum_ref, near_ref, far_ref)

    for core, ref in enumerate((keep_ref, give_ref)):

        def two(at, _, core=core, ref=ref):
            slot = at + core * half
            grad = dot_nt(dkv_ref[slot], wkv[...])
            ref[at] = grad.astype(bf16)
            low = ref[at, own, :].astype(f32)
            ref[at, own, :] = (low + dot_nt(dq_ref[slot], wq[...])).astype(bf16)
            return 0

        loop(0, half, two, 0)


def stream_back_kernel(place, part0, part1, part2, part3, resid_ref, grad_middle_ref, vec_ref, out_ref):
    grad = sum(part[...].astype(f32) for part in (part0, part1, part2, part3))
    resid = resid_ref[...]
    inverse = inverse_rms(resid)
    unit = resid * inverse
    total = grad_middle_ref[...] + norm_back(grad * vec_ref[0:1, :], unit, inverse)
    out_ref[...] = (total - total[:, D - 1 :]).astype(bf16)[:, : D - 1]


def down_out_kernel(place, part0, part1, part2, part3, down_ref, out_ref):
    wide, rows = down_ref.shape[0] // PIECES, out_ref.shape[0] // PIECES
    for near, part in enumerate((part0, part1, part2, part3)):
        for side in range(2):
            at = (side << 2 | near) ^ place[3]
            down_ref[pl.ds(pl.multiple_of(at * wide, wide), wide), :] = part[side, :wide].astype(f32)
            out_ref[pl.ds(pl.multiple_of(at * rows, rows), rows), :] = part[side, wide:].astype(f32)


def up_out_kernel(place, part0, part1, part2, part3, up_ref):
    rows = part0.shape[2]
    for near, part in enumerate((part0, part1, part2, part3)):
        for side in range(2):
            at = pl.multiple_of(((side << 2 | near) ^ place[3]) * rows, rows)
            for slab in range(4):
                col = pl.multiple_of((slab ^ place[1]) * D, LANES)
                up_ref[pl.ds(at, rows), pl.ds(col, D)] = part[side, slab].astype(f32)


def heads_out_kernel(place, part0, part1, part2, part3, weight_ref, out_ref, gain_ref, bias_ref, pieces):
    piece = part0.shape[1] - EXTRA
    mine, low = place[1], place[3]
    for near, part in enumerate((part0, part1, part2, part3)):
        pieces[near] = part[...]
    for part in range(2):
        for group in range(HEAD_GROUPS):
            value = pieces[(group ^ low) & 3, part ^ ((low >> 2) & 1)].astype(f32)
            for kind in range(3):
                start = kind * D + group * GROUP_COLS
                out_ref[part * piece : (part + 1) * piece, start : start + GROUP_COLS] = value[
                    :piece, kind * GROUP_COLS : (kind + 1) * GROUP_COLS
                ]
    gain_ref[...] = jnp.sum(out_ref[...] * weight_ref[...].astype(f32), axis=1, keepdims=True)
    sides = []
    for side in range(2):
        group = ((2 * mine) & 3) + side
        value = pieces[(group ^ low) & 3, 0].astype(f32)[piece : piece + 1]
        sides.append(jnp.where(mine < 2, value[:, :GROUP_COLS], value[:, GROUP_COLS : 2 * GROUP_COLS]))
    bias_ref[...] = jnp.concatenate(sides, axis=1)


def solution(mesh):
    fsdp_count, ctx_count = mesh.shape["fsdp"], mesh.shape["ctx"]
    half = ctx_count // 2
    steps = half.bit_length() - 1
    ctx_steps = steps + 1
    splits = ctx_count // HEAD_GROUPS
    shard = D // fsdp_count

    def send(value, target):
        pairs = []
        for source in range(fsdp_count * ctx_count):
            row, at = target(*divmod(source, ctx_count))
            pairs.append((source, row * ctx_count + at))
        return lax.ppermute(value, AXES, pairs)

    def to_core(value):
        return send(value, lambda row, at: (row ^ 1, at))

    def to_chip_row(value):
        return send(value, lambda row, at: (row ^ 2, at))

    def to_ctx(value, bit):
        return send(value, lambda row, at: (row, at ^ bit))

    def swap_sequences(value):
        return send(
            value, lambda row, at: (row, at) if (row & 1) == at // half else (row ^ 1, at ^ half)
        )

    groups = [
        [(row + core) * ctx_count + side * half + at for core in range(2) for at in range(half)]
        for row in range(0, fsdp_count, 2)
        for side in range(2)
    ]

    def group_all_to_all(value):
        return lax.all_to_all(value, AXES, 0, 0, axis_index_groups=groups, tiled=True)

    def to_fsdp(value, distance):
        return send(value, lambda row, at: (row ^ distance, at))

    def over_fsdp(value):
        far = to_chip_row(value)
        return value, to_core(value), far, to_core(far)

    def to_square(values):
        return tuple(to_ctx(value, near + 1) for near, value in enumerate(values))

    def gather_square(value):
        pair = jnp.stack([value, to_ctx(value, 4)])
        return (pair, *to_square((pair,) * 3))

    def over_rest(value):
        for step in range(3, ctx_steps):
            value = value + to_ctx(value, 1 << step)
        return value

    together = lax.optimization_barrier

    def widened(value):
        width = value.shape[-1]
        return value if width >= LANES else jnp.pad(value, ((0, 0), (0, 0), (0, LANES - width)))

    def local(
        stream_in,
        gain_attn,
        w_qkv,
        bias_qv,
        w_out,
        bias_out,
        gain_mlp,
        w_up,
        bias_up,
        w_down,
        bias_down,
        grad_out,
    ):
        rows = stream_in.shape[0]
        query_rows = rows // splits
        width = max(query_rows, LANES)
        fsdp_at, ctx_at = lax.axis_index("fsdp"), lax.axis_index("ctx")
        core, inner = fsdp_at & 1, ctx_at % half
        member = core * half + inner
        head_group = inner % HEAD_GROUPS
        place = jnp.stack([member, fsdp_at, member // HEAD_GROUPS, ctx_at & 7]).astype(jnp.int32)

        hidden = w_down.shape[0]
        stream = swap_sequences(stream_in)
        w_part, *up_sent = call(
            cut_kernel,
            "cut",
            (
                shape((shard, 3 * GROUP_COLS), bf16),
                *(shape((shard, hidden), bf16) for _ in range(fsdp_count)),
            ),
            (place, w_qkv, w_up),
        )
        vectors = jnp.concatenate(
            [
                part.astype(f32).reshape(1, -1)
                for part in (gain_attn, bias_out, gain_mlp, bias_down, bias_qv, bias_up)
            ],
            axis=1,
        )
        far_heads, far_vectors = together((to_chip_row(w_part), to_chip_row(vectors)))
        w_heads = (w_part, to_core(w_part), far_heads, to_core(far_heads))
        vectors = (vectors, to_core(vectors), far_vectors, to_core(far_vectors))
        far_heads, w_out_sent, stream = together((far_heads, w_out, stream))

        resid, unit = call(
            norm_kernel,
            "norm",
            (shape((rows, D), f32), shape((1, rows, D), bf16)),
            (place, stream),
        )
        got = to_square((unit,) * 3)
        *got, out_far = together((*got, to_chip_row(w_out_sent)))
        pieces = [unit, *got]
        for bit in range(2, steps):
            pieces.append(to_ctx(jnp.concatenate(pieces), 1 << bit))
        pieces = pieces + [to_core(piece) for piece in pieces]

        def by_row(values):
            ordered = []
            for row in range(fsdp_count):
                first = jnp.where((fsdp_at ^ row) & 1 == 0, values[0], values[1])
                second = jnp.where((fsdp_at ^ row) & 1 == 0, values[2], values[3])
                ordered.append(jnp.where((fsdp_at ^ row) < 2, first, second))
            return jnp.concatenate(ordered)

        vectors = by_row(vectors)
        vec = vectors[:, :D].reshape(fsdp_count, 4, shard).transpose(1, 0, 2).reshape(4, D)
        bias_heads = vectors[:, D : D + 2 * shard].reshape(2, HEAD_GROUPS, GROUP_COLS)
        bias_heads = lax.dynamic_index_in_dim(bias_heads, head_group, 1, keepdims=False)
        bias_hidden = lax.dynamic_slice_in_dim(vectors[:, D + 2 * shard :], fsdp_at, 1)
        gain = vec[0:1]

        head_weights = [pltpu.VMEM((D, GROUP_COLS), bf16), pltpu.VMEM((D, 2 * GROUP_COLS), bf16)]
        tokens = ctx_count * rows
        projected = (
            shape((ctx_count, rows, GROUP_COLS), bf16),
            shape((ctx_count, rows, GROUP_COLS), bf16),
            shape((GROUP_COLS, tokens), bf16),
            shape((ctx_count, GROUP_COLS, query_rows), bf16),
        )
        work = 5 * tokens * D * GROUP_COLS
        if 4 * tokens * D * 2 < VMEM_LIMIT:
            normed, keys, values, values_t, queries_t = call(
                project_kernel,
                "project",
                (shape((ctx_count, rows, D), bf16), *projected),
                (place, *w_heads, gain, bias_heads, *pieces),
                flops=work,
                scratch=head_weights,
            )
        else:
            normed = (jnp.concatenate(pieces).astype(f32) * gain).astype(bf16)
            block = lambda *dims: pl.BlockSpec((1,) + dims, lambda at: (at, 0, 0))
            whole = lambda *dims: pl.BlockSpec(dims, lambda at: (0,) * len(dims))
            keys, values, values_t, queries_t = call(
                project_block_kernel,
                "project",
                projected,
                (place, *w_heads, bias_heads, normed),
                flops=work,
                scratch=head_weights,
                grid=(ctx_count,),
                in_specs=[pl.BlockSpec(memory_space=pltpu.SMEM)]
                + [whole(shard, 3 * GROUP_COLS)] * 4
                + [whole(2, GROUP_COLS), block(rows, D)],
                out_specs=(
                    block(rows, GROUP_COLS),
                    block(rows, GROUP_COLS),
                    pl.BlockSpec((GROUP_COLS, rows), lambda at: (0, at)),
                    block(GROUP_COLS, query_rows),
                ),
            )
        queries_t = widened(queries_t)
        pairs = GROUP_HEADS * query_rows * rows * ctx_count * (ctx_count + 1) // 2
        outs, logs = call(
            attend_kernel,
            "attend",
            (
                shape((ctx_count, GROUP_COLS, width), bf16),
                shape((ctx_count, 1, GROUP_HEADS * width), f32),
            ),
            (place, queries_t, keys, values_t),
            flops=4 * HD * pairs,
            exps=pairs,
        )
        outs, *up_got = together(
            (outs, *(to_fsdp(up_sent[distance], distance) for distance in (1, 2, 3)))
        )
        attended = group_all_to_all(outs[:, :, :query_rows])
        if 4 * tokens * D * 2 < VMEM_LIMIT:
            normed_t, query_t, keys_t = call(
                collect_kernel,
                "collect",
                (
                    shape((D, tokens), bf16),
                    shape((D, ctx_count * query_rows), bf16),
                    shape((GROUP_COLS, tokens), bf16),
                ),
                (place, normed, keys),
            )
        else:
            normed_query = lax.dynamic_index_in_dim(
                normed.reshape(ctx_count, splits, query_rows, D), place[2], 1, keepdims=False
            )
            normed_t, query_t = normed.reshape(tokens, D).T, normed_query.reshape(-1, D).T
            keys_t = keys.reshape(tokens, GROUP_COLS).T
        attended, normed_t, query_t, keys_t = together((attended, normed_t, query_t, keys_t))

        w_out_all = (w_out, to_core(w_out), out_far, to_core(out_far))
        top = swap_sequences(grad_out)
        grad_result = jnp.pad(top.astype(f32), ((0, 0), (0, 1)))
        grad_branch_mlp = centered(grad_result).astype(bf16)
        grads_mlp = over_fsdp(grad_branch_mlp)
        middle, normed_mlp = call(
            middle_kernel,
            "middle",
            (shape((rows, D), f32), shape((rows, D), bf16)),
            (place, attended, resid, vec, *w_out_all),
            flops=2 * rows * D * D,
            scratch=[pltpu.VMEM((rows, D), f32)],
        )
        piece = shard // PIECES
        (
            branch_own,
            branch_far,
            branch_give,
            norm_own,
            norm_far,
            norm_give,
            *both_sums,
            bias_up_sum,
        ) = call(
            mlp_kernel,
            "mlp",
            (
                shape((rows, D), f32),
                shape((rows, D), f32),
                shape((2, rows, D), bf16),
                shape((rows, D), f32),
                shape((rows, D), f32),
                shape((2, rows, D), bf16),
                *(shape((2, hidden // PIECES, D), bf16) for _ in range(4)),
                *(shape((2, fsdp_count, piece, hidden), bf16) for _ in range(4)),
                shape((1, hidden), f32),
            ),
            (
                place,
                *over_fsdp(normed_mlp),
                *grads_mlp,
                up_sent[0],
                *up_got,
                w_down,
                bias_hidden,
            ),
            flops=48 * rows * D * hidden,
            exps=4 * rows * hidden,
            scratch=[
                pltpu.VMEM((D, hidden), bf16),
                pltpu.VMEM((hidden, D), f32),
                pltpu.VMEM((D, hidden), f32),
            ],
        )
        norm_got = to_core(norm_give)
        norm_far_got = to_chip_row((norm_far + norm_got[1]).astype(bf16))
        down_sums, up_sums = both_sums[:4], both_sums[4:]
        norm_far_got, *down_got = together((norm_far_got, *to_square(down_sums[1:])))
        down_keep, down_give = (
            sum((part[side] for part in down_got), start=down_sums[0][side]) for side in range(2)
        )
        grad_middle, grad_branch, grad_attended, row_sums = call(
            branch_back_kernel,
            "branch_back",
            (
                shape((rows, D), f32),
                shape((rows, D), bf16),
                shape((ctx_count, GROUP_COLS, query_rows), bf16),
                shape((8, D), f32),
            ),
            (place, norm_own, norm_got, norm_far_got, middle, top, vec, *w_out_all),
            flops=4 * rows * D * D,
        )
        grads = group_all_to_all(grad_attended)
        out_near, out_give = call(
            out_back_kernel,
            "out_back",
            (shape((2, PIECES, piece + EXTRA, D), bf16), shape((2, PIECES, piece + EXTRA, D), bf16)),
            (place, attended, grad_branch, row_sums, bias_up_sum),
            flops=2 * rows * D * D,
            scratch=[pltpu.VMEM((D + 8, D), f32)],
        )
        out_sum = out_near + to_core(out_give)
        branch_got = to_core(branch_give)
        branch_far_got = to_chip_row((branch_far + branch_got[1]).astype(bf16))
        branch_mlp = branch_own + branch_got[0] + branch_far_got + vec[3:4]
        stream_out = (middle + centered(branch_mlp)).astype(bf16)[:, : D - 1]
        grads, out_sum = together((grads, out_sum))
        out_got = to_chip_row(out_sum[1])
        up_got = to_square(up_sums[1:])
        down_got = to_ctx(down_give, 4)
        dq, dkv, head_sums = call(
            attend_back_kernel,
            "attend_back",
            (
                shape((ctx_count, width, GROUP_COLS), bf16),
                shape((ctx_count, rows, 2 * GROUP_COLS), bf16),
                shape((8, GROUP_COLS), f32),
            ),
            (place, queries_t, keys, values, keys_t, widened(grads), outs, logs),
            flops=10 * HD * pairs,
            exps=pairs,
            scratch=[
                pltpu.VMEM((rows, GROUP_COLS), f32),
                pltpu.VMEM((rows, GROUP_COLS), f32),
                pltpu.VMEM((ctx_count, GROUP_COLS, width), f32),
                pltpu.VMEM((ctx_count, 1, GROUP_HEADS * width), f32),
            ],
        )
        dq = dq[:, :query_rows]
        dq, dkv, out_got, down_got, *up_got = together((dq, dkv, out_got, down_got, *up_got))
        up_keep, up_give = (
            sum((part[side] for part in up_got), start=up_sums[0][side]) for side in range(2)
        )
        out_sums = [
            out_sum[0, 2 * near : 2 * near + 2] + out_got[2 * near : 2 * near + 2] for near in range(4)
        ]
        dq, dkv, up_give, *out_sums = together((dq, dkv, up_give, *out_sums))
        up_got = to_ctx(up_give, 4)
        out_got = to_square(out_sums[1:])

        row_shapes = (shape((half, rows, D), bf16), shape((half, rows, D), bf16))
        head_shapes = tuple(
            shape((2, 2, shard // 2 + EXTRA, 3 * GROUP_COLS), bf16) for _ in range(2)
        )
        if 4 * tokens * D * 2 < VMEM_LIMIT:
            keep_rows, give_rows, head_near, head_give = call(
                project_back_kernel,
                "project_back",
                row_shapes + head_shapes,
                (place, normed_t, query_t, dq, dkv, head_sums, *w_heads),
                flops=2 * work,
                scratch=head_weights
                + [pltpu.VMEM((D, GROUP_COLS), f32), pltpu.VMEM((D, 2 * GROUP_COLS), f32)],
            )
        else:
            weights = by_row(w_heads)
            flat_q, flat_kv = dq.reshape(-1, GROUP_COLS), dkv.reshape(tokens, 2 * GROUP_COLS)
            grad_rows = dot_nt(flat_kv, weights[:, GROUP_COLS:]).reshape(
                ctx_count, splits, query_rows, D
            )
            grad_query = dot_nt(flat_q, weights[:, :GROUP_COLS]).reshape(ctx_count, 1, query_rows, D)
            chosen = (jnp.arange(splits) == place[2])[None, :, None, None]
            grad_rows = (grad_rows + jnp.where(chosen, grad_query, 0.0)).astype(bf16)
            grad_rows = grad_rows.reshape(ctx_count, rows, D)
            keep_rows, give_rows = grad_rows[:half], grad_rows[half:]
            head_near, head_give = call(
                arrange_heads,
                "arrange_heads",
                head_shapes,
                (place, dot(query_t, flat_q), dot(normed_t, flat_kv), head_sums),
            )
        keep_rows, up_got, *out_got = together((keep_rows, up_got, *out_got))
        head_got, rows_got = together((to_core(head_give), to_core(give_rows)))
        head_sum = head_near + head_got
        head_got = to_chip_row(head_sum[1])
        if steps == 2:
            parts = [keep_rows[slot] + rows_got[slot] for slot in range(4)]
        else:
            both = keep_rows + rows_got
            for bit in reversed(range(2, steps)):
                both = both[: 1 << bit] + to_ctx(both[1 << bit :], 1 << bit)
            parts = [both[slot] for slot in range(4)]
        rows_got = to_square(parts[1:])
        out_keep, out_give = (
            sum((part[side] for part in out_got), start=out_sums[0][side]) for side in range(2)
        )
        out_got = to_ctx(out_give, 4)
        down, up_rows = over_rest(down_keep + down_got), over_rest(up_keep + up_got)
        up_got = [to_fsdp(up_rows[distance], distance) for distance in (1, 2, 3)]

        head_got, out_got, *up_got = together((head_got, out_got, *up_got))
        head_sum = head_sum[0] + head_got
        head_got = to_ctx(head_sum[1], 4)
        ups = jnp.stack([up_rows[0], *up_got])
        up_got = to_ctx(ups, 4)
        out_rows = over_rest(out_keep + out_got)
        sums = out_rows[piece:].astype(f32)
        downs = jnp.concatenate([down, out_rows[:piece]])
        down_got = to_ctx(downs, 4)

        *rows_got, head_got, up_got, down_got = together((*rows_got, head_got, up_got, down_got))
        (grad_stream,) = call(
            stream_back_kernel,
            "stream_back",
            (shape((rows, D - 1), bf16),),
            (place, parts[0], *rows_got, resid, grad_middle, vec),
        )
        grad_stream = swap_sequences(grad_stream)
        heads = over_rest(head_sum[0] + head_got)
        head_got = to_ctx(heads, 4)
        downs = jnp.stack([downs, down_got])
        downs = (downs, *to_square((downs,) * 3))
        ups = jnp.stack([ups, up_got])
        ups = (ups, *to_square((ups,) * 3))
        heads = jnp.stack([heads, head_got])
        heads = (heads, *to_square((heads,) * 3))
        grad_w_qkv, grad_gain_attn, grad_bias_qv = call(
            heads_out_kernel,
            "heads_out",
            (
                shape((shard, 3 * D), f32),
                shape((shard, 1), f32),
                shape((1, 2 * shard), f32),
            ),
            (place, *heads, w_qkv),
            scratch=[pltpu.VMEM((4, 2, shard // 2 + EXTRA, 3 * GROUP_COLS), bf16)],
        )
        grad_w_down, grad_w_out = call(
            down_out_kernel,
            "down_out",
            (shape((hidden, D), f32), shape((shard, D), f32)),
            (place, *downs),
        )
        (grad_w_up,) = call(
            up_out_kernel, "up_out", (shape((shard, fsdp_count * hidden), f32),), (place, *ups)
        )

        return (
            swap_sequences(stream_out),
            grad_stream.astype(f32),
            grad_gain_attn.reshape(-1) / gain_attn.astype(f32),
            grad_w_qkv,
            grad_bias_qv.reshape(-1),
            grad_w_out,
            sums[0, :shard],
            sums[0, shard : 2 * shard],
            grad_w_up,
            sums[1],
            grad_w_down,
            sums[0, 2 * shard : 3 * shard],
        )

    rows_spec, matrix_spec, vector_spec = P(AXES, None), P("fsdp", None), P("fsdp")
    return jax.shard_map(
        local,
        mesh=mesh,
        in_specs=(
            rows_spec,
            vector_spec,
            matrix_spec,
            vector_spec,
            matrix_spec,
            vector_spec,
            vector_spec,
            matrix_spec,
            vector_spec,
            matrix_spec,
            vector_spec,
            rows_spec,
        ),
        out_specs=(
            rows_spec,
            rows_spec,
            vector_spec,
            matrix_spec,
            vector_spec,
            matrix_spec,
            vector_spec,
            vector_spec,
            matrix_spec,
            vector_spec,
            matrix_spec,
            vector_spec,
        ),
        check_vma=False,
    )
```

profile of v0, /device:TPU:0, one launch (start us, length us, event | category | flops | bytes accessed | tf_op | source)
XLA Modules:
  0.0 311.6 jit_solution(18206473554720955158)
XLA Ops:
  19.0 3.0 collective-permute-start.9
  24.5 6.8 %collective-permute-done.10.slab2 = bf16[192,768]{1,0:T(8,128)(2,1)S(1)} collective-permute-done((bf16[192,768]{1,0:T(8,128)(2,1)S(1)}, bf16[192,768]{1,0:T(8,128)(2,1)S(1)}, u32[]{:S(2)}, u32[]{:S(2)}) %collective-permute-start.10) | collective-permute-done | bytes 294944 | tf_op jit(solution)/shard_map/ppermute | solution.py:556
  32.2 8.3 %collective-permute-done.8.refs_8_ = bf16[1,256,768]{2,1,0:T(8,128)(2,1)S(1)} collective-permute-done((bf16[1,256,768]{2,1,0:T(8,128)(2,1)}, bf16[1,256,768]{2,1,0:T(8,128)(2,1)S(1)}, u32[]{:S(2)}, u32[]{:S(2)}) %collective-permute-start.8) | collective-permute-done | bytes 393248 | tf_op jit(solution)/shard_map/ppermute | solution.py:556
  48.4 7.0 %project.1 = (bf16[8,256,768]{2,1,0:T(8,128)(2,1)}, bf16[8,256,192]{2,1,0:T(8,128)(2,1)}, bf16[8,256,192]{2,1,0:T(8,128)(2,1)}, bf16[192,2048]{1,0:T(8,128)(2,1)}, bf16[8,192,128]{2,1,0:T(8,128)(2,1)}) custom-call(s32[4]{0:T(128)} %pad_add_fusion.place, bf16[192,576]{1,0:T(8,128)(2,1)} %get-tuple-element.118.refs_0_.slab0, bf16[192,576]{1,0:T(8,128)(2,1)} %copy-done.58, ...), custom_call_target="tpu_custom_call" | custom-call | flops 1509949440 | bytes 9933328 | tf_op jit(solution)/shard_map/project/pallas_call | solution.py:74
  55.3 13.1 %attend.1 = (bf16[8,192,128]{2,1,0:T(8,128)(2,1)}, f32[8,1,384]{2,1,0:T(1,128)}) custom-call(s32[4]{0:T(128)} %pad_add_fusion.place, bf16[8,192,128]{2,1,0:T(8,128)(2,1)} %get-tuple-element.127.qt_ref, bf16[8,256,192]{2,1,0:T(8,128)(2,1)} %get-tuple-element.128.k_ref, bf16[192,2048]{1,0:T(8,128)(2,1)} %get-tuple-element.129.vt_ref), custom_call_target="tpu_custom_call" | custom-call | flops 905969664 | bytes 2371600 | tf_op jit(solution)/shard_map/attend/pallas_call | solution.py:74
  69.2 6.3 %all-to-all-start = ((bf16[8,192,128]{2,1,0:T(8,128)(2,1)}), bf16[8,192,128]{2,1,0:T(8,128)(2,1)S(1)}, u32[]{:S(2)}, u32[]{:S(2)}) async-start(bf16[8,192,128]{2,1,0:T(8,128)(2,1)} %get-tuple-element.134.out_ref), calls=%async_computation | async-start | bytes 786432 | tf_op jit(solution)/shard_map/all_to_all | solution.py:579
  78.7 6.2 %collect.1 = (bf16[768,2048]{1,0:T(8,128)(2,1)}, bf16[768,1024]{1,0:T(8,128)(2,1)}, bf16[192,2048]{1,0:T(8,128)(2,1)}) custom-call(s32[4]{0:T(128)} %pad_add_fusion.place, bf16[8,256,768]{2,1,0:T(8,128)(2,1)} %get-tuple-element.135.normed_ref, bf16[8,256,192]{2,1,0:T(8,128)(2,1)} %get-tuple-element.128.k_ref), custom_call_target="tpu_custom_call" | custom-call | bytes 9437200 | tf_op jit(solution)/shard_map/collect/pallas_call | solution.py:74
  85.8 3.5 %middle.1 = (f32[256,768]{1,0:T(8,128)}, bf16[256,768]{1,0:T(8,128)(2,1)}) custom-call(s32[4]{0:T(128)} %pad_add_fusion.place, bf16[8,192,128]{2,1,0:T(8,128)(2,1)} %copy-done.4, f32[256,768]{1,0:T(8,128)} %get-tuple-element.140.resid_ref, f32[4,768]{1,0:T(4,128)} %reshape.124.vec_ref, bf16[192,768]{1,0:T(8,128)(2,1)} %slab0.3, bf16[192,768]{1,0:T(8,128)(2,1)} %copy-done.9, ...), custom_call_target="tpu_custom_call" | custom-call | flops 301989888 | bytes 3551248 | tf_op jit(solution)/shard_map/middle/pallas_call | solution.py:74
  90.4 10.3 %collective-permute-done.21.refs_2_ = bf16[256,768]{1,0:T(8,128)(2,1)S(1)} collective-permute-done((bf16[256,768]{1,0:T(8,128)(2,1)}, bf16[256,768]{1,0:T(8,128)(2,1)S(1)}, u32[]{:S(2)}, u32[]{:S(2)}) %collective-permute-start.21) | collective-permute-done | bytes 393248 | tf_op jit(solution)/shard_map/ppermute | solution.py:556
  103.2 12.6 %mlp.1 = (f32[256,768]{1,0:T(8,128)}, f32[256,768]{1,0:T(8,128)}, bf16[2,256,768]{2,1,0:T(8,128)(2,1)}, f32[256,768]{1,0:T(8,128)}, f32[256,768]{1,0:T(8,128)}, ...) custom-call(s32[4]{0:T(128)} %pad_add_fusion.place, ...), custom_call_target="tpu_custom_call" | custom-call | flops 7247757312 | bytes 12589072 | tf_op jit(solution)/shard_map/mlp/pallas_call | solution.py:74
  124.0 5.6 %collective-permute-done.32 = bf16[2,96,768]{2,1,0:T(8,128)(2,1)} collective-permute-done((bf16[2,96,768]{2,1,0:T(8,128)(2,1)S(1)}, bf16[2,96,768]{2,1,0:T(8,128)(2,1)}, u32[]{:S(2)}, u32[]{:S(2)}) %collective-permute-start.32) | collective-permute-done | bytes 294944 | tf_op jit(solution)/shard_map/ppermute | solution.py:556
  132.1 4.7 %collective-permute-done.34 = bf16[2,96,768]{2,1,0:T(8,128)(2,1)S(1)} collective-permute-done((bf16[2,96,768]{2,1,0:T(8,128)(2,1)S(1)}, bf16[2,96,768]{2,1,0:T(8,128)(2,1)S(1)}, u32[]{:S(2)}, u32[]{:S(2)}) %collective-permute-start.34) | collective-permute-done | bytes 294944 | tf_op jit(solution)/shard_map/ppermute | solution.py:556
  137.6 4.4 %branch_back.1 = (f32[256,768]{1,0:T(8,128)}, bf16[256,768]{1,0:T(8,128)(2,1)}, bf16[8,192,128]{2,1,0:T(8,128)(2,1)}, f32[8,768]{1,0:T(8,128)}) custom-call(s32[4]{0:T(128)} %pad_add_fusion.place, f32[256,768]{1,0:T(8,128)} %get-tuple-element.155.own_ref, bf16[2,256,768]{2,1,0:T(8,128)(2,1)} %copy-done.2, bf16[256,768]{1,0:T(8,128)(2,1)} %copy-done.23, ...), custom_call_target="tpu_custom_call" | custom-call | flops 603979776 | bytes 5934608 | tf_op jit(solution)/shard_map/branch_back/pallas_call | solution.py:74
  142.0 3.2 %out_back.1 = (bf16[2,8,32,768]{3,2,1,0:T(8,128)(2,1)}, bf16[2,8,32,768]{3,2,1,0:T(8,128)(2,1)}) custom-call(s32[4]{0:T(128)} %pad_add_fusion.place, bf16[8,192,128]{2,1,0:T(8,128)(2,1)} %copy-done.4, bf16[256,768]{1,0:T(8,128)(2,1)} %get-tuple-element.163.grad_ref, f32[8,768]{1,0:T(8,128)} %get-tuple-element.164.sum_ref, ...), custom_call_target="tpu_custom_call" | custom-call | flops 301989888 | bytes 2386960 | tf_op jit(solution)/shard_map/out_back/pallas_call | solution.py:74
  145.3 4.0 %all-to-all-start.1 = ((bf16[8,192,128]{2,1,0:T(8,128)(2,1)}), bf16[8,192,128]{2,1,0:T(8,128)(2,1)S(1)}, u32[]{:S(2)}, u32[]{:S(2)}) async-start(bf16[8,192,128]{2,1,0:T(8,128)(2,1)} %get-tuple-element.162), calls=%async_computation.1 | async-start | bytes 786432 | tf_op jit(solution)/shard_map/all_to_all | solution.py:579
  153.9 3.3 %all-to-all-done.1.gt_ref = bf16[8,192,128]{2,1,0:T(8,128)(2,1)S(1)} async-done(((bf16[8,192,128]{2,1,0:T(8,128)(2,1)}), bf16[8,192,128]{2,1,0:T(8,128)(2,1)S(1)}, u32[]{:S(2)}, u32[]{:S(2)}) %all-to-all-start.1) | async-done | bytes 393248 | tf_op jit(solution)/shard_map/all_to_all | solution.py:579
  162.3 18.1 %attend_back.1 = (bf16[8,128,192]{2,1,0:T(8,128)(2,1)}, bf16[8,256,384]{2,1,0:T(8,128)(2,1)}, f32[8,192]{1,0:T(8,128)}) custom-call(s32[4]{0:T(128)} %pad_add_fusion.place, bf16[8,192,128]{2,1,0:T(8,128)(2,1)} %get-tuple-element.127.qt_ref, bf16[8,256,192]{2,1,0:T(8,128)(2,1)} %get-tuple-element.128.k_ref, bf16[8,256,192]{2,1,0:T(8,128)(2,1)} %get-tuple-element.153.v_ref, ...), custom_call_target="tpu_custom_call" | custom-call | flops 2264924160 | bytes 5523472 | tf_op jit(solution)/shard_map/attend_back/pallas_call | solution.py:74
  182.8 10.4 %project_back.1 = (bf16[4,256,768]{2,1,0:T(8,128)(2,1)}, bf16[4,256,768]{2,1,0:T(8,128)(2,1)}, bf16[2,2,104,576]{3,2,1,0:T(8,128)(2,1)}, bf16[2,2,104,576]{3,2,1,0:T(8,128)(2,1)}) custom-call(s32[4]{0:T(128)} %pad_add_fusion.place, bf16[768,2048]{1,0:T(8,128)(2,1)} %get-tuple-element.151.normed_t_ref, bf16[768,1024]{1,0:T(8,128)(2,1)} %get-tuple-element.152.query_t_ref, ...), custom_call_target="tpu_custom_call" | custom-call | flops 3019898880 | bytes 11679760 | tf_op jit(solution)/shard_map/project_back/pallas_call | solution.py:74
  200.4 5.5 %collective-permute-done.44 = bf16[2,32,768]{2,1,0:T(8,128)(2,1)S(1)} collective-permute-done((bf16[2,32,768]{2,1,0:T(8,128)(2,1)S(1)}, bf16[2,32,768]{2,1,0:T(8,128)(2,1)S(1)}, u32[]{:S(2)}, u32[]{:S(2)}) %collective-permute-start.44) | collective-permute-done | bytes 98336 | tf_op jit(solution)/shard_map/ppermute | solution.py:556
  222.3 8.2 %collective-permute-start.57 = (bf16[120,768]{1,0:T(8,128)(2,1)S(1)}, bf16[120,768]{1,0:T(8,128)(2,1)S(1)}, u32[]{:S(2)}, u32[]{:S(2)}) collective-permute-start(bf16[120,768]{1,0:T(8,128)(2,1)S(1)} %get-tuple-element.235), channel_id=1, source_target_pairs={{0,4},{1,5},{2,6},{3,7},{4,0},{5,1},{6,2},{7,3},{8,12},{9,13},{10,... | collective-permute-start | bytes 552968 | tf_op jit(solution)/shard_map/ppermute | solution.py:556
  231.6 3.4 %collective-permute-start.56 = (bf16[4,24,768]{2,1,0:T(8,128)(2,1)S(1)}, bf16[4,24,768]{2,1,0:T(8,128)(2,1)S(1)}, u32[]{:S(2)}, u32[]{:S(2)}) collective-permute-start(bf16[4,24,768]{2,1,0:T(8,128)(2,1)S(1)} %get-tuple-element.237), channel_id=1, source_target_pairs={{0,4},{1,5},{2,6},{3,7},{4,0},{5,1},{6,2},{7,3},{8,12},{9,13},{10,... | collective-permute-start | bytes 442376 | tf_op jit(solution)/shard_map/ppermute | solution.py:556
  235.0 7.6 %collective-permute-done.56 = bf16[4,24,768]{2,1,0:T(8,128)(2,1)S(1)} collective-permute-done((bf16[4,24,768]{2,1,0:T(8,128)(2,1)S(1)}, bf16[4,24,768]{2,1,0:T(8,128)(2,1)S(1)}, u32[]{:S(2)}, u32[]{:S(2)}) %collective-permute-start.56) | collective-permute-done | bytes 147488 | tf_op jit(solution)/shard_map/ppermute | solution.py:556
  242.7 4.3 %collective-permute-done.48.part2 = bf16[256,768]{1,0:T(8,128)(2,1)S(1)} collective-permute-done((bf16[256,768]{1,0:T(8,128)(2,1)S(1)}, bf16[256,768]{1,0:T(8,128)(2,1)S(1)}, u32[]{:S(2)}, u32[]{:S(2)}) %collective-permute-start.48) | collective-permute-done | bytes 393248 | tf_op jit(solution)/shard_map/ppermute | solution.py:556
  247.1 11.9 %collective-permute-start.68 = (bf16[2,4,24,768]{3,2,1,0:T(8,128)(2,1)S(1)}, bf16[2,4,24,768]{3,2,1,0:T(8,128)(2,1)S(1)}, u32[]{:S(2)}, u32[]{:S(2)}) collective-permute-start(bf16[2,4,24,768]{3,2,1,0:T(8,128)(2,1)S(1)} %pad_maximum_fusion.1.part0), channel_id=1, source_target_pairs={{0,3},{1,2},{2,1},{3,0},{4,7},{5,6},{6,5},{7,4},{8,11},{9,10},{10,... | collective-permute-start | bytes 884744 | tf_op jit(solution)/shard_map/ppermute | solution.py:556
  259.7 3.7 %collective-permute-start.62 = (bf16[2,104,576]{2,1,0:T(8,128)(2,1)S(1)}, bf16[2,104,576]{2,1,0:T(8,128)(2,1)}, u32[]{:S(2)}, u32[]{:S(2)}) collective-permute-start(bf16[2,104,576]{2,1,0:T(8,128)(2,1)S(1)} %pad_maximum_fusion.2.part0), channel_id=1, source_target_pairs={{0,3},{1,2},{2,1},{3,0},{4,7},{5,6},{6,5},{7,4},{8,11},{9,10},{10,... | collective-permute-start | bytes 718856 | tf_op jit(solution)/shard_map/ppermute | solution.py:556
  263.4 3.2 %stream_back.1 = bf16[256,767]{1,0:T(8,128)(2,1)} custom-call(s32[4]{0:T(128)} %pad_add_fusion.place, bf16[256,768]{1,0:T(8,128)(2,1)} %get-tuple-element.229.part0, bf16[256,768]{1,0:T(8,128)(2,1)} %copy-done.18, bf16[256,768]{1,0:T(8,128)(2,1)} %copy-done.17, bf16[256,768]{1,0:T(8,128)(2,1)} %copy-done.16, f32[256,768]{1,0:T(8,128)} %get-tuple-element.140.resid_ref, ...), custom_call_target="tpu_custom_call" | custom-call | bytes 3550736 | tf_op jit(solution)/shard_map/stream_back/pallas_call | solution.py:74
  275.9 3.3 %collective-permute-done.62.part3 = bf16[2,104,576]{2,1,0:T(8,128)(2,1)} collective-permute-done((bf16[2,104,576]{2,1,0:T(8,128)(2,1)S(1)}, bf16[2,104,576]{2,1,0:T(8,128)(2,1)}, u32[]{:S(2)}, u32[]{:S(2)}) %collective-permute-start.62) | collective-permute-done | bytes 239648 | tf_op jit(solution)/shard_map/ppermute | solution.py:556
  280.8 3.5 %collective-permute-done.61.part2 = bf16[2,104,576]{2,1,0:T(8,128)(2,1)} collective-permute-done((bf16[2,104,576]{2,1,0:T(8,128)(2,1)S(1)}, bf16[2,104,576]{2,1,0:T(8,128)(2,1)}, u32[]{:S(2)}, u32[]{:S(2)}) %collective-permute-start.61) | collective-permute-done | bytes 239648 | tf_op jit(solution)/shard_map/ppermute | solution.py:556
  284.3 5.3 %collective-permute-start.60 = (bf16[2,104,576]{2,1,0:T(8,128)(2,1)S(1)}, bf16[2,104,576]{2,1,0:T(8,128)(2,1)S(1)}, u32[]{:S(2)}, u32[]{:S(2)}) collective-permute-start(bf16[2,104,576]{2,1,0:T(8,128)(2,1)S(1)} %pad_maximum_fusion.2.part0), channel_id=1, source_target_pairs={{0,1},{1,0},{2,3},{3,2},{4,5},{5,4},{6,7},{7,6},{8,9},{9,8},{10,11... | collective-permute-start | bytes 718856 | tf_op jit(solution)/shard_map/ppermute | solution.py:556
  293.6 4.7 %collective-permute-done.60.part1 = bf16[2,104,576]{2,1,0:T(8,128)(2,1)S(1)} collective-permute-done((bf16[2,104,576]{2,1,0:T(8,128)(2,1)S(1)}, bf16[2,104,576]{2,1,0:T(8,128)(2,1)S(1)}, u32[]{:S(2)}, u32[]{:S(2)}) %collective-permute-start.60) | collective-permute-done | bytes 239648 | tf_op jit(solution)/shard_map/ppermute | solution.py:556
  299.0 3.1 %heads_out.1 = (f32[192,2304]{1,0:T(8,128)}, f32[192,1]{1,0:T(8,128)}, f32[1,384]{1,0:T(1,128)}) custom-call(s32[4]{0:T(128)} %pad_add_fusion.place, bf16[2,104,576]{2,1,0:T(8,128)(2,1)} %copy-done.11, bf16[2,104,576]{2,1,0:T(8,128)(2,1)} %copy-done.34, bf16[2,104,576]{2,1,0:T(8,128)(2,1)} %collective-permute-done.61.part2, ...), custom_call_target="tpu_custom_call" | custom-call | bytes 3614992 | tf_op jit(solution)/shard_map/heads_out/pallas_call | solution.py:74
  306.6 3.1 down_out.1
  (311 shorter events, 107.9 us)
Async XLA Ops:
  0.7 15.3 %collective-permute-start.6 = (bf16[256,767]{1,0:T(8,128)(2,1)}, bf16[256,767]{1,0:T(8,128)(2,1)S(1)}, u32[]{:S(2)}, u32[]{:S(2)}) collective-permute-start(bf16[256,767]{1,0:T(8,128)(2,1)} %param.12), channel_id=1, source_target_pairs={{0,0},{1,1},{2,2},{3,3},{4,8},{5,9},{6,10},{7,11},{8,4},{9,5},{10,... | collective-permute-start | bytes 1178120 | tf_op jit(solution)/shard_map/ppermute | solution.py:556
  16.0 25.5 %collective-permute-start = (bf16[192,576]{1,0:T(8,128)(2,1)}, bf16[192,576]{1,0:T(8,128)(2,1)S(1)}, u32[]{:S(2)}, u32[]{:S(2)}) collective-permute-start(bf16[192,576]{1,0:T(8,128)(2,1)} %get-tuple-element.118.refs_0_.slab0), channel_id=1, source_target_pairs={{0,8},{1,9},{2,10},{3,11},{4,12},{5,13},{6,14},{7,15},{8,0},{9,1},... | collective-permute-start | bytes 663560 | tf_op jit(solution)/shard_map/ppermute | solution.py:556
  19.0 13.3 %collective-permute-start.9 = (bf16[1,256,768]{2,1,0:T(8,128)(2,1)}, bf16[1,256,768]{2,1,0:T(8,128)(2,1)S(1)}, u32[]{:S(2)}, u32[]{:S(2)}) collective-permute-start(bf16[1,256,768]{2,1,0:T(8,128)(2,1)} %get-tuple-element.122.refs_6_), channel_id=1, source_target_pairs={{0,3},{1,2},{2,1},{3,0},{4,7},{5,6},{6,5},{7,4},{8,11},{9,10},{10,... | collective-permute-start | bytes 1179656 | tf_op jit(solution)/shard_map/ppermute | solution.py:556
  22.0 18.6 %collective-permute-start.8 = (bf16[1,256,768]{2,1,0:T(8,128)(2,1)}, bf16[1,256,768]{2,1,0:T(8,128)(2,1)S(1)}, u32[]{:S(2)}, u32[]{:S(2)}) collective-permute-start(bf16[1,256,768]{2,1,0:T(8,128)(2,1)} %get-tuple-element.122.refs_6_), channel_id=1, source_target_pairs={{0,2},{1,3},{2,0},{3,1},{4,6},{5,7},{6,4},{7,5},{8,10},{9,11},{10,... | collective-permute-start | bytes 1179656 | tf_op jit(solution)/shard_map/ppermute | solution.py:556
  22.5 18.1 %collective-permute-start.7 = (bf16[1,256,768]{2,1,0:T(8,128)(2,1)}, bf16[1,256,768]{2,1,0:T(8,128)(2,1)S(1)}, u32[]{:S(2)}, u32[]{:S(2)}) collective-permute-start(bf16[1,256,768]{2,1,0:T(8,128)(2,1)} %get-tuple-element.122.refs_6_), channel_id=1, source_target_pairs={{0,1},{1,0},{2,3},{3,2},{4,5},{5,4},{6,7},{7,6},{8,9},{9,8},{10,11... | collective-permute-start | bytes 1179656 | tf_op jit(solution)/shard_map/ppermute | solution.py:556
  44.3 24.1 %collective-permute-start.15 = (bf16[192,768]{1,0:T(8,128)(2,1)}, bf16[192,768]{1,0:T(8,128)(2,1)S(1)}, u32[]{:S(2)}, u32[]{:S(2)}) collective-permute-start(bf16[192,768]{1,0:T(8,128)(2,1)} %get-tuple-element.131), channel_id=1, source_target_pairs={{0,8},{1,9},{2,10},{3,11},{4,12},{5,13},{6,14},{7,15},{8,0},{9,1},... | collective-permute-start | bytes 884744 | tf_op jit(solution)/shard_map/ppermute | solution.py:556
  44.6 23.9 %collective-permute-start.16 = (bf16[192,768]{1,0:T(8,128)(2,1)}, bf16[192,768]{1,0:T(8,128)(2,1)S(1)}, u32[]{:S(2)}, u32[]{:S(2)}) collective-permute-start(bf16[192,768]{1,0:T(8,128)(2,1)} %get-tuple-element.132), channel_id=1, source_target_pairs={{0,16},{1,17},{2,18},{3,19},{4,20},{5,21},{6,22},{7,23},{8,24},{9,... | collective-permute-start | bytes 884744 | tf_op jit(solution)/shard_map/ppermute | solution.py:556
  46.1 22.8 %collective-permute-start.17 = (bf16[192,768]{1,0:T(8,128)(2,1)}, bf16[192,768]{1,0:T(8,128)(2,1)}, u32[]{:S(2)}, u32[]{:S(2)}) collective-permute-start(bf16[192,768]{1,0:T(8,128)(2,1)} %get-tuple-element.133), channel_id=1, source_target_pairs={{0,24},{1,25},{2,26},{3,27},{4,28},{5,29},{6,30},{7,31},{8,16},{9,... | collective-permute-start | bytes 884744 | tf_op jit(solution)/shard_map/ppermute | solution.py:556
  47.4 29.3 %collective-permute-start.23 = (bf16[256,767]{1,0:T(8,128)(2,1)S(1)}, bf16[256,767]{1,0:T(8,128)(2,1)S(1)}, u32[]{:S(2)}, u32[]{:S(2)}) collective-permute-start(bf16[256,767]{1,0:T(8,128)(2,1)S(1)} %copy-done.42), channel_id=1, source_target_pairs={{0,0},{1,1},{2,2},{3,3},{4,8},{5,9},{6,10},{7,11},{8,4},{9,5},{10,... | collective-permute-start | bytes 1178120 | tf_op jit(solution)/shard_map/ppermute | solution.py:556
  69.2 15.7 %all-to-all-start = ((bf16[8,192,128]{2,1,0:T(8,128)(2,1)}), bf16[8,192,128]{2,1,0:T(8,128)(2,1)S(1)}, u32[]{:S(2)}, u32[]{:S(2)}) async-start(bf16[8,192,128]{2,1,0:T(8,128)(2,1)} %get-tuple-element.134.out_ref), calls=%async_computation | async-start | bytes 786432 | tf_op jit(solution)/shard_map/all_to_all | solution.py:579
  119.9 16.8 %collective-permute-start.31 = (bf16[256,768]{1,0:T(8,128)(2,1)S(1)}, bf16[256,768]{1,0:T(8,128)(2,1)S(1)}, u32[]{:S(2)}, u32[]{:S(2)}) collective-permute-start(bf16[256,768]{1,0:T(8,128)(2,1)S(1)} %fusion.2), channel_id=1, source_target_pairs={{0,16},{1,17},{2,18},{3,19},{4,20},{5,21},{6,22},{7,23},{8,24},{9,... | collective-permute-start | bytes 1179656 | tf_op jit(solution)/shard_map/ppermute | solution.py:556
  124.0 28.9 %collective-permute-start.27 = (bf16[2,256,768]{2,1,0:T(8,128)(2,1)}, bf16[2,256,768]{2,1,0:T(8,128)(2,1)S(1)}, u32[]{:S(2)}, u32[]{:S(2)}) collective-permute-start(bf16[2,256,768]{2,1,0:T(8,128)(2,1)} %get-tuple-element.149), channel_id=1, source_target_pairs={{0,8},{1,9},{2,10},{3,11},{4,12},{5,13},{6,14},{7,15},{8,0},{9,1},... | collective-permute-start | bytes 2359304 | tf_op jit(solution)/shard_map/ppermute | solution.py:556
  149.3 31.0 %collective-permute-start.38 = (bf16[2,4,24,768]{3,2,1,0:T(8,128)(2,1)}, bf16[2,4,24,768]{3,2,1,0:T(8,128)(2,1)}, u32[]{:S(2)}, u32[]{:S(2)}) collective-permute-start(bf16[2,4,24,768]{3,2,1,0:T(8,128)(2,1)} %get-tuple-element.177), channel_id=1, source_target_pairs={{0,1},{1,0},{2,3},{3,2},{4,5},{5,4},{6,7},{7,6},{8,9},{9,8},{10,11... | collective-permute-start | bytes 884744 | tf_op jit(solution)/shard_map/ppermute | solution.py:556
  151.4 29.6 %collective-permute-start.39 = (bf16[2,4,24,768]{3,2,1,0:T(8,128)(2,1)}, bf16[2,4,24,768]{3,2,1,0:T(8,128)(2,1)}, u32[]{:S(2)}, u32[]{:S(2)}) collective-permute-start(bf16[2,4,24,768]{3,2,1,0:T(8,128)(2,1)} %get-tuple-element.178), channel_id=1, source_target_pairs={{0,2},{1,3},{2,0},{3,1},{4,6},{5,7},{6,4},{7,5},{8,10},{9,11},{10,... | collective-permute-start | bytes 884744 | tf_op jit(solution)/shard_map/ppermute | solution.py:556
  152.8 28.1 %collective-permute-start.40 = (bf16[2,4,24,768]{3,2,1,0:T(8,128)(2,1)}, bf16[2,4,24,768]{3,2,1,0:T(8,128)(2,1)}, u32[]{:S(2)}, u32[]{:S(2)}) collective-permute-start(bf16[2,4,24,768]{3,2,1,0:T(8,128)(2,1)} %get-tuple-element.179), channel_id=1, source_target_pairs={{0,3},{1,2},{2,1},{3,0},{4,7},{5,6},{6,5},{7,4},{8,11},{9,10},{10,... | collective-permute-start | bytes 884744 | tf_op jit(solution)/shard_map/ppermute | solution.py:556
  157.3 23.7 %collective-permute-start.36 = (bf16[8,32,768]{2,1,0:T(8,128)(2,1)S(1)}, bf16[8,32,768]{2,1,0:T(8,128)(2,1)S(1)}, u32[]{:S(2)}, u32[]{:S(2)}) collective-permute-start(bf16[8,32,768]{2,1,0:T(8,128)(2,1)S(1)} %slice_bitcast_fusion.3), channel_id=1, source_target_pairs={{0,16},{1,17},{2,18},{3,19},{4,20},{5,21},{6,22},{7,23},{8,24},{9,... | collective-permute-start | bytes 1179656 | tf_op jit(solution)/shard_map/ppermute | solution.py:556
  160.6 20.3 %collective-permute-start.37 = (bf16[96,768]{1,0:T(8,128)(2,1)}, bf16[96,768]{1,0:T(8,128)(2,1)S(1)}, u32[]{:S(2)}, u32[]{:S(2)}) collective-permute-start(bf16[96,768]{1,0:T(8,128)(2,1)} %add_bitcast_fusion.5), channel_id=1, source_target_pairs={{0,4},{1,5},{2,6},{3,7},{4,0},{5,1},{6,2},{7,3},{8,12},{9,13},{10,... | collective-permute-start | bytes 442376 | tf_op jit(solution)/shard_map/ppermute | solution.py:556
  193.2 17.5 %collective-permute-start.46 = (bf16[4,256,768]{2,1,0:T(8,128)(2,1)}, bf16[4,256,768]{2,1,0:T(8,128)(2,1)S(1)}, u32[]{:S(2)}, u32[]{:S(2)}) collective-permute-start(bf16[4,256,768]{2,1,0:T(8,128)(2,1)} %get-tuple-element.197), channel_id=1, source_target_pairs={{0,8},{1,9},{2,10},{3,11},{4,12},{5,13},{6,14},{7,15},{8,0},{9,1},... | collective-permute-start | bytes 4718600 | tf_op jit(solution)/shard_map/ppermute | solution.py:556
  214.1 28.5 %collective-permute-start.49 = (bf16[256,768]{1,0:T(8,128)(2,1)S(1)}, bf16[256,768]{1,0:T(8,128)(2,1)S(1)}, u32[]{:S(2)}, u32[]{:S(2)}) collective-permute-start(bf16[256,768]{1,0:T(8,128)(2,1)S(1)} %get-tuple-element.226), channel_id=1, source_target_pairs={{0,3},{1,2},{2,1},{3,0},{4,7},{5,6},{6,5},{7,4},{8,11},{9,10},{10,... | collective-permute-start | bytes 1179656 | tf_op jit(solution)/shard_map/ppermute | solution.py:556
  214.3 32.7 %collective-permute-start.48 = (bf16[256,768]{1,0:T(8,128)(2,1)S(1)}, bf16[256,768]{1,0:T(8,128)(2,1)S(1)}, u32[]{:S(2)}, u32[]{:S(2)}) collective-permute-start(bf16[256,768]{1,0:T(8,128)(2,1)S(1)} %get-tuple-element.227), channel_id=1, source_target_pairs={{0,2},{1,3},{2,0},{3,1},{4,6},{5,7},{6,4},{7,5},{8,10},{9,11},{10,... | collective-permute-start | bytes 1179656 | tf_op jit(solution)/shard_map/ppermute | solution.py:556
  217.1 29.8 %collective-permute-start.47 = (bf16[256,768]{1,0:T(8,128)(2,1)S(1)}, bf16[256,768]{1,0:T(8,128)(2,1)S(1)}, u32[]{:S(2)}, u32[]{:S(2)}) collective-permute-start(bf16[256,768]{1,0:T(8,128)(2,1)S(1)} %get-tuple-element.228), channel_id=1, source_target_pairs={{0,1},{1,0},{2,3},{3,2},{4,5},{5,4},{6,7},{7,6},{8,9},{9,8},{10,11... | collective-permute-start | bytes 1179656 | tf_op jit(solution)/shard_map/ppermute | solution.py:556
  222.3 24.6 %collective-permute-start.57 = (bf16[120,768]{1,0:T(8,128)(2,1)S(1)}, bf16[120,768]{1,0:T(8,128)(2,1)S(1)}, u32[]{:S(2)}, u32[]{:S(2)}) collective-permute-start(bf16[120,768]{1,0:T(8,128)(2,1)S(1)} %get-tuple-element.235), channel_id=1, source_target_pairs={{0,4},{1,5},{2,6},{3,7},{4,0},{5,1},{6,2},{7,3},{8,12},{9,13},{10,... | collective-permute-start | bytes 552968 | tf_op jit(solution)/shard_map/ppermute | solution.py:556
  247.1 19.8 %collective-permute-start.68 = (bf16[2,4,24,768]{3,2,1,0:T(8,128)(2,1)S(1)}, bf16[2,4,24,768]{3,2,1,0:T(8,128)(2,1)S(1)}, u32[]{:S(2)}, u32[]{:S(2)}) collective-permute-start(bf16[2,4,24,768]{3,2,1,0:T(8,128)(2,1)S(1)} %pad_maximum_fusion.1.part0), channel_id=1, source_target_pairs={{0,3},{1,2},{2,1},{3,0},{4,7},{5,6},{6,5},{7,4},{8,11},{9,10},{10,... | collective-permute-start | bytes 884744 | tf_op jit(solution)/shard_map/ppermute | solution.py:556
  259.0 13.8 %collective-permute-start.67 = (bf16[2,4,24,768]{3,2,1,0:T(8,128)(2,1)S(1)}, bf16[2,4,24,768]{3,2,1,0:T(8,128)(2,1)}, u32[]{:S(2)}, u32[]{:S(2)}) collective-permute-start(bf16[2,4,24,768]{3,2,1,0:T(8,128)(2,1)S(1)} %pad_maximum_fusion.1.part0), channel_id=1, source_target_pairs={{0,2},{1,3},{2,0},{3,1},{4,6},{5,7},{6,4},{7,5},{8,10},{9,11},{10,... | collective-permute-start | bytes 884744 | tf_op jit(solution)/shard_map/ppermute | solution.py:556
  259.0 16.4 %collective-permute-start.66 = (bf16[2,4,24,768]{3,2,1,0:T(8,128)(2,1)S(1)}, bf16[2,4,24,768]{3,2,1,0:T(8,128)(2,1)}, u32[]{:S(2)}, u32[]{:S(2)}) collective-permute-start(bf16[2,4,24,768]{3,2,1,0:T(8,128)(2,1)S(1)} %pad_maximum_fusion.1.part0), channel_id=1, source_target_pairs={{0,1},{1,0},{2,3},{3,2},{4,5},{5,4},{6,7},{7,6},{8,9},{9,8},{10,11... | collective-permute-start | bytes 884744 | tf_op jit(solution)/shard_map/ppermute | solution.py:556
  259.7 19.5 %collective-permute-start.62 = (bf16[2,104,576]{2,1,0:T(8,128)(2,1)S(1)}, bf16[2,104,576]{2,1,0:T(8,128)(2,1)}, u32[]{:S(2)}, u32[]{:S(2)}) collective-permute-start(bf16[2,104,576]{2,1,0:T(8,128)(2,1)S(1)} %pad_maximum_fusion.2.part0), channel_id=1, source_target_pairs={{0,3},{1,2},{2,1},{3,0},{4,7},{5,6},{6,5},{7,4},{8,11},{9,10},{10,... | collective-permute-start | bytes 718856 | tf_op jit(solution)/shard_map/ppermute | solution.py:556
  263.4 20.9 %collective-permute-start.61 = (bf16[2,104,576]{2,1,0:T(8,128)(2,1)S(1)}, bf16[2,104,576]{2,1,0:T(8,128)(2,1)}, u32[]{:S(2)}, u32[]{:S(2)}) collective-permute-start(bf16[2,104,576]{2,1,0:T(8,128)(2,1)S(1)} %pad_maximum_fusion.2.part0), channel_id=1, source_target_pairs={{0,2},{1,3},{2,0},{3,1},{4,6},{5,7},{6,4},{7,5},{8,10},{9,11},{10,... | collective-permute-start | bytes 718856 | tf_op jit(solution)/shard_map/ppermute | solution.py:556
  266.9 38.0 %collective-permute-start.65 = (bf16[2,120,768]{2,1,0:T(8,128)(2,1)S(1)}, bf16[2,120,768]{2,1,0:T(8,128)(2,1)S(1)}, u32[]{:S(2)}, u32[]{:S(2)}) collective-permute-start(bf16[2,120,768]{2,1,0:T(8,128)(2,1)S(1)} %pad_maximum_fusion.part0), channel_id=1, source_target_pairs={{0,3},{1,2},{2,1},{3,0},{4,7},{5,6},{6,5},{7,4},{8,11},{9,10},{10,... | collective-permute-start | bytes 1105928 | tf_op jit(solution)/shard_map/ppermute | solution.py:556
  272.8 32.1 %collective-permute-start.64 = (bf16[2,120,768]{2,1,0:T(8,128)(2,1)S(1)}, bf16[2,120,768]{2,1,0:T(8,128)(2,1)S(1)}, u32[]{:S(2)}, u32[]{:S(2)}) collective-permute-start(bf16[2,120,768]{2,1,0:T(8,128)(2,1)S(1)} %pad_maximum_fusion.part0), channel_id=1, source_target_pairs={{0,2},{1,3},{2,0},{3,1},{4,6},{5,7},{6,4},{7,5},{8,10},{9,11},{10,... | collective-permute-start | bytes 1105928 | tf_op jit(solution)/shard_map/ppermute | solution.py:556
  275.4 29.6 %collective-permute-start.63 = (bf16[2,120,768]{2,1,0:T(8,128)(2,1)S(1)}, bf16[2,120,768]{2,1,0:T(8,128)(2,1)S(1)}, u32[]{:S(2)}, u32[]{:S(2)}) collective-permute-start(bf16[2,120,768]{2,1,0:T(8,128)(2,1)S(1)} %pad_maximum_fusion.part0), channel_id=1, source_target_pairs={{0,1},{1,0},{2,3},{3,2},{4,5},{5,4},{6,7},{7,6},{8,9},{9,8},{10,11... | collective-permute-start | bytes 1105928 | tf_op jit(solution)/shard_map/ppermute | solution.py:556
  279.2 30.6 %collective-permute-start.58 = (bf16[256,767]{1,0:T(8,128)(2,1)}, bf16[256,767]{1,0:T(8,128)(2,1)S(1)}, u32[]{:S(2)}, u32[]{:S(2)}) collective-permute-start(bf16[256,767]{1,0:T(8,128)(2,1)} %stream_back.1), channel_id=1, source_target_pairs={{0,0},{1,1},{2,2},{3,3},{4,8},{5,9},{6,10},{7,11},{8,4},{9,5},{10,... | collective-permute-start | bytes 1178120 | tf_op jit(solution)/shard_map/ppermute | solution.py:556
  284.3 14.0 %collective-permute-start.60 = (bf16[2,104,576]{2,1,0:T(8,128)(2,1)S(1)}, bf16[2,104,576]{2,1,0:T(8,128)(2,1)S(1)}, u32[]{:S(2)}, u32[]{:S(2)}) collective-permute-start(bf16[2,104,576]{2,1,0:T(8,128)(2,1)S(1)} %pad_maximum_fusion.2.part0), channel_id=1, source_target_pairs={{0,1},{1,0},{2,3},{3,2},{4,5},{5,4},{6,7},{7,6},{8,9},{9,8},{10,11... | collective-permute-start | bytes 718856 | tf_op jit(solution)/shard_map/ppermute | solution.py:556
  (102 other events, 963.7 us)
where the time goes:
time: 315 us; the launch traced here: 312 us
  starting transfers between devices  102 us (32%)
  Pallas kernels  95.7 us (30%)
  waiting for transfers between devices  84.8 us (27%)
  other arithmetic  15.4 us (5%)
  local copies, waits for them, and re-layouts  11.8 us (4%)
    pallas_call x15, Pallas kernels, call(): pl.pallas_call(body, out_shape=tuple(outs), scratch_shapes=list(scratch),...  95.7 us
    ppermute x69, starting transfers between devices, send(): return lax.ppermute(value, AXES, pairs)  91.4 us
    ppermute x69, waiting for transfers between devices, send(): return lax.ppermute(value, AXES, pairs)  81.5 us
    all_to_all x2, starting transfers between devices, group_all_to_all(): lax.all_to_all(value, AXES, 0, 0, axis_index_groups=groups, tiled=True)  10.3 us
    unnamed x128, local copies, waits for them, and re-layouts  8.78 us
  transfers between devices with their start and end apart: 71, of which 23 were waited for; matrix products, arithmetic and copies ran while one was open for 5% of the time, Pallas kernels for 27%

commit v1 on v0

--- a/solution.py
+++ b/solution.py
@@ -19,6 +19,7 @@
 LANES = 128
 PIECES = 8
 EXTRA = 8
+LONG = 10**11
 AXES = ("fsdp", "ctx")
 VMEM_LIMIT = 120 << 19
 UNROLL_BLOCKS = 8
@@ -120,7 +121,7 @@
         wkv[at, :] = slab_ref[:, GROUP_COLS:]
 
 
-def project(place, normed_ref, slots, base, bias_ref, k_ref, v_ref, vt_ref, qt_ref, wq, wkv):
+def project(place, normed_ref, slots, bias_ref, k_ref, v_ref, q_ref, qt_ref, wq, wkv):
     rows, query_rows = normed_ref.shape[1], qt_ref.shape[2]
     own = pl.ds(pl.multiple_of(place[2] * query_rows, query_rows), query_rows)
     for start in range(0, slots, 2):
@@ -134,14 +135,14 @@
             here = slice(at * rows, (at + 1) * rows)
             k_ref[slot] = keys[here].astype(bf16)
             v_ref[slot] = values[here].astype(bf16)
-            vt_ref[:, slot * rows : (slot + 1) * rows] = values[here].T.astype(bf16)
-            qt_ref[slot] = queries[at * query_rows : (at + 1) * query_rows].T.astype(bf16)
+            query = queries[at * query_rows : (at + 1) * query_rows]
+            q_ref[slot], qt_ref[slot] = query.astype(bf16), query.T.astype(bf16)
 
 
 def project_kernel(place, *refs):
     slabs, (gain_ref, bias_ref) = refs[:4], refs[4:6]
     pieces = refs[6:-7]
-    normed_ref, k_ref, v_ref, vt_ref, qt_ref, wq, wkv = refs[-7:]
+    normed_ref, k_ref, v_ref, q_ref, qt_ref, wq, wkv = refs[-7:]
     load_heads(place, slabs, wq, wkv)
     gain = gain_ref[...]
     slot = 0
@@ -149,30 +150,28 @@
         for at in range(ref.shape[0]):
             normed_ref[slot] = (ref[at].astype(f32) * gain).astype(bf16)
             slot += 1
-    project(place, normed_ref, slot, 0, bias_ref, k_ref, v_ref, vt_ref, qt_ref, wq, wkv)
+    project(place, normed_ref, slot, bias_ref, k_ref, v_ref, q_ref, qt_ref, wq, wkv)
 
 
 def project_block_kernel(place, *refs):
     slabs, bias_ref, normed_ref = refs[:4], refs[4], refs[5]
-    k_ref, v_ref, vt_ref, qt_ref, wq, wkv = refs[6:]
+    k_ref, v_ref, q_ref, qt_ref, wq, wkv = refs[6:]
 
     @pl.when(pl.program_id(0) == 0)
     def _():
         load_heads(place, slabs, wq, wkv)
 
     slots = normed_ref.shape[0]
-    project(place, normed_ref, slots, 0, bias_ref, k_ref, v_ref, vt_ref, qt_ref, wq, wkv)
-
-
-def collect_kernel(place, normed_ref, k_ref, normed_t_ref, query_t_ref, kt_ref):
-    blocks, rows, _ = k_ref.shape
+    project(place, normed_ref, slots, bias_ref, k_ref, v_ref, q_ref, qt_ref, wq, wkv)
+
+
+def collect_kernel(place, normed_ref, normed_t_ref, query_t_ref):
+    blocks, rows, _ = normed_ref.shape
     query_rows = query_t_ref.shape[1] // blocks
     own = pl.ds(pl.multiple_of(place[2] * query_rows, query_rows), query_rows)
     for slot in range(blocks):
-        tokens = slice(slot * rows, (slot + 1) * rows)
-        normed_t_ref[:, tokens] = normed_ref[slot].T
+        normed_t_ref[:, slot * rows : (slot + 1) * rows] = normed_ref[slot].T
         query_t_ref[:, slot * query_rows : (slot + 1) * query_rows] = normed_ref[slot, own, :].T
-        kt_ref[:, tokens] = k_ref[slot].T
 
 
 def by_head(value):
@@ -181,51 +180,59 @@
     return jnp.concatenate([jnp.where(head == at, value, zero) for at in range(GROUP_HEADS)], axis=1)
 
 
-def attend_kernel(place, qt_ref, k_ref, vt_ref, out_ref, log_ref):
-    blocks, _, width = qt_ref.shape
-    rows = k_ref.shape[1]
+def by_head_rows(value):
+    head = lax.broadcasted_iota(jnp.int32, value.shape, 1) // HD
+    zero = jnp.zeros_like(value)
+    return jnp.concatenate([jnp.where(head == at, value, zero) for at in range(GROUP_HEADS)], axis=0)
+
+
+def lane_halves(value, join):
+    return join(value[:, :LANES], value[:, LANES:])
+
+
+def attend_kernel(place, q_ref, k_ref, v_ref, out_ref, log_ref, score_ref):
+    blocks, width, _ = q_ref.shape
     member = place[0]
 
     def one_query_block(block, _):
-        queries = by_head(qt_ref[block ^ member])
-
-        def one_key_block(key_block, carried):
-            top, total, accs = carried
-            slot = key_block ^ member
-            at = pl.multiple_of(slot * rows, rows)
-            scores = dot(k_ref[slot], queries)
-            new_top = jnp.maximum(top, jnp.max(scores, axis=0, keepdims=True))
-            weights = jnp.exp(scores - new_top)
-            fading = jnp.exp(top - new_top)
-            total = total * fading + jnp.sum(weights, axis=0, keepdims=True)
-            low = weights.astype(bf16)
-            kept = []
-            for head in range(GROUP_HEADS):
-                lanes = slice(head * width, (head + 1) * width)
-                values = vt_ref[head * HD : (head + 1) * HD, pl.ds(at, rows)]
-                kept.append(accs[head] * fading[:, lanes] + dot(values, low[:, lanes]))
-            return new_top, total, tuple(kept)
+        queries = by_head_rows(q_ref[block ^ member])
+
+        def one_score(key_block, top):
+            scores = dot_nt(queries, k_ref[key_block ^ member])
+            score_ref[key_block] = scores
+            return jnp.maximum(top, lane_halves(scores, jnp.maximum))
+
+        top = loop(0, block + 1, one_score, jnp.full((GROUP_HEADS * width, LANES), NEG_BIG, f32))
+        top = jnp.max(top, axis=1, keepdims=True)
+
+        def one_value(key_block, carried):
+            total, acc = carried
+            weights = jnp.exp(score_ref[key_block] - top)
+            total = total + lane_halves(weights, jnp.add)
+            return total, acc + dot(weights.astype(bf16), v_ref[key_block ^ member])
 
         start_state = (
-            jnp.full((1, GROUP_HEADS * width), NEG_BIG, f32),
-            jnp.zeros((1, GROUP_HEADS * width), f32),
-            tuple(jnp.zeros((HD, width), f32) for _ in range(GROUP_HEADS)),
-        )
-        top, total, accs = loop(0, block + 1, one_key_block, start_state)
+            jnp.zeros((GROUP_HEADS * width, LANES), f32),
+            jnp.zeros((GROUP_HEADS * width, GROUP_COLS), f32),
+        )
+        total, acc = loop(0, block + 1, one_value, start_state)
+        total = jnp.sum(total, axis=1, keepdims=True)
+        acc = acc / total
+        log_sums = jnp.broadcast_to(top + jnp.log(total), (GROUP_HEADS * width, LANES))
         for head in range(GROUP_HEADS):
-            lanes = slice(head * width, (head + 1) * width)
-            out_ref[block, head * HD : (head + 1) * HD, :] = (accs[head] / total[:, lanes]).astype(bf16)
-        log_ref[block] = top + jnp.log(total)
+            here = slice(head * width, (head + 1) * width)
+            cols = slice(head * HD, (head + 1) * HD)
+            out_ref[block, cols, :] = acc[here, :].T[cols].astype(bf16)
+            log_ref[block, :, here] = log_sums[here].T[:1]
         return 0
 
     loop(0, blocks, one_query_block, 0)
 
 
 def attend_back_kernel(
-    place, qt_ref, k_ref, v_ref, kt_ref, gt_ref, out_ref, log_ref, dq_ref, dkv_ref, sum_ref, dk_acc, dv_acc, dq_acc, delta_ref
+    place, qt_ref, k_ref, v_ref, gt_ref, out_ref, log_ref, dq_ref, dkv_ref, sum_ref, dk_acc, dv_acc, dq_acc, delta_ref
 ):
     blocks, _, width = qt_ref.shape
-    rows = k_ref.shape[1]
     member = place[0]
 
     def prepare(block, _):
@@ -240,9 +247,10 @@
     dq_acc[...] = jnp.zeros_like(dq_acc)
     sum_ref[...] = jnp.zeros_like(sum_ref)
 
+    head_at = lax.broadcasted_iota(jnp.int32, (width, GROUP_COLS), 1) // HD
+
     def one_key_block(key_block, _):
         slot = key_block ^ member
-        at = pl.multiple_of(slot * rows, rows)
         dk_acc[...] = jnp.zeros_like(dk_acc)
         dv_acc[...] = jnp.zeros_like(dv_acc)
 
@@ -253,10 +261,11 @@
             grad_scores = (prob * (grad_prob - delta_ref[block])).astype(bf16)
             dv_acc[...] += dot_nt(prob.astype(bf16), grads)
             dk_acc[...] += dot_nt(grad_scores, queries)
+            every = dot_tn(grad_scores, k_ref[slot])
+            grad = jnp.zeros((width, GROUP_COLS), f32)
             for head in range(GROUP_HEADS):
-                part = slice(head * HD, (head + 1) * HD)
-                lanes = slice(head * width, (head + 1) * width)
-                dq_acc[block, part, :] += dot(kt_ref[part, pl.ds(at, rows)], grad_scores[:, lanes])
+                grad = jnp.where(head_at == head, every[head * width : (head + 1) * width], grad)
+            dq_acc[block] += grad
             return 0
 
         loop(key_block, blocks, one_query_block, 0)
@@ -267,7 +276,7 @@
     loop(0, blocks, one_key_block, 0)
 
     def write(block, _):
-        grads = dq_acc[block].T * HEAD_SCALE
+        grads = dq_acc[block] * HEAD_SCALE
         dq_ref[block ^ member] = grads.astype(bf16)
         sum_ref[0:1, :] += jnp.sum(grads, axis=0, keepdims=True)
         return 0
@@ -291,16 +300,11 @@
 
 
 def mlp_kernel(place, *refs):
-    normed, grads, slabs = refs[:4], refs[4:8], refs[8:12]
-    down_ref, bias_ref = refs[12:14]
-    branch_own, branch_far, branch_give, norm_own, norm_far, norm_give = refs[14:20]
-    downs, ups, (bias_grad, weight, down_total, up_total) = refs[20:24], refs[24:28], refs[28:]
-    rows = normed[0].shape[0]
-    shard, wide = slabs[0].shape[0], down_ref.shape[0] // PIECES
-    piece = shard // PIECES
-    mine, low = place[1], place[3]
+    normed, grads, slabs, (down_ref, bias_ref) = refs[:4], refs[4:8], refs[8:12], refs[12:14]
+    norm_own, norm_far, norm_give, active_ref, hidden_ref, bias_grad, weight = refs[14:]
+    rows, shard = normed[0].shape[0], slabs[0].shape[0]
     for distance, slab in enumerate(slabs):
-        at = pl.multiple_of((distance ^ mine) * shard, shard)
+        at = pl.multiple_of((distance ^ place[1]) * shard, shard)
         weight[pl.ds(at, shard), :] = slab[...]
     for tile in range(2):
         blocks = (tile, 2 + tile)
@@ -310,32 +314,50 @@
         square = hidden * hidden
         bent = jnp.tanh(GELU_A * hidden * (1.0 + GELU_B * square))
         half = 0.5 * (1.0 + bent)
-        active = (hidden * half).astype(bf16)
+        active_ref[tile] = (hidden * half).astype(bf16)
         slope = half + 0.5 * hidden * (1.0 - bent * bent) * (GELU_A * (1.0 + 3.0 * GELU_B * square))
         grad_hidden = (dot_nt(grad, down_ref[...]) * slope).astype(bf16)
-        norm, branch = dot_nt(grad_hidden, weight[...]), dot(active, down_ref[...])
-        for at in range(2):
-            here = slice(at * rows, (at + 1) * rows)
-            if tile:
-                norm_give[at], branch_give[at] = norm[here].astype(bf16), branch[here].astype(bf16)
-            else:
-                (norm_own, norm_far)[at][...] = norm[here]
-                (branch_own, branch_far)[at][...] = branch[here]
-        down, up = dot_tn(active, grad), dot_tn(tokens, grad_hidden)
+        hidden_ref[tile] = grad_hidden
+        norm = dot_nt(grad_hidden, weight[...])
         bias = jnp.sum(grad_hidden.astype(f32), axis=0, keepdims=True)
-        if tile == 0:
-            down_total[...], up_total[...], bias_grad[...] = down, up, bias
+        if tile:
+            norm_give[0], norm_give[1] = norm[:rows].astype(bf16), norm[rows:].astype(bf16)
+            bias_grad[...] += bias
         else:
+            norm_own[...], norm_far[...] = norm[:rows], norm[rows:]
+            bias_grad[...] = bias
+
+
+def mlp_back_kernel(place, *refs):
+    normed, grads, (active_ref, hidden_ref, down_ref) = refs[:4], refs[4:8], refs[8:11]
+    branch_own, branch_far, branch_give = refs[11:14]
+    pieces, (down_total, up_total) = refs[14:18], refs[18:]
+    rows = normed[0].shape[0]
+    wide = down_ref.shape[0] // PIECES
+    piece = (pieces[0].shape[1] - wide) // 4
+    shard = piece * PIECES
+    mine, low = place[1], place[3]
+    for tile in range(2):
+        blocks = (tile, 2 + tile)
+        tokens = jnp.concatenate([normed[at][...] for at in blocks], axis=0)
+        grad = jnp.concatenate([grads[at][...] for at in blocks], axis=0)
+        down, up = dot_tn(active_ref[tile], grad), dot_tn(tokens, hidden_ref[tile])
+        branch = dot(active_ref[tile], down_ref[...])
+        if tile:
             down_total[...] += down
             up_total[...] += up
-            bias_grad[...] += bias
-    for near, (down_ref, up_ref) in enumerate(zip(downs, ups)):
+            branch_give[0], branch_give[1] = branch[:rows].astype(bf16), branch[rows:].astype(bf16)
+        else:
+            down_total[...], up_total[...] = down, up
+            branch_own[...], branch_far[...] = branch[:rows], branch[rows:]
+    for near, target in enumerate(pieces):
         for side in range(2):
             at = (side << 2 | near) ^ low
-            down_ref[side] = down_total[pl.ds(pl.multiple_of(at * wide, wide), wide), :].astype(bf16)
+            target[side, :wide] = down_total[pl.ds(pl.multiple_of(at * wide, wide), wide), :].astype(bf16)
             for distance in range(4):
                 here = pl.multiple_of((distance ^ mine) * shard + at * piece, piece)
-                up_ref[side, distance] = up_total[pl.ds(here, piece), :].astype(bf16)
+                start = wide + distance * piece
+                target[side, start : start + piece] = up_total[pl.ds(here, piece), :].astype(bf16)
 
 
 def branch_back_kernel(
@@ -398,20 +420,38 @@
         row = grad_w[pl.ds(D + (distance ^ mine), 1), :]
         up_row = jnp.zeros_like(row) if distance else bias_up_ref[...]
         extra = jnp.concatenate([row, up_row, jnp.zeros((EXTRA - 2, D), f32)], axis=0)
-        for near in range(4):
-            for side in range(2):
-                at = (distance ^ mine) * shard + ((side << 2 | near) ^ low) * piece
-                part = grad_w[pl.ds(pl.multiple_of(at, piece), piece), :]
-                target = (near_ref, far_ref)[core]
-                target[far, near * 2 + side] = jnp.concatenate([part, extra], axis=0).astype(bf16)
-
-
-def sum_kernel(place, *refs):
-    firsts, seconds, targets = refs[:4], refs[4:8], refs[8:]
-    wide = firsts[0].shape[1]
-    for side, target in enumerate(targets):
-        target[:wide, :] = sum(ref[side].astype(f32) for ref in firsts).astype(bf16)
-        target[wide:, :] = sum(ref[side].astype(f32) for ref in seconds).astype(bf16)
+
+        def one(index, _, distance=distance, extra=extra):
+            at = (distance ^ mine) * shard + (((index & 1) << 2 | index >> 1) ^ low) * piece
+            part = grad_w[pl.ds(pl.multiple_of(at, piece), piece), :]
+            target = (near_ref, far_ref)[distance & 1]
+            target[distance >> 1, index] = jnp.concatenate([part, extra], axis=0).astype(bf16)
+            return 0
+
+        lax.fori_loop(0, PIECES, one, 0)
+
+
+def sum_kernel(place, part0, part1, part2, part3, down_ref, up_ref):
+    parts, wide = (part0, part1, part2, part3), down_ref.shape[1]
+    down_ref[...] = sum(part[:, :wide].astype(f32) for part in parts).astype(bf16)
+    up_ref[...] = sum(part[:, wide:].astype(f32) for part in parts).astype(bf16)
+
+
+def heads_back_kernel(place, normed_t_ref, query_t_ref, dq_ref, dkv_ref, sum_ref, near_ref, far_ref, aq, akv):
+    blocks, query_rows, _ = dq_ref.shape
+    rows = dkv_ref.shape[1]
+    chunk = min(blocks, 4)
+    for start in range(0, blocks, chunk):
+        dkv = jnp.concatenate([dkv_ref[start + at] for at in range(chunk)], axis=0)
+        dq = jnp.concatenate([dq_ref[start + at] for at in range(chunk)], axis=0)
+        kv = dot(normed_t_ref[:, start * rows : (start + chunk) * rows], dkv)
+        q = dot(query_t_ref[:, start * query_rows : (start + chunk) * query_rows], dq)
+        if start:
+            akv[...] += kv
+            aq[...] += q
+        else:
+            akv[...], aq[...] = kv, q
+    arrange_heads(place, aq, akv, sum_ref, near_ref, far_ref)
 
 
 def arrange_heads(place, q_ref, kv_ref, sum_ref, near_ref, far_ref):
@@ -435,59 +475,20 @@
                     target[relative >> 1, part ^ ((place[3] >> 2) & 1)] = both
 
 
-def project_back_kernel(
-    place,
-    normed_t_ref,
-    query_t_ref,
-    dq_ref,
-    dkv_ref,
-    sum_ref,
-    slab0,
-    slab1,
-    slab2,
-    slab3,
-    keep_ref,
-    give_ref,
-    near_ref,
-    far_ref,
-    wq,
-    wkv,
-    aq,
-    akv,
-):
+def rows_back_kernel(place, dq_ref, dkv_ref, slab0, slab1, slab2, slab3, keep_ref, give_ref, wq, wkv):
     load_heads(place, (slab0, slab1, slab2, slab3), wq, wkv)
-    blocks, query_rows, _ = dq_ref.shape
-    rows = dkv_ref.shape[1]
-    half = keep_ref.shape[0]
+    query_rows, half = dq_ref.shape[1], keep_ref.shape[0]
     own = pl.ds(pl.multiple_of(place[2] * query_rows, query_rows), query_rows)
-    aq[...] = jnp.zeros_like(aq)
-    akv[...] = jnp.zeros_like(akv)
-    chunk = min(blocks, max(4, LANES // query_rows))
-
-    def one(at, _):
-        start = at * chunk
-        dkv = jnp.concatenate([dkv_ref[start + k] for k in range(chunk)], axis=0)
-        dq = jnp.concatenate([dq_ref[start + k] for k in range(chunk)], axis=0)
-        tokens = pl.ds(pl.multiple_of(start * rows, chunk * rows), chunk * rows)
-        queries = pl.ds(pl.multiple_of(start * query_rows, chunk * query_rows), chunk * query_rows)
-        akv[...] += dot(normed_t_ref[:, tokens], dkv)
-        aq[...] += dot(query_t_ref[:, queries], dq)
-        return 0
-
-    loop(0, blocks // chunk, one, 0)
-    arrange_heads(place, aq, akv, sum_ref, near_ref, far_ref)
-
-    for core, ref in enumerate((keep_ref, give_ref)):
-
-        def two(at, _, core=core, ref=ref):
+    for core, ref in ((1, give_ref), (0, keep_ref)):
+
+        def one(at, _, core=core, ref=ref):
             slot = at + core * half
-            grad = dot_nt(dkv_ref[slot], wkv[...])
-            ref[at] = grad.astype(bf16)
+            ref[at] = dot_nt(dkv_ref[slot], wkv[...]).astype(bf16)
             low = ref[at, own, :].astype(f32)
             ref[at, own, :] = (low + dot_nt(dq_ref[slot], wq[...])).astype(bf16)
             return 0
 
-        loop(0, half, two, 0)
+        loop(0, half, one, 0)
 
 
 def stream_back_kernel(place, part0, part1, part2, part3, resid_ref, grad_middle_ref, vec_ref, out_ref):
@@ -499,23 +500,24 @@
     out_ref[...] = (total - total[:, D - 1 :]).astype(bf16)[:, : D - 1]
 
 
-def down_out_kernel(place, part0, part1, part2, part3, down_ref, out_ref):
-    wide, rows = down_ref.shape[0] // PIECES, out_ref.shape[0] // PIECES
+def down_out_kernel(place, part0, part1, part2, part3, out_ref):
+    wide = part0.shape[1]
     for near, part in enumerate((part0, part1, part2, part3)):
         for side in range(2):
-            at = (side << 2 | near) ^ place[3]
-            down_ref[pl.ds(pl.multiple_of(at * wide, wide), wide), :] = part[side, :wide].astype(f32)
-            out_ref[pl.ds(pl.multiple_of(at * rows, rows), rows), :] = part[side, wide:].astype(f32)
-
-
-def up_out_kernel(place, part0, part1, part2, part3, up_ref):
-    rows = part0.shape[2]
+            at = pl.multiple_of(((side << 2 | near) ^ place[3]) * wide, wide)
+            out_ref[pl.ds(at, wide), :] = part[side].astype(f32)
+
+
+def up_out_kernel(place, part0, part1, part2, part3, up_ref, out_ref):
+    rows = out_ref.shape[0] // PIECES
     for near, part in enumerate((part0, part1, part2, part3)):
         for side in range(2):
             at = pl.multiple_of(((side << 2 | near) ^ place[3]) * rows, rows)
             for slab in range(4):
                 col = pl.multiple_of((slab ^ place[1]) * D, LANES)
-                up_ref[pl.ds(at, rows), pl.ds(col, D)] = part[side, slab].astype(f32)
+                value = part[side, slab * rows : (slab + 1) * rows]
+                up_ref[pl.ds(at, rows), pl.ds(col, D)] = value.astype(f32)
+            out_ref[pl.ds(at, rows), :] = part[side, 4 * rows :].astype(f32)
 
 
 def heads_out_kernel(place, part0, part1, part2, part3, weight_ref, out_ref, gain_ref, bias_ref, pieces):
@@ -682,12 +684,12 @@
         projected = (
             shape((ctx_count, rows, GROUP_COLS), bf16),
             shape((ctx_count, rows, GROUP_COLS), bf16),
-            shape((GROUP_COLS, tokens), bf16),
+            shape((ctx_count, query_rows, GROUP_COLS), bf16),
             shape((ctx_count, GROUP_COLS, query_rows), bf16),
         )
         work = 5 * tokens * D * GROUP_COLS
         if 4 * tokens * D * 2 < VMEM_LIMIT:
-            normed, keys, values, values_t, queries_t = call(
+            normed, keys, values, queries, queries_t = call(
                 project_kernel,
                 "project",
                 (shape((ctx_count, rows, D), bf16), *projected),
@@ -699,7 +701,7 @@
             normed = (jnp.concatenate(pieces).astype(f32) * gain).astype(bf16)
             block = lambda *dims: pl.BlockSpec((1,) + dims, lambda at: (at, 0, 0))
             whole = lambda *dims: pl.BlockSpec(dims, lambda at: (0,) * len(dims))
-            keys, values, values_t, queries_t = call(
+            keys, values, queries, queries_t = call(
                 project_block_kernel,
                 "project",
                 projected,
@@ -713,11 +715,12 @@
                 out_specs=(
                     block(rows, GROUP_COLS),
                     block(rows, GROUP_COLS),
-                    pl.BlockSpec((GROUP_COLS, rows), lambda at: (0, at)),
+                    block(query_rows, GROUP_COLS),
                     block(GROUP_COLS, query_rows),
                 ),
             )
         queries_t = widened(queries_t)
+        queries = jnp.pad(queries, ((0, 0), (0, width - query_rows), (0, 0)))
         pairs = GROUP_HEADS * query_rows * rows * ctx_count * (ctx_count + 1) // 2
         outs, logs = call(
             attend_kernel,
@@ -726,33 +729,15 @@
                 shape((ctx_count, GROUP_COLS, width), bf16),
                 shape((ctx_count, 1, GROUP_HEADS * width), f32),
             ),
-            (place, queries_t, keys, values_t),
+            (place, queries, keys, values),
             flops=4 * HD * pairs,
             exps=pairs,
+            scratch=[pltpu.VMEM((ctx_count, GROUP_HEADS * width, rows), f32)],
         )
         outs, *up_got = together(
             (outs, *(to_fsdp(up_sent[distance], distance) for distance in (1, 2, 3)))
         )
         attended = group_all_to_all(outs[:, :, :query_rows])
-        if 4 * tokens * D * 2 < VMEM_LIMIT:
-            normed_t, query_t, keys_t = call(
-                collect_kernel,
-                "collect",
-                (
-                    shape((D, tokens), bf16),
-                    shape((D, ctx_count * query_rows), bf16),
-                    shape((GROUP_COLS, tokens), bf16),
-                ),
-                (place, normed, keys),
-            )
-        else:
-            normed_query = lax.dynamic_index_in_dim(
-                normed.reshape(ctx_count, splits, query_rows, D), place[2], 1, keepdims=False
-            )
-            normed_t, query_t = normed.reshape(tokens, D).T, normed_query.reshape(-1, D).T
-            keys_t = keys.reshape(tokens, GROUP_COLS).T
-        attended, normed_t, query_t, keys_t = together((attended, normed_t, query_t, keys_t))
-
         w_out_all = (w_out, to_core(w_out), out_far, to_core(out_far))
         top = swap_sequences(grad_out)
         grad_result = jnp.pad(top.astype(f32), ((0, 0), (0, 1)))
@@ -767,52 +752,59 @@
             scratch=[pltpu.VMEM((rows, D), f32)],
         )
         piece = shard // PIECES
-        (
-            branch_own,
-            branch_far,
-            branch_give,
-            norm_own,
-            norm_far,
-            norm_give,
-            *both_sums,
-            bias_up_sum,
-        ) = call(
+        normed_mlp, normed = together((normed_mlp, normed))
+        if 4 * tokens * D * 2 < VMEM_LIMIT:
+            normed_t, query_t = call(
+                collect_kernel,
+                "collect",
+                (
+                    shape((D, tokens), bf16),
+                    shape((D, ctx_count * query_rows), bf16),
+                ),
+                (place, normed),
+            )
+        else:
+            normed_query = lax.dynamic_index_in_dim(
+                normed.reshape(ctx_count, splits, query_rows, D), place[2], 1, keepdims=False
+            )
+            normed_t, query_t = normed.reshape(tokens, D).T, normed_query.reshape(-1, D).T
+        normed_all = over_fsdp(normed_mlp)
+        far_normed, normed_t, query_t = together((normed_all[2], normed_t, query_t))
+        normed_all = (normed_all[0], normed_all[1], far_normed, to_core(far_normed))
+        norm_own, norm_far, norm_give, active, grad_hidden, bias_up_sum = call(
             mlp_kernel,
             "mlp",
             (
                 shape((rows, D), f32),
                 shape((rows, D), f32),
                 shape((2, rows, D), bf16),
+                shape((2, 2 * rows, hidden), bf16),
+                shape((2, 2 * rows, hidden), bf16),
+                shape((1, hidden), f32),
+            ),
+            (place, *normed_all, *grads_mlp, up_sent[0], *up_got, w_down, bias_hidden),
+            flops=24 * rows * D * hidden,
+            exps=4 * rows * hidden,
+            scratch=[pltpu.VMEM((D, hidden), bf16)],
+        )
+        norm_got = to_core(norm_give)
+        norm_far_got = to_chip_row((norm_far + norm_got[1]).astype(bf16))
+        norm_sent, active, grad_hidden = together((norm_got, active, grad_hidden))
+        branch_own, branch_far, branch_give, *both_sums = call(
+            mlp_back_kernel,
+            "mlp_back",
+            (
                 shape((rows, D), f32),
                 shape((rows, D), f32),
                 shape((2, rows, D), bf16),
-                *(shape((2, hidden // PIECES, D), bf16) for _ in range(4)),
-                *(shape((2, fsdp_count, piece, hidden), bf16) for _ in range(4)),
-                shape((1, hidden), f32),
+                *(shape((2, hidden // PIECES + 4 * piece, D), bf16) for _ in range(4)),
             ),
-            (
-                place,
-                *over_fsdp(normed_mlp),
-                *grads_mlp,
-                up_sent[0],
-                *up_got,
-                w_down,
-                bias_hidden,
-            ),
-            flops=48 * rows * D * hidden,
-            exps=4 * rows * hidden,
-            scratch=[
-                pltpu.VMEM((D, hidden), bf16),
-                pltpu.VMEM((hidden, D), f32),
-                pltpu.VMEM((D, hidden), f32),
-            ],
-        )
-        norm_got = to_core(norm_give)
-        norm_far_got = to_chip_row((norm_far + norm_got[1]).astype(bf16))
-        down_sums, up_sums = both_sums[:4], both_sums[4:]
-        norm_far_got, *down_got = together((norm_far_got, *to_square(down_sums[1:])))
-        down_keep, down_give = (
-            sum((part[side] for part in down_got), start=down_sums[0][side]) for side in range(2)
+            (place, *normed_all, *grads_mlp, active, grad_hidden, w_down),
+            flops=LONG,
+            scratch=[pltpu.VMEM((hidden, D), f32), pltpu.VMEM((D, hidden), f32)],
+        )
+        norm_far_got, branch_own, branch_far, branch_give, *both_sums = together(
+            (norm_far_got, branch_own, branch_far, branch_give, *both_sums)
         )
         grad_middle, grad_branch, grad_attended, row_sums = call(
             branch_back_kernel,
@@ -840,10 +832,10 @@
         branch_far_got = to_chip_row((branch_far + branch_got[1]).astype(bf16))
         branch_mlp = branch_own + branch_got[0] + branch_far_got + vec[3:4]
         stream_out = (middle + centered(branch_mlp)).astype(bf16)[:, : D - 1]
-        grads, out_sum = together((grads, out_sum))
+        grads, out_sum, stream_out = together((grads, out_sum, stream_out))
+        stream_out = swap_sequences(stream_out)
         out_got = to_chip_row(out_sum[1])
-        up_got = to_square(up_sums[1:])
-        down_got = to_ctx(down_give, 4)
+        both_got = to_square(both_sums[1:])
         dq, dkv, head_sums = call(
             attend_back_kernel,
             "attend_back",
@@ -852,41 +844,71 @@
                 shape((ctx_count, rows, 2 * GROUP_COLS), bf16),
                 shape((8, GROUP_COLS), f32),
             ),
-            (place, queries_t, keys, values, keys_t, widened(grads), outs, logs),
+            (place, queries_t, keys, values, widened(grads), outs, logs),
             flops=10 * HD * pairs,
             exps=pairs,
             scratch=[
                 pltpu.VMEM((rows, GROUP_COLS), f32),
                 pltpu.VMEM((rows, GROUP_COLS), f32),
-                pltpu.VMEM((ctx_count, GROUP_COLS, width), f32),
+                pltpu.VMEM((ctx_count, width, GROUP_COLS), f32),
                 pltpu.VMEM((ctx_count, 1, GROUP_HEADS * width), f32),
             ],
         )
         dq = dq[:, :query_rows]
-        dq, dkv, out_got, down_got, *up_got = together((dq, dkv, out_got, down_got, *up_got))
-        up_keep, up_give = (
-            sum((part[side] for part in up_got), start=up_sums[0][side]) for side in range(2)
+        dq, dkv, out_got = together((dq, dkv, out_got))
+
+        head_shapes = tuple(
+            shape((2, 2, shard // 2 + EXTRA, 3 * GROUP_COLS), bf16) for _ in range(2)
+        )
+        if 4 * tokens * D * 2 < VMEM_LIMIT:
+            head_near, head_give = call(
+                heads_back_kernel,
+                "heads_back",
+                head_shapes,
+                (place, normed_t, query_t, dq, dkv, head_sums),
+                flops=work,
+                scratch=[pltpu.VMEM((D, GROUP_COLS), f32), pltpu.VMEM((D, 2 * GROUP_COLS), f32)],
+            )
+        else:
+            flat_q, flat_kv = dq.reshape(-1, GROUP_COLS), dkv.reshape(tokens, 2 * GROUP_COLS)
+            head_near, head_give = call(
+                arrange_heads,
+                "arrange_heads",
+                head_shapes,
+                (place, dot(query_t, flat_q), dot(normed_t, flat_kv), head_sums),
+            )
+        head_near, head_give, stream_out, out_got, *both_got = together(
+            (head_near, head_give, stream_out, out_got, *both_got)
+        )
+        down_sum, up_sum = call(
+            sum_kernel,
+            "sum",
+            (
+                shape((2, hidden // PIECES, D), bf16),
+                shape((2, fsdp_count * piece, hidden), bf16),
+            ),
+            (place, both_sums[0], *both_got),
         )
         out_sums = [
             out_sum[0, 2 * near : 2 * near + 2] + out_got[2 * near : 2 * near + 2] for near in range(4)
         ]
-        dq, dkv, up_give, *out_sums = together((dq, dkv, up_give, *out_sums))
-        up_got = to_ctx(up_give, 4)
+        head_sum = head_near + to_core(head_give)
+        dq, head_near, head_give, down_sum, up_sum, *out_sums = together(
+            (dq, head_sum[0], head_sum[1], down_sum, up_sum, *out_sums)
+        )
+        head_got = to_chip_row(head_give)
+        down_got, up_got = to_ctx(down_sum, 4), to_ctx(up_sum, 4)
         out_got = to_square(out_sums[1:])
 
         row_shapes = (shape((half, rows, D), bf16), shape((half, rows, D), bf16))
-        head_shapes = tuple(
-            shape((2, 2, shard // 2 + EXTRA, 3 * GROUP_COLS), bf16) for _ in range(2)
-        )
         if 4 * tokens * D * 2 < VMEM_LIMIT:
-            keep_rows, give_rows, head_near, head_give = call(
-                project_back_kernel,
-                "project_back",
-                row_shapes + head_shapes,
-                (place, normed_t, query_t, dq, dkv, head_sums, *w_heads),
-                flops=2 * work,
-                scratch=head_weights
-                + [pltpu.VMEM((D, GROUP_COLS), f32), pltpu.VMEM((D, 2 * GROUP_COLS), f32)],
+            keep_rows, give_rows = call(
+                rows_back_kernel,
+                "rows_back",
+                row_shapes,
+                (place, dq, dkv, *w_heads),
+                flops=work,
+                scratch=head_weights,
             )
         else:
             weights = by_row(w_heads)
@@ -899,16 +921,18 @@
             grad_rows = (grad_rows + jnp.where(chosen, grad_query, 0.0)).astype(bf16)
             grad_rows = grad_rows.reshape(ctx_count, rows, D)
             keep_rows, give_rows = grad_rows[:half], grad_rows[half:]
-            head_near, head_give = call(
-                arrange_heads,
-                "arrange_heads",
-                head_shapes,
-                (place, dot(query_t, flat_q), dot(normed_t, flat_kv), head_sums),
-            )
-        keep_rows, up_got, *out_got = together((keep_rows, up_got, *out_got))
-        head_got, rows_got = together((to_core(head_give), to_core(give_rows)))
+        keep_rows, give_rows, head_got, *out_got = together(
+            (keep_rows, give_rows, head_got, *out_got)
+        )
+
+        def both_sides(own, other):
+            return over_rest(jnp.stack([own[0] + other[1], own[1] + other[0]]))
+
+        rows_got = to_core(give_rows)
         head_sum = head_near + head_got
-        head_got = to_chip_row(head_sum[1])
+        out_sum = sum(out_got, start=out_sums[0])
+        rows_got, head_sum, out_sum = together((rows_got, head_sum, out_sum))
+        head_got, out_got = to_ctx(head_sum, 4), to_ctx(out_sum, 4)
         if steps == 2:
             parts = [keep_rows[slot] + rows_got[slot] for slot in range(4)]
         else:
@@ -917,24 +941,19 @@
                 both = both[: 1 << bit] + to_ctx(both[1 << bit :], 1 << bit)
             parts = [both[slot] for slot in range(4)]
         rows_got = to_square(parts[1:])
-        out_keep, out_give = (
-            sum((part[side] for part in out_got), start=out_sums[0][side]) for side in range(2)
-        )
-        out_got = to_ctx(out_give, 4)
-        down, up_rows = over_rest(down_keep + down_got), over_rest(up_keep + up_got)
-        up_got = [to_fsdp(up_rows[distance], distance) for distance in (1, 2, 3)]
-
-        head_got, out_got, *up_got = together((head_got, out_got, *up_got))
-        head_sum = head_sum[0] + head_got
-        head_got = to_ctx(head_sum[1], 4)
-        ups = jnp.stack([up_rows[0], *up_got])
-        up_got = to_ctx(ups, 4)
-        out_rows = over_rest(out_keep + out_got)
-        sums = out_rows[piece:].astype(f32)
-        downs = jnp.concatenate([down, out_rows[:piece]])
-        down_got = to_ctx(downs, 4)
-
-        *rows_got, head_got, up_got, down_got = together((*rows_got, head_got, up_got, down_got))
+        up_got, down_got, *rows_got = together((up_got, down_got, *rows_got))
+        up_sum = both_sides(up_sum, up_got)
+        ups = [up_sum[:, distance * piece : (distance + 1) * piece] for distance in range(fsdp_count)]
+        ups = [ups[0]] + [to_fsdp(ups[distance], distance) for distance in (1, 2, 3)]
+        downs = both_sides(down_sum, down_got)
+        downs = (downs, *to_square((downs,) * 3))
+        *ups, head_got, out_got = together((*ups, head_got, out_got))
+        outs = both_sides(out_sum, out_got)
+        sums = outs[0, piece:].astype(f32)
+        ups = jnp.concatenate([*ups, outs[:, :piece]], axis=1)
+        ups = (ups, *to_square((ups,) * 3))
+        heads = both_sides(head_sum, head_got)
+        heads = (heads, *to_square((heads,) * 3))
         (grad_stream,) = call(
             stream_back_kernel,
             "stream_back",
@@ -942,14 +961,13 @@
             (place, parts[0], *rows_got, resid, grad_middle, vec),
         )
         grad_stream = swap_sequences(grad_stream)
-        heads = over_rest(head_sum[0] + head_got)
-        head_got = to_ctx(heads, 4)
-        downs = jnp.stack([downs, down_got])
-        downs = (downs, *to_square((downs,) * 3))
-        ups = jnp.stack([ups, up_got])
-        ups = (ups, *to_square((ups,) * 3))
-        heads = jnp.stack([heads, head_got])
-        heads = (heads, *to_square((heads,) * 3))
+        (grad_w_down,) = call(down_out_kernel, "down_out", (shape((hidden, D), f32),), (place, *downs))
+        grad_w_up, grad_w_out = call(
+            up_out_kernel,
+            "up_out",
+            (shape((shard, fsdp_count * hidden), f32), shape((shard, D), f32)),
+            (place, *ups),
+        )
         grad_w_qkv, grad_gain_attn, grad_bias_qv = call(
             heads_out_kernel,
             "heads_out",
@@ -961,18 +979,8 @@
             (place, *heads, w_qkv),
             scratch=[pltpu.VMEM((4, 2, shard // 2 + EXTRA, 3 * GROUP_COLS), bf16)],
         )
-        grad_w_down, grad_w_out = call(
-            down_out_kernel,
-            "down_out",
-            (shape((hidden, D), f32), shape((shard, D), f32)),
-            (place, *downs),
-        )
-        (grad_w_up,) = call(
-            up_out_kernel, "up_out", (shape((shard, fsdp_count * hidden), f32),), (place, *ups)
-        )
-
         return (
-            swap_sequences(stream_out),
+            stream_out,
             grad_stream.astype(f32),
             grad_gain_attn.reshape(-1) / gain_attn.astype(f32),
             grad_w_qkv,

time: 315 us -> 295 us (0.937)
  starting transfers between devices: 102 us -> 73.1 us
  waiting for transfers between devices: 84.8 us -> 91.4 us
  Pallas kernels: 95.7 us -> 99.7 us
  other arithmetic: 15.4 us -> 12.1 us
    ppermute x69 -> x63, starting transfers between devices: 91.4 us -> 62.7 us  [send(): return lax.ppermute(value, AXES, pairs)]
    ppermute x69 -> x63, waiting for transfers between devices: 81.5 us -> 87.3 us  [send(): return lax.ppermute(value, AXES, pairs)]
    add x8 -> x5, other arithmetic: 5.19 us -> 0.27 us  [the longest x1 0.13 us: local(): head_sum = head_near + to_core(head_give)]
    pallas_call x15 -> x18, Pallas kernels: 95.7 us -> 99.7 us  [call(): pl.pallas_call(body, out_shape=tuple(outs), scratch_shapes=list(scratch),...]
    unnamed x128 -> x114, local copies, waits for them, and re-layouts: 8.78 us -> 10.3 us
  transfers between devices with their start and end apart: 71 -> 65, of which waited for: 23 -> 23; matrix products, arithmetic and copies ran while one was open for 5% -> 5% of each run, Pallas kernels for 27% -> 30%
where the time goes in v1:
time: 295 us; the launch traced here: 291 us
  Pallas kernels  99.7 us (34%)
  waiting for transfers between devices  91.4 us (31%)
  starting transfers between devices  73.1 us (25%)
  local copies, waits for them, and re-layouts  13.3 us (5%)
  other arithmetic  12.1 us (4%)
    pallas_call x18, Pallas kernels, call(): pl.pallas_call(body, out_shape=tuple(outs), scratch_shapes=list(scratch),...  99.7 us
    ppermute x63, waiting for transfers between devices, send(): return lax.ppermute(value, AXES, pairs)  87.3 us
    ppermute x63, starting transfers between devices, send(): return lax.ppermute(value, AXES, pairs)  62.7 us
    all_to_all x2, starting transfers between devices, group_all_to_all(): lax.all_to_all(value, AXES, 0, 0, axis_index_groups=groups, tiled=True)  10.4 us
    unnamed x114, local copies, waits for them, and re-layouts  10.3 us
  transfers between devices with their start and end apart: 65, of which 23 were waited for; matrix products, arithmetic and copies ran while one was open for 5% of the time, Pallas kernels for 30%

profile of v1, /device:TPU:0, one launch (start us, length us, event | category | flops | bytes accessed | tf_op | source)
XLA Modules:
  0.0 291.4 jit_solution(1837760036671309123)
XLA Ops:
  19.0 3.0 %collective-permute-start.9 = (bf16[1,256,768]{2,1,0:T(8,128)(2,1)}, bf16[1,256,768]{2,1,0:T(8,128)(2,1)S(1)}, u32[]{:S(2)}, u32[]{:S(2)}) collective-permute-start(bf16[1,256,768]{2,1,0:T(8,128)(2,1)} %get-tuple-element.136.refs_6_), channel_id=1, source_target_pairs={{0,3},{1,2},{2,1},{3,0},{4,7},{5,6},{6,5},{7,4},{8,11},{9,10},{10,... | collective-permute-start | bytes 1179656 | tf_op jit(solution)/shard_map/ppermute | solution.py:558
  24.6 6.8 %collective-permute-done.10.slab2 = bf16[192,768]{1,0:T(8,128)(2,1)S(1)} collective-permute-done((bf16[192,768]{1,0:T(8,128)(2,1)S(1)}, bf16[192,768]{1,0:T(8,128)(2,1)S(1)}, u32[]{:S(2)}, u32[]{:S(2)}) %collective-permute-start.10) | collective-permute-done | bytes 294944 | tf_op jit(solution)/shard_map/ppermute | solution.py:558
  32.2 8.3 %collective-permute-done.8.refs_8_ = bf16[1,256,768]{2,1,0:T(8,128)(2,1)S(1)} collective-permute-done((bf16[1,256,768]{2,1,0:T(8,128)(2,1)}, bf16[1,256,768]{2,1,0:T(8,128)(2,1)S(1)}, u32[]{:S(2)}, u32[]{:S(2)}) %collective-permute-start.8) | collective-permute-done | bytes 393248 | tf_op jit(solution)/shard_map/ppermute | solution.py:558
  48.5 6.9 %project.1 = (bf16[8,256,768]{2,1,0:T(8,128)(2,1)}, bf16[8,256,192]{2,1,0:T(8,128)(2,1)}, bf16[8,256,192]{2,1,0:T(8,128)(2,1)}, bf16[8,128,192]{2,1,0:T(8,128)(2,1)}, bf16[8,192,128]{2,1,0:T(8,128)(2,1)}) custom-call(s32[4]{0:T(128)} %pad_add_fusion.place, bf16[192,576]{1,0:T(8,128)(2,1)} %get-tuple-element.132.refs_0_.slab0, bf16[192,576]{1,0:T(8,128)(2,1)} %copy-done.49, ...), custom_call_target="tpu_custom_call" | custom-call | flops 1509949440 | bytes 9540112 | tf_op jit(solution)/shard_map/project/pallas_call | solution.py:75
  55.4 8.6 %attend.1 = (bf16[8,192,128]{2,1,0:T(8,128)(2,1)}, f32[8,1,384]{2,1,0:T(1,128)}) custom-call(s32[4]{0:T(128)} %pad_add_fusion.place, bf16[8,128,192]{2,1,0:T(8,128)(2,1)} %get-tuple-element.141.q_ref, bf16[8,256,192]{2,1,0:T(8,128)(2,1)} %get-tuple-element.142.k_ref, bf16[8,256,192]{2,1,0:T(8,128)(2,1)} %get-tuple-element.143.v_ref), custom_call_target="tpu_custom_call" | custom-call | flops 905969664 | bytes 2371600 | tf_op jit(solution)/shard_map/attend/pallas_call | solution.py:75
  64.8 6.8 %all-to-all-start = ((bf16[8,192,128]{2,1,0:T(8,128)(2,1)}), bf16[8,192,128]{2,1,0:T(8,128)(2,1)S(1)}, u32[]{:S(2)}, u32[]{:S(2)}) async-start(bf16[8,192,128]{2,1,0:T(8,128)(2,1)} %get-tuple-element.148.out_ref), calls=%async_computation | async-start | bytes 786432 | tf_op jit(solution)/shard_map/all_to_all | solution.py:581
  74.8 4.1 %all-to-all-done.att_ref = bf16[8,192,128]{2,1,0:T(8,128)(2,1)S(1)} async-done(((bf16[8,192,128]{2,1,0:T(8,128)(2,1)}), bf16[8,192,128]{2,1,0:T(8,128)(2,1)S(1)}, u32[]{:S(2)}, u32[]{:S(2)}) %all-to-all-start) | async-done | bytes 393248 | tf_op jit(solution)/shard_map/all_to_all | solution.py:581
  79.7 3.5 %middle.1 = (f32[256,768]{1,0:T(8,128)}, bf16[256,768]{1,0:T(8,128)(2,1)}) custom-call(s32[4]{0:T(128)} %pad_add_fusion.place, bf16[8,192,128]{2,1,0:T(8,128)(2,1)} %copy-done.3, f32[256,768]{1,0:T(8,128)} %get-tuple-element.149.resid_ref, f32[4,768]{1,0:T(4,128)} %reshape.109.vec_ref, bf16[192,768]{1,0:T(8,128)(2,1)} %slab0.3, bf16[192,768]{1,0:T(8,128)(2,1)} %copy-done.7, ...), custom_call_target="tpu_custom_call" | custom-call | flops 301989888 | bytes 3551248 | tf_op jit(solution)/shard_map/middle/pallas_call | solution.py:75
  85.3 5.4 %collect.1 = (bf16[768,2048]{1,0:T(8,128)(2,1)}, bf16[768,1024]{1,0:T(8,128)(2,1)}) custom-call(s32[4]{0:T(128)} %pad_add_fusion.place, bf16[8,256,768]{2,1,0:T(8,128)(2,1)} %get-tuple-element.154.normed_ref), custom_call_target="tpu_custom_call" | custom-call | bytes 7864336 | tf_op jit(solution)/shard_map/collect/pallas_call | solution.py:75
  90.8 4.0 %collective-permute-done.20.refs_2_ = bf16[256,768]{1,0:T(8,128)(2,1)S(1)} collective-permute-done((bf16[256,768]{1,0:T(8,128)(2,1)}, bf16[256,768]{1,0:T(8,128)(2,1)S(1)}, u32[]{:S(2)}, u32[]{:S(2)}) %collective-permute-start.20) | collective-permute-done | bytes 393248 | tf_op jit(solution)/shard_map/ppermute | solution.py:558
  97.3 8.8 %mlp.1 = (f32[256,768]{1,0:T(8,128)}, f32[256,768]{1,0:T(8,128)}, bf16[2,256,768]{2,1,0:T(8,128)(2,1)}, bf16[2,512,768]{2,1,0:T(8,128)(2,1)}, bf16[2,512,768]{2,1,0:T(8,128)(2,1)}, /*index=5*/f32[1,768]{1,0:T(1,128)}) custom-call(s32[4]{0:T(128)} %pad_add_fusion.place, bf16[256,768]{1,0:T(8,128)(2,1)} %get-tuple-element.153.refs_0_, ...), custom_call_target="tpu_custom_call" | custom-call | flops 3623878656 | bytes 11016208 | tf_op jit(solution)/shard_map/mlp/pallas_call | solution.py:75
  111.7 9.0 %mlp_back.1 = (f32[256,768]{1,0:T(8,128)}, f32[256,768]{1,0:T(8,128)}, bf16[2,256,768]{2,1,0:T(8,128)(2,1)}, bf16[2,192,768]{2,1,0:T(8,128)(2,1)}, bf16[2,192,76...) custom-call(s32[4]{0:T(128)} %pad_add_fusion.place, ...), custom_call_target="tpu_custom_call" | custom-call | flops 99999997952 | bytes 12189712 | tf_op jit(solution)/shard_map/mlp_back/pallas_call | solution.py:75
  122.1 4.2 %branch_back.1 = (f32[256,768]{1,0:T(8,128)}, bf16[256,768]{1,0:T(8,128)(2,1)}, bf16[8,192,128]{2,1,0:T(8,128)(2,1)}, f32[8,768]{1,0:T(8,128)}) custom-call(s32[4]{0:T(128)} %pad_add_fusion.place, f32[256,768]{1,0:T(8,128)} %get-tuple-element.165.own_ref, bf16[2,256,768]{2,1,0:T(8,128)(2,1)} %copy-done.2, bf16[256,768]{1,0:T(8,128)(2,1)} %copy-done.24, ...), custom_call_target="tpu_custom_call" | custom-call | flops 603979776 | bytes 5934608 | tf_op jit(solution)/shard_map/branch_back/pallas_call | solution.py:75
  126.3 3.7 %out_back.1 = (bf16[2,8,32,768]{3,2,1,0:T(8,128)(2,1)}, bf16[2,8,32,768]{3,2,1,0:T(8,128)(2,1)}) custom-call(s32[4]{0:T(128)} %pad_add_fusion.place, bf16[8,192,128]{2,1,0:T(8,128)(2,1)} %copy-done.3, bf16[256,768]{1,0:T(8,128)(2,1)} %get-tuple-element.182.grad_ref, f32[8,768]{1,0:T(8,128)} %get-tuple-element.183.sum_ref, ...), custom_call_target="tpu_custom_call" | custom-call | flops 301989888 | bytes 2386960 | tf_op jit(solution)/shard_map/out_back/pallas_call | solution.py:75
  132.4 3.6 %all-to-all-start.1 = ((bf16[8,192,128]{2,1,0:T(8,128)(2,1)}), bf16[8,192,128]{2,1,0:T(8,128)(2,1)S(1)}, u32[]{:S(2)}, u32[]{:S(2)}) async-start(bf16[8,192,128]{2,1,0:T(8,128)(2,1)} %get-tuple-element.181), calls=%async_computation.1 | async-start | bytes 786432 | tf_op jit(solution)/shard_map/all_to_all | solution.py:581
  147.0 16.9 %attend_back.1 = (bf16[8,128,192]{2,1,0:T(8,128)(2,1)}, bf16[8,256,384]{2,1,0:T(8,128)(2,1)}, f32[8,192]{1,0:T(8,128)}) custom-call(s32[4]{0:T(128)} %pad_add_fusion.place, bf16[8,192,128]{2,1,0:T(8,128)(2,1)} %get-tuple-element.159.qt_ref, bf16[8,256,192]{2,1,0:T(8,128)(2,1)} %get-tuple-element.142.k_ref, bf16[8,256,192]{2,1,0:T(8,128)(2,1)} %get-tuple-element.143.v_ref, ...), custom_call_target="tpu_custom_call" | custom-call | flops 2264924160 | bytes 4737040 | tf_op jit(solution)/shard_map/attend_back/pallas_call | solution.py:75
  163.9 6.8 %heads_back.1 = (bf16[2,2,104,576]{3,2,1,0:T(8,128)(2,1)}, bf16[2,2,104,576]{3,2,1,0:T(8,128)(2,1)}) custom-call(s32[4]{0:T(128)} %pad_add_fusion.place, bf16[768,2048]{1,0:T(8,128)(2,1)} %get-tuple-element.157.normed_t_ref, bf16[768,1024]{1,0:T(8,128)(2,1)} %get-tuple-element.158.query_t_ref, bf16[8,128,192]{2,1,0:T(8,128)(2,1)} %get-tuple-element.215.dq_ref, ...), custom_call_target="tpu_custom_call" | custom-call | flops 1509949440 | bytes 7649296 | tf_op jit(solution)/shard_map/heads_back/pallas_call | solution.py:75
  170.8 3.1 %collective-permute-done.36.part3 = bf16[2,192,768]{2,1,0:T(8,128)(2,1)} collective-permute-done((bf16[2,192,768]{2,1,0:T(8,128)(2,1)}, bf16[2,192,768]{2,1,0:T(8,128)(2,1)}, u32[]{:S(2)}, u32[]{:S(2)}) %collective-permute-start.36) | collective-permute-done | bytes 589856 | tf_op jit(solution)/shard_map/ppermute | solution.py:558
  180.9 6.0 %rows_back.1 = (bf16[4,256,768]{2,1,0:T(8,128)(2,1)}, bf16[4,256,768]{2,1,0:T(8,128)(2,1)}) custom-call(s32[4]{0:T(128)} %pad_add_fusion.place, bf16[8,128,192]{2,1,0:T(8,128)(2,1)} %get-tuple-element.215.dq_ref, bf16[8,256,384]{2,1,0:T(8,128)(2,1)} %get-tuple-element.196.dkv_ref, bf16[192,576]{1,0:T(8,128)(2,1)} %get-tuple-element.132.refs_0_.slab0, ...), custom_call_target="tpu_custom_call" | custom-call | flops 1509949440 | bytes 5996560 | tf_op jit(solution)/shard_map/rows_back/pallas_call | solution.py:75
  187.2 3.5 %collective-permute-done.42 = bf16[4,256,768]{2,1,0:T(8,128)(2,1)S(1)} collective-permute-done((bf16[4,256,768]{2,1,0:T(8,128)(2,1)}, bf16[4,256,768]{2,1,0:T(8,128)(2,1)S(1)}, u32[]{:S(2)}, u32[]{:S(2)}) %collective-permute-start.42) | collective-permute-done | bytes 1572896 | tf_op jit(solution)/shard_map/ppermute | solution.py:558
  199.4 19.1 %collective-permute-done.43 = bf16[2,96,768]{2,1,0:T(8,128)(2,1)S(1)} collective-permute-done((bf16[2,96,768]{2,1,0:T(8,128)(2,1)S(1)}, bf16[2,96,768]{2,1,0:T(8,128)(2,1)S(1)}, u32[]{:S(2)}, u32[]{:S(2)}) %collective-permute-start.43) | collective-permute-done | bytes 294944 | tf_op jit(solution)/shard_map/ppermute | solution.py:558
  218.5 3.4 %collective-permute-start.53 = (bf16[2,32,768]{2,1,0:T(8,128)(2,1)S(1)}, bf16[2,32,768]{2,1,0:T(8,128)(2,1)S(1)}, u32[]{:S(2)}, u32[]{:S(2)}) collective-permute-start(bf16[2,32,768]{2,1,0:T(8,128)(2,1)S(1)} %add_add_fusion), channel_id=1, source_target_pairs={{0,4},{1,5},{2,6},{3,7},{4,0},{5,1},{6,2},{7,3},{8,12},{9,13},{10,... | collective-permute-start | bytes 294920 | tf_op jit(solution)/shard_map/ppermute | solution.py:558
  224.9 3.4 %collective-permute-start.52 = (bf16[2,104,576]{2,1,0:T(8,128)(2,1)S(1)}, bf16[2,104,576]{2,1,0:T(8,128)(2,1)S(1)}, u32[]{:S(2)}, u32[]{:S(2)}) collective-permute-start(bf16[2,104,576]{2,1,0:T(8,128)(2,1)S(1)} %add.149), channel_id=1, source_target_pairs={{0,4},{1,5},{2,6},{3,7},{4,0},{5,1},{6,2},{7,3},{8,12},{9,13},{10,... | collective-permute-start | bytes 718856 | tf_op jit(solution)/shard_map/ppermute | solution.py:558
  230.7 3.2 %stream_back.1 = bf16[256,767]{1,0:T(8,128)(2,1)} custom-call(s32[4]{0:T(128)} %pad_add_fusion.place, bf16[256,768]{1,0:T(8,128)(2,1)} %get-tuple-element.257.part0, bf16[256,768]{1,0:T(8,128)(2,1)} %copy-done.20, bf16[256,768]{1,0:T(8,128)(2,1)} %copy-done.19, bf16[256,768]{1,0:T(8,128)(2,1)} %copy-done.18, f32[256,768]{1,0:T(8,128)} %get-tuple-element.149.resid_ref, ...), custom_call_target="tpu_custom_call" | custom-call | bytes 3550736 | tf_op jit(solution)/shard_map/stream_back/pallas_call | solution.py:75
  236.3 5.5 %collective-permute-done.52 = bf16[2,104,576]{2,1,0:T(8,128)(2,1)S(1)} collective-permute-done((bf16[2,104,576]{2,1,0:T(8,128)(2,1)S(1)}, bf16[2,104,576]{2,1,0:T(8,128)(2,1)S(1)}, u32[]{:S(2)}, u32[]{:S(2)}) %collective-permute-start.52) | collective-permute-done | bytes 239648 | tf_op jit(solution)/shard_map/ppermute | solution.py:558
  249.3 5.1 %collective-permute-done.61.part2 = bf16[2,96,768]{2,1,0:T(8,128)(2,1)S(1)} collective-permute-done((bf16[2,96,768]{2,1,0:T(8,128)(2,1)S(1)}, bf16[2,96,768]{2,1,0:T(8,128)(2,1)S(1)}, u32[]{:S(2)}, u32[]{:S(2)}) %collective-permute-start.61) | collective-permute-done | bytes 294944 | tf_op jit(solution)/shard_map/ppermute | solution.py:558
  255.5 3.4 %collective-permute-start.59 = (bf16[2,120,768]{2,1,0:T(8,128)(2,1)S(1)}, bf16[2,120,768]{2,1,0:T(8,128)(2,1)S(1)}, u32[]{:S(2)}, u32[]{:S(2)}) collective-permute-start(bf16[2,120,768]{2,1,0:T(8,128)(2,1)S(1)} %fusion.9.part0), channel_id=1, source_target_pairs={{0,3},{1,2},{2,1},{3,0},{4,7},{5,6},{6,5},{7,4},{8,11},{9,10},{10,... | collective-permute-start | bytes 1105928 | tf_op jit(solution)/shard_map/ppermute | solution.py:558
  258.9 6.1 %collective-permute-done.56.part3 = bf16[2,104,576]{2,1,0:T(8,128)(2,1)} collective-permute-done((bf16[2,104,576]{2,1,0:T(8,128)(2,1)S(1)}, bf16[2,104,576]{2,1,0:T(8,128)(2,1)}, u32[]{:S(2)}, u32[]{:S(2)}) %collective-permute-start.56) | collective-permute-done | bytes 239648 | tf_op jit(solution)/shard_map/ppermute | solution.py:558
  265.0 5.2 %collective-permute-done.55.part2 = bf16[2,104,576]{2,1,0:T(8,128)(2,1)} collective-permute-done((bf16[2,104,576]{2,1,0:T(8,128)(2,1)S(1)}, bf16[2,104,576]{2,1,0:T(8,128)(2,1)}, u32[]{:S(2)}, u32[]{:S(2)}) %collective-permute-start.55) | collective-permute-done | bytes 239648 | tf_op jit(solution)/shard_map/ppermute | solution.py:558
  275.3 3.1 %heads_out.1 = (f32[192,2304]{1,0:T(8,128)}, f32[192,1]{1,0:T(8,128)}, f32[1,384]{1,0:T(1,128)}) custom-call(s32[4]{0:T(128)} %pad_add_fusion.place, bf16[2,104,576]{2,1,0:T(8,128)(2,1)} %copy-done.9, bf16[2,104,576]{2,1,0:T(8,128)(2,1)} %collective-permute-done.54.part1, bf16[2,104,576]{2,1,0:T(8,128)(2,1)} %collective-permute-done.55.part2, ...), custom_call_target="tpu_custom_call" | custom-call | bytes 3614992 | tf_op jit(solution)/shard_map/heads_out/pallas_call | solution.py:75
  282.3 3.6 %collective-permute-done.58.part2 = bf16[2,120,768]{2,1,0:T(8,128)(2,1)S(1)} collective-permute-done((bf16[2,120,768]{2,1,0:T(8,128)(2,1)S(1)}, bf16[2,120,768]{2,1,0:T(8,128)(2,1)S(1)}, u32[]{:S(2)}, u32[]{:S(2)}) %collective-permute-start.58) | collective-permute-done | bytes 368672 | tf_op jit(solution)/shard_map/ppermute | solution.py:558
  287.3 3.1 %up_out.1 = (f32[192,3072]{1,0:T(8,128)}, f32[192,768]{1,0:T(8,128)}) custom-call(s32[4]{0:T(128)} %pad_add_fusion.place, bf16[2,120,768]{2,1,0:T(8,128)(2,1)} %copy-done.16, bf16[2,120,768]{2,1,0:T(8,128)(2,1)} %copy-done.27, bf16[2,120,768]{2,1,0:T(8,128)(2,1)} %copy-done.26, bf16[2,120,768]{2,1,0:T(8,128)(2,1)} %copy-done.25), custom_call_target="tpu_custom_call" | custom-call | bytes 4423696 | tf_op jit(solution)/shard_map/up_out/pallas_call | solution.py:75
  (281 shorter events, 102.4 us)
Async XLA Ops:
  0.7 15.4 %collective-permute-start.6 = (bf16[256,767]{1,0:T(8,128)(2,1)}, bf16[256,767]{1,0:T(8,128)(2,1)S(1)}, u32[]{:S(2)}, u32[]{:S(2)}) collective-permute-start(bf16[256,767]{1,0:T(8,128)(2,1)} %param.12), channel_id=1, source_target_pairs={{0,0},{1,1},{2,2},{3,3},{4,8},{5,9},{6,10},{7,11},{8,4},{9,5},{10,... | collective-permute-start | bytes 1178120 | tf_op jit(solution)/shard_map/ppermute | solution.py:558
  16.0 25.5 %collective-permute-start = (bf16[192,576]{1,0:T(8,128)(2,1)}, bf16[192,576]{1,0:T(8,128)(2,1)S(1)}, u32[]{:S(2)}, u32[]{:S(2)}) collective-permute-start(bf16[192,576]{1,0:T(8,128)(2,1)} %get-tuple-element.132.refs_0_.slab0), channel_id=1, source_target_pairs={{0,8},{1,9},{2,10},{3,11},{4,12},{5,13},{6,14},{7,15},{8,0},{9,1},... | collective-permute-start | bytes 663560 | tf_op jit(solution)/shard_map/ppermute | solution.py:558
  19.0 13.3 %collective-permute-start.9 = (bf16[1,256,768]{2,1,0:T(8,128)(2,1)}, bf16[1,256,768]{2,1,0:T(8,128)(2,1)S(1)}, u32[]{:S(2)}, u32[]{:S(2)}) collective-permute-start(bf16[1,256,768]{2,1,0:T(8,128)(2,1)} %get-tuple-element.136.refs_6_), channel_id=1, source_target_pairs={{0,3},{1,2},{2,1},{3,0},{4,7},{5,6},{6,5},{7,4},{8,11},{9,10},{10,... | collective-permute-start | bytes 1179656 | tf_op jit(solution)/shard_map/ppermute | solution.py:558
  22.0 18.6 %collective-permute-start.8 = (bf16[1,256,768]{2,1,0:T(8,128)(2,1)}, bf16[1,256,768]{2,1,0:T(8,128)(2,1)S(1)}, u32[]{:S(2)}, u32[]{:S(2)}) collective-permute-start(bf16[1,256,768]{2,1,0:T(8,128)(2,1)} %get-tuple-element.136.refs_6_), channel_id=1, source_target_pairs={{0,2},{1,3},{2,0},{3,1},{4,6},{5,7},{6,4},{7,5},{8,10},{9,11},{10,... | collective-permute-start | bytes 1179656 | tf_op jit(solution)/shard_map/ppermute | solution.py:558
  22.5 18.1 %collective-permute-start.7 = (bf16[1,256,768]{2,1,0:T(8,128)(2,1)}, bf16[1,256,768]{2,1,0:T(8,128)(2,1)S(1)}, u32[]{:S(2)}, u32[]{:S(2)}) collective-permute-start(bf16[1,256,768]{2,1,0:T(8,128)(2,1)} %get-tuple-element.136.refs_6_), channel_id=1, source_target_pairs={{0,1},{1,0},{2,3},{3,2},{4,5},{5,4},{6,7},{7,6},{8,9},{9,8},{10,11... | collective-permute-start | bytes 1179656 | tf_op jit(solution)/shard_map/ppermute | solution.py:558
  44.4 19.7 %collective-permute-start.15 = (bf16[192,768]{1,0:T(8,128)(2,1)}, bf16[192,768]{1,0:T(8,128)(2,1)S(1)}, u32[]{:S(2)}, u32[]{:S(2)}) collective-permute-start(bf16[192,768]{1,0:T(8,128)(2,1)} %get-tuple-element.145), channel_id=1, source_target_pairs={{0,8},{1,9},{2,10},{3,11},{4,12},{5,13},{6,14},{7,15},{8,0},{9,1},... | collective-permute-start | bytes 884744 | tf_op jit(solution)/shard_map/ppermute | solution.py:558
  44.6 19.4 %collective-permute-start.16 = (bf16[192,768]{1,0:T(8,128)(2,1)}, bf16[192,768]{1,0:T(8,128)(2,1)S(1)}, u32[]{:S(2)}, u32[]{:S(2)}) collective-permute-start(bf16[192,768]{1,0:T(8,128)(2,1)} %get-tuple-element.146), channel_id=1, source_target_pairs={{0,16},{1,17},{2,18},{3,19},{4,20},{5,21},{6,22},{7,23},{8,24},{9,... | collective-permute-start | bytes 884744 | tf_op jit(solution)/shard_map/ppermute | solution.py:558
  46.2 17.9 %collective-permute-start.17 = (bf16[192,768]{1,0:T(8,128)(2,1)}, bf16[192,768]{1,0:T(8,128)(2,1)}, u32[]{:S(2)}, u32[]{:S(2)}) collective-permute-start(bf16[192,768]{1,0:T(8,128)(2,1)} %get-tuple-element.147), channel_id=1, source_target_pairs={{0,24},{1,25},{2,26},{3,27},{4,28},{5,29},{6,30},{7,31},{8,16},{9,... | collective-permute-start | bytes 884744 | tf_op jit(solution)/shard_map/ppermute | solution.py:558
  47.5 25.3 %collective-permute-start.23 = (bf16[256,767]{1,0:T(8,128)(2,1)S(1)}, bf16[256,767]{1,0:T(8,128)(2,1)S(1)}, u32[]{:S(2)}, u32[]{:S(2)}) collective-permute-start(bf16[256,767]{1,0:T(8,128)(2,1)S(1)} %copy-done.36), channel_id=1, source_target_pairs={{0,0},{1,1},{2,2},{3,3},{4,8},{5,9},{6,10},{7,11},{8,4},{9,5},{10,... | collective-permute-start | bytes 1178120 | tf_op jit(solution)/shard_map/ppermute | solution.py:558
  64.8 14.2 %all-to-all-start = ((bf16[8,192,128]{2,1,0:T(8,128)(2,1)}), bf16[8,192,128]{2,1,0:T(8,128)(2,1)S(1)}, u32[]{:S(2)}, u32[]{:S(2)}) async-start(bf16[8,192,128]{2,1,0:T(8,128)(2,1)} %get-tuple-element.148.out_ref), calls=%async_computation | async-start | bytes 786432 | tf_op jit(solution)/shard_map/all_to_all | solution.py:581
  136.0 34.8 %collective-permute-start.34 = (bf16[2,192,768]{2,1,0:T(8,128)(2,1)}, bf16[2,192,768]{2,1,0:T(8,128)(2,1)}, u32[]{:S(2)}, u32[]{:S(2)}) collective-permute-start(bf16[2,192,768]{2,1,0:T(8,128)(2,1)} %get-tuple-element.202), channel_id=1, source_target_pairs={{0,1},{1,0},{2,3},{3,2},{4,5},{5,4},{6,7},{7,6},{8,9},{9,8},{10,11... | collective-permute-start | bytes 1769480 | tf_op jit(solution)/shard_map/ppermute | solution.py:558
  137.9 32.9 %collective-permute-start.35 = (bf16[2,192,768]{2,1,0:T(8,128)(2,1)}, bf16[2,192,768]{2,1,0:T(8,128)(2,1)}, u32[]{:S(2)}, u32[]{:S(2)}) collective-permute-start(bf16[2,192,768]{2,1,0:T(8,128)(2,1)} %get-tuple-element.203), channel_id=1, source_target_pairs={{0,2},{1,3},{2,0},{3,1},{4,6},{5,7},{6,4},{7,5},{8,10},{9,11},{10,... | collective-permute-start | bytes 1769480 | tf_op jit(solution)/shard_map/ppermute | solution.py:558
  139.4 34.5 %collective-permute-start.36 = (bf16[2,192,768]{2,1,0:T(8,128)(2,1)}, bf16[2,192,768]{2,1,0:T(8,128)(2,1)}, u32[]{:S(2)}, u32[]{:S(2)}) collective-permute-start(bf16[2,192,768]{2,1,0:T(8,128)(2,1)} %get-tuple-element.204), channel_id=1, source_target_pairs={{0,3},{1,2},{2,1},{3,0},{4,7},{5,6},{6,5},{7,4},{8,11},{9,10},{10,... | collective-permute-start | bytes 1769480 | tf_op jit(solution)/shard_map/ppermute | solution.py:558
  144.8 19.1 %collective-permute-start.32 = (bf16[8,32,768]{2,1,0:T(8,128)(2,1)S(1)}, bf16[8,32,768]{2,1,0:T(8,128)(2,1)S(1)}, u32[]{:S(2)}, u32[]{:S(2)}) collective-permute-start(bf16[8,32,768]{2,1,0:T(8,128)(2,1)S(1)} %slice_bitcast_fusion.3), channel_id=1, source_target_pairs={{0,16},{1,17},{2,18},{3,19},{4,20},{5,21},{6,22},{7,23},{8,24},{9,... | collective-permute-start | bytes 1179656 | tf_op jit(solution)/shard_map/ppermute | solution.py:558
  146.3 27.5 %collective-permute-start.33 = (bf16[256,767]{1,0:T(8,128)(2,1)S(1)}, bf16[256,767]{1,0:T(8,128)(2,1)S(1)}, u32[]{:S(2)}, u32[]{:S(2)}) collective-permute-start(bf16[256,767]{1,0:T(8,128)(2,1)S(1)} %fusion.1), channel_id=1, source_target_pairs={{0,0},{1,1},{2,2},{3,3},{4,8},{5,9},{6,10},{7,11},{8,4},{9,5},{10,... | collective-permute-start | bytes 1178120 | tf_op jit(solution)/shard_map/ppermute | solution.py:558
  193.0 35.4 %collective-permute-start.47 = (bf16[256,768]{1,0:T(8,128)(2,1)S(1)}, bf16[256,768]{1,0:T(8,128)(2,1)S(1)}, u32[]{:S(2)}, u32[]{:S(2)}) collective-permute-start(bf16[256,768]{1,0:T(8,128)(2,1)S(1)} %get-tuple-element.254), channel_id=1, source_target_pairs={{0,3},{1,2},{2,1},{3,0},{4,7},{5,6},{6,5},{7,4},{8,11},{9,10},{10,... | collective-permute-start | bytes 1179656 | tf_op jit(solution)/shard_map/ppermute | solution.py:558
  194.3 34.1 %collective-permute-start.46 = (bf16[256,768]{1,0:T(8,128)(2,1)S(1)}, bf16[256,768]{1,0:T(8,128)(2,1)S(1)}, u32[]{:S(2)}, u32[]{:S(2)}) collective-permute-start(bf16[256,768]{1,0:T(8,128)(2,1)S(1)} %get-tuple-element.255), channel_id=1, source_target_pairs={{0,2},{1,3},{2,0},{3,1},{4,6},{5,7},{6,4},{7,5},{8,10},{9,11},{10,... | collective-permute-start | bytes 1179656 | tf_op jit(solution)/shard_map/ppermute | solution.py:558
  195.0 33.4 %collective-permute-start.45 = (bf16[256,768]{1,0:T(8,128)(2,1)S(1)}, bf16[256,768]{1,0:T(8,128)(2,1)S(1)}, u32[]{:S(2)}, u32[]{:S(2)}) collective-permute-start(bf16[256,768]{1,0:T(8,128)(2,1)S(1)} %get-tuple-element.256), channel_id=1, source_target_pairs={{0,1},{1,0},{2,3},{3,2},{4,5},{5,4},{6,7},{7,6},{8,9},{9,8},{10,11... | collective-permute-start | bytes 1179656 | tf_op jit(solution)/shard_map/ppermute | solution.py:558
  196.5 22.1 %collective-permute-start.43 = (bf16[2,96,768]{2,1,0:T(8,128)(2,1)S(1)}, bf16[2,96,768]{2,1,0:T(8,128)(2,1)S(1)}, u32[]{:S(2)}, u32[]{:S(2)}) collective-permute-start(bf16[2,96,768]{2,1,0:T(8,128)(2,1)S(1)} %copy-done.29), channel_id=1, source_target_pairs={{0,4},{1,5},{2,6},{3,7},{4,0},{5,1},{6,2},{7,3},{8,12},{9,13},{10,... | collective-permute-start | bytes 884744 | tf_op jit(solution)/shard_map/ppermute | solution.py:558
  197.4 27.5 %collective-permute-start.44 = (bf16[2,96,768]{2,1,0:T(8,128)(2,1)S(1)}, bf16[2,96,768]{2,1,0:T(8,128)(2,1)S(1)}, u32[]{:S(2)}, u32[]{:S(2)}) collective-permute-start(bf16[2,96,768]{2,1,0:T(8,128)(2,1)S(1)} %copy-done.28), channel_id=1, source_target_pairs={{0,4},{1,5},{2,6},{3,7},{4,0},{5,1},{6,2},{7,3},{8,12},{9,13},{10,... | collective-permute-start | bytes 884744 | tf_op jit(solution)/shard_map/ppermute | solution.py:558
  218.5 17.5 %collective-permute-start.53 = (bf16[2,32,768]{2,1,0:T(8,128)(2,1)S(1)}, bf16[2,32,768]{2,1,0:T(8,128)(2,1)S(1)}, u32[]{:S(2)}, u32[]{:S(2)}) collective-permute-start(bf16[2,32,768]{2,1,0:T(8,128)(2,1)S(1)} %add_add_fusion), channel_id=1, source_target_pairs={{0,4},{1,5},{2,6},{3,7},{4,0},{5,1},{6,2},{7,3},{8,12},{9,13},{10,... | collective-permute-start | bytes 294920 | tf_op jit(solution)/shard_map/ppermute | solution.py:558
  224.9 16.8 %collective-permute-start.52 = (bf16[2,104,576]{2,1,0:T(8,128)(2,1)S(1)}, bf16[2,104,576]{2,1,0:T(8,128)(2,1)S(1)}, u32[]{:S(2)}, u32[]{:S(2)}) collective-permute-start(bf16[2,104,576]{2,1,0:T(8,128)(2,1)S(1)} %add.149), channel_id=1, source_target_pairs={{0,4},{1,5},{2,6},{3,7},{4,0},{5,1},{6,2},{7,3},{8,12},{9,13},{10,... | collective-permute-start | bytes 718856 | tf_op jit(solution)/shard_map/ppermute | solution.py:558
  228.5 13.3 %collective-permute-start.51 = (bf16[2,24,768]{2,1,0:T(8,128)(2,1)S(1)}, bf16[2,24,768]{2,1,0:T(8,128)(2,1)}, u32[]{:S(2)}, u32[]{:S(2)}) collective-permute-start(bf16[2,24,768]{2,1,0:T(8,128)(2,1)S(1)} %get-tuple-element.270), channel_id=1, source_target_pairs={{0,24},{1,25},{2,26},{3,27},{4,28},{5,29},{6,30},{7,31},{8,16},{9,... | collective-permute-start | bytes 221192 | tf_op jit(solution)/shard_map/ppermute | solution.py:558
  228.6 14.2 %collective-permute-start.49 = (bf16[2,24,768]{2,1,0:T(8,128)(2,1)S(1)}, bf16[2,24,768]{2,1,0:T(8,128)(2,1)}, u32[]{:S(2)}, u32[]{:S(2)}) collective-permute-start(bf16[2,24,768]{2,1,0:T(8,128)(2,1)S(1)} %get-tuple-element.272), channel_id=1, source_target_pairs={{0,8},{1,9},{2,10},{3,11},{4,12},{5,13},{6,14},{7,15},{8,0},{9,1},... | collective-permute-start | bytes 221192 | tf_op jit(solution)/shard_map/ppermute | solution.py:558
  241.8 13.7 %collective-permute-start.60 = (bf16[2,96,768]{2,1,0:T(8,128)(2,1)S(1)}, bf16[2,96,768]{2,1,0:T(8,128)(2,1)S(1)}, u32[]{:S(2)}, u32[]{:S(2)}) collective-permute-start(bf16[2,96,768]{2,1,0:T(8,128)(2,1)S(1)} %pad_maximum_fusion.part0), channel_id=1, source_target_pairs={{0,1},{1,0},{2,3},{3,2},{4,5},{5,4},{6,7},{7,6},{8,9},{9,8},{10,11... | collective-permute-start | bytes 884744 | tf_op jit(solution)/shard_map/ppermute | solution.py:558
  242.9 22.1 %collective-permute-start.56 = (bf16[2,104,576]{2,1,0:T(8,128)(2,1)S(1)}, bf16[2,104,576]{2,1,0:T(8,128)(2,1)}, u32[]{:S(2)}, u32[]{:S(2)}) collective-permute-start(bf16[2,104,576]{2,1,0:T(8,128)(2,1)S(1)} %pad_maximum_fusion.1.part0), channel_id=1, source_target_pairs={{0,3},{1,2},{2,1},{3,0},{4,7},{5,6},{6,5},{7,4},{8,11},{9,10},{10,... | collective-permute-start | bytes 718856 | tf_op jit(solution)/shard_map/ppermute | solution.py:558
  245.4 24.8 %collective-permute-start.55 = (bf16[2,104,576]{2,1,0:T(8,128)(2,1)S(1)}, bf16[2,104,576]{2,1,0:T(8,128)(2,1)}, u32[]{:S(2)}, u32[]{:S(2)}) collective-permute-start(bf16[2,104,576]{2,1,0:T(8,128)(2,1)S(1)} %pad_maximum_fusion.1.part0), channel_id=1, source_target_pairs={{0,2},{1,3},{2,0},{3,1},{4,6},{5,7},{6,4},{7,5},{8,10},{9,11},{10,... | collective-permute-start | bytes 718856 | tf_op jit(solution)/shard_map/ppermute | solution.py:558
  248.6 32.7 %collective-permute-start.48 = (bf16[256,767]{1,0:T(8,128)(2,1)S(1)}, bf16[256,767]{1,0:T(8,128)(2,1)S(1)}, u32[]{:S(2)}, u32[]{:S(2)}) collective-permute-start(bf16[256,767]{1,0:T(8,128)(2,1)S(1)} %copy-done.17), channel_id=1, source_target_pairs={{0,0},{1,1},{2,2},{3,3},{4,8},{5,9},{6,10},{7,11},{8,4},{9,5},{10,... | collective-permute-start | bytes 1178120 | tf_op jit(solution)/shard_map/ppermute | solution.py:558
  254.4 20.9 %collective-permute-start.54 = (bf16[2,104,576]{2,1,0:T(8,128)(2,1)S(1)}, bf16[2,104,576]{2,1,0:T(8,128)(2,1)}, u32[]{:S(2)}, u32[]{:S(2)}) collective-permute-start(bf16[2,104,576]{2,1,0:T(8,128)(2,1)S(1)} %pad_maximum_fusion.1.part0), channel_id=1, source_target_pairs={{0,1},{1,0},{2,3},{3,2},{4,5},{5,4},{6,7},{7,6},{8,9},{9,8},{10,11... | collective-permute-start | bytes 718856 | tf_op jit(solution)/shard_map/ppermute | solution.py:558
  255.5 26.8 %collective-permute-start.59 = (bf16[2,120,768]{2,1,0:T(8,128)(2,1)S(1)}, bf16[2,120,768]{2,1,0:T(8,128)(2,1)S(1)}, u32[]{:S(2)}, u32[]{:S(2)}) collective-permute-start(bf16[2,120,768]{2,1,0:T(8,128)(2,1)S(1)} %fusion.9.part0), channel_id=1, source_target_pairs={{0,3},{1,2},{2,1},{3,0},{4,7},{5,6},{6,5},{7,4},{8,11},{9,10},{10,... | collective-permute-start | bytes 1105928 | tf_op jit(solution)/shard_map/ppermute | solution.py:558
  265.0 20.8 %collective-permute-start.58 = (bf16[2,120,768]{2,1,0:T(8,128)(2,1)S(1)}, bf16[2,120,768]{2,1,0:T(8,128)(2,1)S(1)}, u32[]{:S(2)}, u32[]{:S(2)}) collective-permute-start(bf16[2,120,768]{2,1,0:T(8,128)(2,1)S(1)} %fusion.9.part0), channel_id=1, source_target_pairs={{0,2},{1,3},{2,0},{3,1},{4,6},{5,7},{6,4},{7,5},{8,10},{9,11},{10,... | collective-permute-start | bytes 1105928 | tf_op jit(solution)/shard_map/ppermute | solution.py:558
  270.2 16.1 %collective-permute-start.57 = (bf16[2,120,768]{2,1,0:T(8,128)(2,1)S(1)}, bf16[2,120,768]{2,1,0:T(8,128)(2,1)S(1)}, u32[]{:S(2)}, u32[]{:S(2)}) collective-permute-start(bf16[2,120,768]{2,1,0:T(8,128)(2,1)S(1)} %fusion.9.part0), channel_id=1, source_target_pairs={{0,1},{1,0},{2,3},{3,2},{4,5},{5,4},{6,7},{7,6},{8,9},{9,8},{10,11... | collective-permute-start | bytes 1105928 | tf_op jit(solution)/shard_map/ppermute | solution.py:558
  (87 other events, 837.8 us)

commit v2 on v1

--- a/solution.py
+++ b/solution.py
@@ -142,7 +142,7 @@
 def project_kernel(place, *refs):
     slabs, (gain_ref, bias_ref) = refs[:4], refs[4:6]
     pieces = refs[6:-7]
-    normed_ref, k_ref, v_ref, q_ref, qt_ref, wq, wkv = refs[-7:]
+    k_ref, v_ref, q_ref, qt_ref, wq, wkv, normed_ref = refs[-7:]
     load_heads(place, slabs, wq, wkv)
     gain = gain_ref[...]
     slot = 0
@@ -165,13 +165,19 @@
     project(place, normed_ref, slots, bias_ref, k_ref, v_ref, q_ref, qt_ref, wq, wkv)
 
 
-def collect_kernel(place, normed_ref, normed_t_ref, query_t_ref):
+def collect_kernel(place, gain_ref, *refs):
+    pieces, (normed_t_ref, query_t_ref, normed_ref) = refs[:-3], refs[-3:]
     blocks, rows, _ = normed_ref.shape
     query_rows = query_t_ref.shape[1] // blocks
     own = pl.ds(pl.multiple_of(place[2] * query_rows, query_rows), query_rows)
-    for slot in range(blocks):
-        normed_t_ref[:, slot * rows : (slot + 1) * rows] = normed_ref[slot].T
-        query_t_ref[:, slot * query_rows : (slot + 1) * query_rows] = normed_ref[slot, own, :].T
+    gain, slot = gain_ref[...], 0
+    for ref in pieces:
+        for at in range(ref.shape[0]):
+            normed_ref[slot] = (ref[at].astype(f32) * gain).astype(bf16)
+            normed_t_ref[:, slot * rows : (slot + 1) * rows] = normed_ref[slot].T
+            mine = normed_ref[slot, own, :].T
+            query_t_ref[:, slot * query_rows : (slot + 1) * query_rows] = mine
+            slot += 1
 
 
 def by_head(value):
@@ -431,10 +437,8 @@
         lax.fori_loop(0, PIECES, one, 0)
 
 
-def sum_kernel(place, part0, part1, part2, part3, down_ref, up_ref):
-    parts, wide = (part0, part1, part2, part3), down_ref.shape[1]
-    down_ref[...] = sum(part[:, :wide].astype(f32) for part in parts).astype(bf16)
-    up_ref[...] = sum(part[:, wide:].astype(f32) for part in parts).astype(bf16)
+def sum_kernel(place, part0, part1, part2, part3, out_ref):
+    out_ref[...] = sum(part[...].astype(f32) for part in (part0, part1, part2, part3)).astype(bf16)
 
 
 def heads_back_kernel(place, normed_t_ref, query_t_ref, dq_ref, dkv_ref, sum_ref, near_ref, far_ref, aq, akv):
@@ -491,8 +495,15 @@
         loop(0, half, one, 0)
 
 
-def stream_back_kernel(place, part0, part1, part2, part3, resid_ref, grad_middle_ref, vec_ref, out_ref):
-    grad = sum(part[...].astype(f32) for part in (part0, part1, part2, part3))
+def by_near(own, got, pair, first):
+    return ((0, own), (first, got), (3 - first, pair.at[0]), (3, pair.at[1]))
+
+
+UP_FIRST, DOWN_FIRST, HEADS_FIRST = 1, 2, 2
+
+
+def stream_back_kernel(place, near_ref, far_ref, last_ref, resid_ref, grad_middle_ref, vec_ref, out_ref):
+    grad = near_ref[0].astype(f32) + far_ref[0].astype(f32) + last_ref[...].astype(f32)
     resid = resid_ref[...]
     inverse = inverse_rms(resid)
     unit = resid * inverse
@@ -500,17 +511,17 @@
     out_ref[...] = (total - total[:, D - 1 :]).astype(bf16)[:, : D - 1]
 
 
-def down_out_kernel(place, part0, part1, part2, part3, out_ref):
-    wide = part0.shape[1]
-    for near, part in enumerate((part0, part1, part2, part3)):
+def down_out_kernel(place, own, got, pair, out_ref):
+    wide = own.shape[1]
+    for near, part in by_near(own, got, pair, DOWN_FIRST):
         for side in range(2):
             at = pl.multiple_of(((side << 2 | near) ^ place[3]) * wide, wide)
             out_ref[pl.ds(at, wide), :] = part[side].astype(f32)
 
 
-def up_out_kernel(place, part0, part1, part2, part3, up_ref, out_ref):
+def up_out_kernel(place, own, got, pair, up_ref, out_ref):
     rows = out_ref.shape[0] // PIECES
-    for near, part in enumerate((part0, part1, part2, part3)):
+    for near, part in by_near(own, got, pair, UP_FIRST):
         for side in range(2):
             at = pl.multiple_of(((side << 2 | near) ^ place[3]) * rows, rows)
             for slab in range(4):
@@ -520,10 +531,10 @@
             out_ref[pl.ds(at, rows), :] = part[side, 4 * rows :].astype(f32)
 
 
-def heads_out_kernel(place, part0, part1, part2, part3, weight_ref, out_ref, gain_ref, bias_ref, pieces):
-    piece = part0.shape[1] - EXTRA
+def heads_out_kernel(place, own, got, pair, weight_ref, out_ref, gain_ref, bias_ref, pieces):
+    piece = own.shape[1] - EXTRA
     mine, low = place[1], place[3]
-    for near, part in enumerate((part0, part1, part2, part3)):
+    for near, part in by_near(own, got, pair, HEADS_FIRST):
         pieces[near] = part[...]
     for part in range(2):
         for group in range(HEAD_GROUPS):
@@ -590,14 +601,14 @@
     def to_square(values):
         return tuple(to_ctx(value, near + 1) for near, value in enumerate(values))
 
-    def gather_square(value):
-        pair = jnp.stack([value, to_ctx(value, 4)])
-        return (pair, *to_square((pair,) * 3))
-
     def over_rest(value):
         for step in range(3, ctx_steps):
             value = value + to_ctx(value, 1 << step)
         return value
+
+    def gather_square(value, first):
+        got = to_ctx(value, first)
+        return value, got, to_ctx(jnp.stack([value, got]), 3 - first)
 
     together = lax.optimization_barrier
 
@@ -689,13 +700,13 @@
         )
         work = 5 * tokens * D * GROUP_COLS
         if 4 * tokens * D * 2 < VMEM_LIMIT:
-            normed, keys, values, queries, queries_t = call(
+            keys, values, queries, queries_t = call(
                 project_kernel,
                 "project",
-                (shape((ctx_count, rows, D), bf16), *projected),
+                projected,
                 (place, *w_heads, gain, bias_heads, *pieces),
                 flops=work,
-                scratch=head_weights,
+                scratch=head_weights + [pltpu.VMEM((ctx_count, rows, D), bf16)],
             )
         else:
             normed = (jnp.concatenate(pieces).astype(f32) * gain).astype(bf16)
@@ -752,7 +763,7 @@
             scratch=[pltpu.VMEM((rows, D), f32)],
         )
         piece = shard // PIECES
-        normed_mlp, normed = together((normed_mlp, normed))
+        normed_mlp, *late_pieces = together((normed_mlp, *pieces))
         if 4 * tokens * D * 2 < VMEM_LIMIT:
             normed_t, query_t = call(
                 collect_kernel,
@@ -761,9 +772,11 @@
                     shape((D, tokens), bf16),
                     shape((D, ctx_count * query_rows), bf16),
                 ),
-                (place, normed),
+                (place, gain, *late_pieces),
+                scratch=[pltpu.VMEM((ctx_count, rows, D), bf16)],
             )
         else:
+            normed = (jnp.concatenate(late_pieces).astype(f32) * gain).astype(bf16)
             normed_query = lax.dynamic_index_in_dim(
                 normed.reshape(ctx_count, splits, query_rows, D), place[2], 1, keepdims=False
             )
@@ -828,12 +841,7 @@
             scratch=[pltpu.VMEM((D + 8, D), f32)],
         )
         out_sum = out_near + to_core(out_give)
-        branch_got = to_core(branch_give)
-        branch_far_got = to_chip_row((branch_far + branch_got[1]).astype(bf16))
-        branch_mlp = branch_own + branch_got[0] + branch_far_got + vec[3:4]
-        stream_out = (middle + centered(branch_mlp)).astype(bf16)[:, : D - 1]
-        grads, out_sum, stream_out = together((grads, out_sum, stream_out))
-        stream_out = swap_sequences(stream_out)
+        grads, out_sum = together((grads, out_sum))
         out_got = to_chip_row(out_sum[1])
         both_got = to_square(both_sums[1:])
         dq, dkv, head_sums = call(
@@ -877,27 +885,25 @@
                 head_shapes,
                 (place, dot(query_t, flat_q), dot(normed_t, flat_kv), head_sums),
             )
-        head_near, head_give, stream_out, out_got, *both_got = together(
-            (head_near, head_give, stream_out, out_got, *both_got)
-        )
-        down_sum, up_sum = call(
+        head_near, head_give, out_got, *both_got = together(
+            (head_near, head_give, out_got, *both_got)
+        )
+        wide = hidden // PIECES
+        (both_sum,) = call(
             sum_kernel,
             "sum",
-            (
-                shape((2, hidden // PIECES, D), bf16),
-                shape((2, fsdp_count * piece, hidden), bf16),
-            ),
+            (shape((2, wide + fsdp_count * piece, D), bf16),),
             (place, both_sums[0], *both_got),
         )
         out_sums = [
             out_sum[0, 2 * near : 2 * near + 2] + out_got[2 * near : 2 * near + 2] for near in range(4)
         ]
         head_sum = head_near + to_core(head_give)
-        dq, head_near, head_give, down_sum, up_sum, *out_sums = together(
-            (dq, head_sum[0], head_sum[1], down_sum, up_sum, *out_sums)
+        dq, head_near, head_give, both_sum, *out_sums = together(
+            (dq, head_sum[0], head_sum[1], both_sum, *out_sums)
         )
         head_got = to_chip_row(head_give)
-        down_got, up_got = to_ctx(down_sum, 4), to_ctx(up_sum, 4)
+        both_got = to_ctx(both_sum, 4)
         out_got = to_square(out_sums[1:])
 
         row_shapes = (shape((half, rows, D), bf16), shape((half, rows, D), bf16))
@@ -921,8 +927,8 @@
             grad_rows = (grad_rows + jnp.where(chosen, grad_query, 0.0)).astype(bf16)
             grad_rows = grad_rows.reshape(ctx_count, rows, D)
             keep_rows, give_rows = grad_rows[:half], grad_rows[half:]
-        keep_rows, give_rows, head_got, *out_got = together(
-            (keep_rows, give_rows, head_got, *out_got)
+        keep_rows, give_rows, head_got, both_got, *out_got = together(
+            (keep_rows, give_rows, head_got, both_got, *out_got)
         )
 
         def both_sides(own, other):
@@ -931,34 +937,40 @@
         rows_got = to_core(give_rows)
         head_sum = head_near + head_got
         out_sum = sum(out_got, start=out_sums[0])
-        rows_got, head_sum, out_sum = together((rows_got, head_sum, out_sum))
+        rows_got, head_sum, out_sum, both_got = together((rows_got, head_sum, out_sum, both_got))
         head_got, out_got = to_ctx(head_sum, 4), to_ctx(out_sum, 4)
+        up_sum = both_sides(both_sum[:, wide:], both_got[:, wide:])
+        ups = [up_sum[:, distance * piece : (distance + 1) * piece] for distance in range(fsdp_count)]
+        ups = [ups[0]] + [to_fsdp(ups[distance], distance) for distance in (1, 2, 3)]
+        keep_rows, both_got, branch_give, *ups = together((keep_rows, both_got, branch_give, *ups))
         if steps == 2:
-            parts = [keep_rows[slot] + rows_got[slot] for slot in range(4)]
+            near_rows, far_rows = (keep_rows[at::2] + rows_got[at::2] for at in range(2))
         else:
             both = keep_rows + rows_got
             for bit in reversed(range(2, steps)):
                 both = both[: 1 << bit] + to_ctx(both[1 << bit :], 1 << bit)
-            parts = [both[slot] for slot in range(4)]
-        rows_got = to_square(parts[1:])
-        up_got, down_got, *rows_got = together((up_got, down_got, *rows_got))
-        up_sum = both_sides(up_sum, up_got)
-        ups = [up_sum[:, distance * piece : (distance + 1) * piece] for distance in range(fsdp_count)]
-        ups = [ups[0]] + [to_fsdp(ups[distance], distance) for distance in (1, 2, 3)]
-        downs = both_sides(down_sum, down_got)
-        downs = (downs, *to_square((downs,) * 3))
-        *ups, head_got, out_got = together((*ups, head_got, out_got))
+            near_rows, far_rows = both[0::2], both[1::2]
+        far_got = to_ctx(far_rows, 1)
+        last_got = to_ctx(near_rows[1] + far_got[1], 2)
+        downs = both_sides(both_sum[:, :wide], both_got[:, :wide])
+        downs = gather_square(downs, DOWN_FIRST)
+        branch_got = to_core(branch_give)
+        branch_far_got = to_chip_row((branch_far + branch_got[1]).astype(bf16))
+        head_got, out_got = together((head_got, out_got))
+        branch_mlp = branch_own + branch_got[0] + branch_far_got + vec[3:4]
+        stream_out = (middle + centered(branch_mlp)).astype(bf16)[:, : D - 1]
+        stream_out = swap_sequences(stream_out)
         outs = both_sides(out_sum, out_got)
         sums = outs[0, piece:].astype(f32)
         ups = jnp.concatenate([*ups, outs[:, :piece]], axis=1)
-        ups = (ups, *to_square((ups,) * 3))
+        ups = gather_square(ups, UP_FIRST)
         heads = both_sides(head_sum, head_got)
-        heads = (heads, *to_square((heads,) * 3))
+        heads = gather_square(heads, HEADS_FIRST)
         (grad_stream,) = call(
             stream_back_kernel,
             "stream_back",
             (shape((rows, D - 1), bf16),),
-            (place, parts[0], *rows_got, resid, grad_middle, vec),
+            (place, near_rows, far_got, last_got, resid, grad_middle, vec),
         )
         grad_stream = swap_sequences(grad_stream)
         (grad_w_down,) = call(down_out_kernel, "down_out", (shape((hidden, D), f32),), (place, *downs))

time: 295 us -> 282 us (0.956)
  starting transfers between devices: 73.1 us -> 63.4 us
  waiting for transfers between devices: 91.4 us -> 85.1 us
  other arithmetic: 12.1 us -> 15.5 us
    ppermute x63 -> x58, waiting for transfers between devices: 87.3 us -> 77.9 us  [send(): return lax.ppermute(value, AXES, pairs)]
    ppermute x63 -> x58, starting transfers between devices: 62.7 us -> 53.4 us  [send(): return lax.ppermute(value, AXES, pairs)]
    all_to_all x2, waiting for transfers between devices: 4.12 us -> 7.21 us  [group_all_to_all(): lax.all_to_all(value, AXES, 0, 0, axis_index_groups=groups, tiled=True)]
    unnamed x114 -> x122, local copies, waits for them, and re-layouts: 10.3 us -> 9.59 us
  transfers between devices with their start and end apart: 65 -> 60, of which waited for: 23 -> 23; matrix products, arithmetic and copies ran while one was open for 5% -> 7% of each run, Pallas kernels for 30% -> 30%
where the time goes in v2:
time: 282 us; the launch traced here: 279 us
  Pallas kernels  100 us (35%)
  waiting for transfers between devices  85.1 us (30%)
  starting transfers between devices  63.4 us (22%)
  other arithmetic  15.5 us (5%)
  local copies, waits for them, and re-layouts  13.2 us (5%)
    pallas_call x18, Pallas kernels, call(): pl.pallas_call(body, out_shape=tuple(outs), scratch_shapes=list(scratch),...  100 us
    ppermute x58, waiting for transfers between devices, send(): return lax.ppermute(value, AXES, pairs)  77.9 us
    ppermute x58, starting transfers between devices, send(): return lax.ppermute(value, AXES, pairs)  53.4 us
    all_to_all x2, starting transfers between devices, group_all_to_all(): lax.all_to_all(value, AXES, 0, 0, axis_index_groups=groups, tiled=True)  9.95 us
    unnamed x122, local copies, waits for them, and re-layouts  9.59 us
    all_to_all x2, waiting for transfers between devices, group_all_to_all(): lax.all_to_all(value, AXES, 0, 0, axis_index_groups=groups, tiled=True)  7.21 us
  transfers between devices with their start and end apart: 60, of which 23 were waited for; matrix products, arithmetic and copies ran while one was open for 7% of the time, Pallas kernels for 30%

profile of v2, /device:TPU:0, one launch (start us, length us, event | category | flops | bytes accessed | tf_op | source)
XLA Modules:
  0.0 278.8 jit_solution(2707044428791945118)
XLA Ops:
  6.0 3.0 %collective-permute-start.1 = (bf16[192,576]{1,0:T(8,128)(2,1)}, bf16[192,576]{1,0:T(8,128)(2,1)S(1)}, u32[]{:S(2)}, u32[]{:S(2)}) collective-permute-start(bf16[192,576]{1,0:T(8,128)(2,1)} %get-tuple-element.133.refs_0_.slab0), channel_id=1, source_target_pairs={{0,16},{1,17},{2,18},{3,19},{4,20},{5,21},{6,22},{7,23},{8,24},{9,... | collective-permute-start | bytes 663560 | tf_op jit(solution)/shard_map/ppermute | solution.py:569
  9.2 2.9 %collective-permute-start.4 = (f32[1,1920]{1,0:T(1,128)S(1)}, f32[1,1920]{1,0:T(1,128)S(1)}, u32[]{:S(2)}, u32[]{:S(2)}) collective-permute-start(f32[1,1920]{1,0:T(1,128)S(1)} %concatenate.9), channel_id=1, source_target_pairs={{0,8},{1,9},{2,10},{3,11},{4,12},{5,13},{6,14},{7,15},{8,0},{9,1},... | collective-permute-start | bytes 23048 | tf_op jit(solution)/shard_map/ppermute | solution.py:569
  18.9 3.0 %collective-permute-start.9 = (bf16[1,256,768]{2,1,0:T(8,128)(2,1)}, bf16[1,256,768]{2,1,0:T(8,128)(2,1)S(1)}, u32[]{:S(2)}, u32[]{:S(2)}) collective-permute-start(bf16[1,256,768]{2,1,0:T(8,128)(2,1)} %get-tuple-element.155.refs_6_.refs_0_), channel_id=1, source_target_pairs={{0,3},{1,2},{2,1},{3,0},{4,7},{5,6},{6,5},{7,4},{8,11},{9,10},{10,... | collective-permute-start | bytes 1179656 | tf_op jit(solution)/shard_map/ppermute | solution.py:569
  24.5 6.8 %collective-permute-done.10.slab2 = bf16[192,768]{1,0:T(8,128)(2,1)S(1)} collective-permute-done((bf16[192,768]{1,0:T(8,128)(2,1)S(1)}, bf16[192,768]{1,0:T(8,128)(2,1)S(1)}, u32[]{:S(2)}, u32[]{:S(2)}) %collective-permute-start.10) | collective-permute-done | bytes 294944 | tf_op jit(solution)/shard_map/ppermute | solution.py:569
  32.2 8.3 %collective-permute-done.8.refs_8_.refs_2_ = bf16[1,256,768]{2,1,0:T(8,128)(2,1)S(1)} collective-permute-done((bf16[1,256,768]{2,1,0:T(8,128)(2,1)}, bf16[1,256,768]{2,1,0:T(8,128)(2,1)S(1)}, u32[]{:S(2)}, u32[]{:S(2)}) %collective-permute-start.8) | collective-permute-done | bytes 393248 | tf_op jit(solution)/shard_map/ppermute | solution.py:569
  48.8 6.9 %project.1 = (bf16[8,256,192]{2,1,0:T(8,128)(2,1)}, bf16[8,256,192]{2,1,0:T(8,128)(2,1)}, bf16[8,128,192]{2,1,0:T(8,128)(2,1)}, bf16[8,192,128]{2,1,0:T(8,128)(2,1)}) custom-call(s32[4]{0:T(128)} %pad_add_fusion.place, bf16[192,576]{1,0:T(8,128)(2,1)} %get-tuple-element.133.refs_0_.slab0, bf16[192,576]{1,0:T(8,128)(2,1)} %collective-permute-done.refs_1_.slab1, ...), custom_call_target="tpu_custom_call" | custom-call | flops 1509949440 | bytes 6394384 | tf_op jit(solution)/shard_map/project/pallas_call | solution.py:75
  55.6 8.6 %attend.1 = (bf16[8,192,128]{2,1,0:T(8,128)(2,1)}, f32[8,1,384]{2,1,0:T(1,128)}) custom-call(s32[4]{0:T(128)} %pad_add_fusion.place, bf16[8,128,192]{2,1,0:T(8,128)(2,1)} %get-tuple-element.142.q_ref, bf16[8,256,192]{2,1,0:T(8,128)(2,1)} %get-tuple-element.143.k_ref, bf16[8,256,192]{2,1,0:T(8,128)(2,1)} %get-tuple-element.144.v_ref), custom_call_target="tpu_custom_call" | custom-call | flops 905969664 | bytes 2371600 | tf_op jit(solution)/shard_map/attend/pallas_call | solution.py:75
  64.3 5.9 %all-to-all-start = ((bf16[8,192,128]{2,1,0:T(8,128)(2,1)}), bf16[8,192,128]{2,1,0:T(8,128)(2,1)S(1)}, u32[]{:S(2)}, u32[]{:S(2)}) async-start(bf16[8,192,128]{2,1,0:T(8,128)(2,1)} %get-tuple-element.149.out_ref), calls=%async_computation | async-start | bytes 786432 | tf_op jit(solution)/shard_map/all_to_all | solution.py:592
  73.4 4.1 %all-to-all-done.att_ref = bf16[8,192,128]{2,1,0:T(8,128)(2,1)S(1)} async-done(((bf16[8,192,128]{2,1,0:T(8,128)(2,1)}), bf16[8,192,128]{2,1,0:T(8,128)(2,1)S(1)}, u32[]{:S(2)}, u32[]{:S(2)}) %all-to-all-start) | async-done | bytes 393248 | tf_op jit(solution)/shard_map/all_to_all | solution.py:592
  78.3 3.4 %middle.1 = (f32[256,768]{1,0:T(8,128)}, bf16[256,768]{1,0:T(8,128)(2,1)}) custom-call(s32[4]{0:T(128)} %pad_add_fusion.place, bf16[8,192,128]{2,1,0:T(8,128)(2,1)} %copy-done.8, f32[256,768]{1,0:T(8,128)} %get-tuple-element.150.resid_ref, f32[4,768]{1,0:T(4,128)} %reshape.106.vec_ref, bf16[192,768]{1,0:T(8,128)(2,1)} %slab0.3, bf16[192,768]{1,0:T(8,128)(2,1)} %copy-done.14, ...), custom_call_target="tpu_custom_call" | custom-call | flops 301989888 | bytes 3551248 | tf_op jit(solution)/shard_map/middle/pallas_call | solution.py:75
  83.9 5.6 %collect.1 = (bf16[768,2048]{1,0:T(8,128)(2,1)}, bf16[768,1024]{1,0:T(8,128)(2,1)}) custom-call(s32[4]{0:T(128)} %pad_add_fusion.place, f32[1,768]{1,0:T(1,128)} %slice.175.refs_4_.gain_ref, bf16[1,256,768]{2,1,0:T(8,128)(2,1)} %get-tuple-element.155.refs_6_.refs_0_, bf16[1,256,768]{2,1,0:T(8,128)(2,1)} %copy-done.32, bf16[1,256,768]{2,1,0:T(8,128)(2,1)} %copy-done.31, ...), custom_call_target="tpu_custom_call" | custom-call | bytes 7867408 | tf_op jit(solution)/shard_map/collect/pallas_call | solution.py:75
  89.5 3.8 %collective-permute-done.21.refs_2_ = bf16[256,768]{1,0:T(8,128)(2,1)S(1)} collective-permute-done((bf16[256,768]{1,0:T(8,128)(2,1)}, bf16[256,768]{1,0:T(8,128)(2,1)S(1)}, u32[]{:S(2)}, u32[]{:S(2)}) %collective-permute-start.21) | collective-permute-done | bytes 393248 | tf_op jit(solution)/shard_map/ppermute | solution.py:569
  95.8 8.8 %mlp.1 = (f32[256,768]{1,0:T(8,128)}, f32[256,768]{1,0:T(8,128)}, bf16[2,256,768]{2,1,0:T(8,128)(2,1)}, bf16[2,512,768]{2,1,0:T(8,128)(2,1)}, bf16[2,512,768]{2,1,0:T(8,128)(2,1)}, /*index=5*/f32[1,768]{1,0:T(1,128)}) custom-call(s32[4]{0:T(128)} %pad_add_fusion.place, bf16[256,768]{1,0:T(8,128)(2,1)} %get-tuple-element.154.refs_0_, ...), custom_call_target="tpu_custom_call" | custom-call | flops 3623878656 | bytes 11016208 | tf_op jit(solution)/shard_map/mlp/pallas_call | solution.py:75
  110.2 9.0 %mlp_back.1 = (f32[256,768]{1,0:T(8,128)}, f32[256,768]{1,0:T(8,128)}, bf16[2,256,768]{2,1,0:T(8,128)(2,1)}, bf16[2,192,768]{2,1,0:T(8,128)(2,1)}, bf16[2,192,76...) custom-call(s32[4]{0:T(128)} %pad_add_fusion.place, ...), custom_call_target="tpu_custom_call" | custom-call | flops 99999997952 | bytes 12189712 | tf_op jit(solution)/shard_map/mlp_back/pallas_call | solution.py:75
  120.6 4.2 %branch_back.1 = (f32[256,768]{1,0:T(8,128)}, bf16[256,768]{1,0:T(8,128)(2,1)}, bf16[8,192,128]{2,1,0:T(8,128)(2,1)}, f32[8,768]{1,0:T(8,128)}) custom-call(s32[4]{0:T(128)} %pad_add_fusion.place, f32[256,768]{1,0:T(8,128)} %get-tuple-element.185.own_ref, bf16[2,256,768]{2,1,0:T(8,128)(2,1)} %copy-done.6, bf16[256,768]{1,0:T(8,128)(2,1)} %copy-done.36, ...), custom_call_target="tpu_custom_call" | custom-call | flops 603979776 | bytes 5934608 | tf_op jit(solution)/shard_map/branch_back/pallas_call | solution.py:75
  124.8 3.6 %out_back.1 = (bf16[2,8,32,768]{3,2,1,0:T(8,128)(2,1)}, bf16[2,8,32,768]{3,2,1,0:T(8,128)(2,1)}) custom-call(s32[4]{0:T(128)} %pad_add_fusion.place, bf16[8,192,128]{2,1,0:T(8,128)(2,1)} %copy-done.8, bf16[256,768]{1,0:T(8,128)(2,1)} %get-tuple-element.188.grad_ref, f32[8,768]{1,0:T(8,128)} %get-tuple-element.189.sum_ref, ...), custom_call_target="tpu_custom_call" | custom-call | flops 301989888 | bytes 2386960 | tf_op jit(solution)/shard_map/out_back/pallas_call | solution.py:75
  128.4 4.1 %all-to-all-start.1 = ((bf16[8,192,128]{2,1,0:T(8,128)(2,1)}), bf16[8,192,128]{2,1,0:T(8,128)(2,1)}, u32[]{:S(2)}, u32[]{:S(2)}) async-start(bf16[8,192,128]{2,1,0:T(8,128)(2,1)} %get-tuple-element.187), calls=%async_computation.1 | async-start | bytes 786432 | tf_op jit(solution)/shard_map/all_to_all | solution.py:592
  137.4 3.1 %all-to-all-done.1.gt_ref = bf16[8,192,128]{2,1,0:T(8,128)(2,1)} async-done(((bf16[8,192,128]{2,1,0:T(8,128)(2,1)}), bf16[8,192,128]{2,1,0:T(8,128)(2,1)}, u32[]{:S(2)}, u32[]{:S(2)}) %all-to-all-start.1) | async-done | bytes 393248 | tf_op jit(solution)/shard_map/all_to_all | solution.py:592
  142.0 16.9 %attend_back.1 = (bf16[8,128,192]{2,1,0:T(8,128)(2,1)}, bf16[8,256,384]{2,1,0:T(8,128)(2,1)}, f32[8,192]{1,0:T(8,128)}) custom-call(s32[4]{0:T(128)} %pad_add_fusion.place, bf16[8,192,128]{2,1,0:T(8,128)(2,1)} %get-tuple-element.184.qt_ref, bf16[8,256,192]{2,1,0:T(8,128)(2,1)} %get-tuple-element.143.k_ref, bf16[8,256,192]{2,1,0:T(8,128)(2,1)} %get-tuple-element.144.v_ref, ...), custom_call_target="tpu_custom_call" | custom-call | flops 2264924160 | bytes 4737040 | tf_op jit(solution)/shard_map/attend_back/pallas_call | solution.py:75
  158.9 6.8 %heads_back.1 = (bf16[2,2,104,576]{3,2,1,0:T(8,128)(2,1)}, bf16[2,2,104,576]{3,2,1,0:T(8,128)(2,1)}) custom-call(s32[4]{0:T(128)} %pad_add_fusion.place, bf16[768,2048]{1,0:T(8,128)(2,1)} %get-tuple-element.199.normed_t_ref, bf16[768,1024]{1,0:T(8,128)(2,1)} %get-tuple-element.200.query_t_ref, bf16[8,128,192]{2,1,0:T(8,128)(2,1)} %get-tuple-element.216.dq_ref, ...), custom_call_target="tpu_custom_call" | custom-call | flops 1509949440 | bytes 7649296 | tf_op jit(solution)/shard_map/heads_back/pallas_call | solution.py:75
  178.0 6.0 %rows_back.1 = (bf16[4,256,768]{2,1,0:T(8,128)(2,1)}, bf16[4,256,768]{2,1,0:T(8,128)(2,1)}) custom-call(s32[4]{0:T(128)} %pad_add_fusion.place, bf16[8,128,192]{2,1,0:T(8,128)(2,1)} %get-tuple-element.216.dq_ref, bf16[8,256,384]{2,1,0:T(8,128)(2,1)} %get-tuple-element.201.dkv_ref, bf16[192,576]{1,0:T(8,128)(2,1)} %get-tuple-element.133.refs_0_.slab0, ...), custom_call_target="tpu_custom_call" | custom-call | flops 1509949440 | bytes 5996560 | tf_op jit(solution)/shard_map/rows_back/pallas_call | solution.py:75
  184.0 5.0 %collective-permute-done.38 = bf16[2,32,768]{2,1,0:T(8,128)(2,1)S(1)} collective-permute-done((bf16[2,32,768]{2,1,0:T(8,128)(2,1)}, bf16[2,32,768]{2,1,0:T(8,128)(2,1)S(1)}, u32[]{:S(2)}, u32[]{:S(2)}) %collective-permute-start.38) | collective-permute-done | bytes 98336 | tf_op jit(solution)/shard_map/ppermute | solution.py:569
  190.7 10.0 %collective-permute-done.36 = bf16[2,192,768]{2,1,0:T(8,128)(2,1)S(1)} collective-permute-done((bf16[2,192,768]{2,1,0:T(8,128)(2,1)S(1)}, bf16[2,192,768]{2,1,0:T(8,128)(2,1)S(1)}, u32[]{:S(2)}, u32[]{:S(2)}) %collective-permute-start.36) | collective-permute-done | bytes 589856 | tf_op jit(solution)/shard_map/ppermute | solution.py:569
  200.8 3.6 %collective-permute-done.40 = bf16[4,256,768]{2,1,0:T(8,128)(2,1)} collective-permute-done((bf16[4,256,768]{2,1,0:T(8,128)(2,1)}, bf16[4,256,768]{2,1,0:T(8,128)(2,1)}, u32[]{:S(2)}, u32[]{:S(2)}) %collective-permute-start.40) | collective-permute-done | bytes 1572896 | tf_op jit(solution)/shard_map/ppermute | solution.py:569
  206.8 2.9 %collective-permute-start.50 = (bf16[2,104,576]{2,1,0:T(8,128)(2,1)S(1)}, bf16[2,104,576]{2,1,0:T(8,128)(2,1)S(1)}, u32[]{:S(2)}, u32[]{:S(2)}) collective-permute-start(bf16[2,104,576]{2,1,0:T(8,128)(2,1)S(1)} %add.131), channel_id=1, source_target_pairs={{0,4},{1,5},{2,6},{3,7},{4,0},{5,1},{6,2},{7,3},{8,12},{9,13},{10,... | collective-permute-start | bytes 718856 | tf_op jit(solution)/shard_map/ppermute | solution.py:569
  214.7 4.7 %collective-permute-done.51 = bf16[2,32,768]{2,1,0:T(8,128)(2,1)S(1)} collective-permute-done((bf16[2,32,768]{2,1,0:T(8,128)(2,1)S(1)}, bf16[2,32,768]{2,1,0:T(8,128)(2,1)S(1)}, u32[]{:S(2)}, u32[]{:S(2)}) %collective-permute-start.51) | collective-permute-done | bytes 98336 | tf_op jit(solution)/shard_map/ppermute | solution.py:569
  219.5 5.6 %collective-permute-done.50 = bf16[2,104,576]{2,1,0:T(8,128)(2,1)S(1)} collective-permute-done((bf16[2,104,576]{2,1,0:T(8,128)(2,1)S(1)}, bf16[2,104,576]{2,1,0:T(8,128)(2,1)S(1)}, u32[]{:S(2)}, u32[]{:S(2)}) %collective-permute-start.50) | collective-permute-done | bytes 239648 | tf_op jit(solution)/shard_map/ppermute | solution.py:569
  225.4 7.8 %collective-permute-done.47.far_ref = bf16[2,256,768]{2,1,0:T(8,128)(2,1)S(1)} collective-permute-done((bf16[2,256,768]{2,1,0:T(8,128)(2,1)S(1)}, bf16[2,256,768]{2,1,0:T(8,128)(2,1)S(1)}, u32[]{:S(2)}, u32[]{:S(2)}) %collective-permute-start.47) | collective-permute-done | bytes 786464 | tf_op jit(solution)/shard_map/ppermute | solution.py:569
  244.9 3.3 %stream_back.1 = bf16[256,767]{1,0:T(8,128)(2,1)} custom-call(s32[4]{0:T(128)} %pad_add_fusion.place, bf16[2,256,768]{2,1,0:T(8,128)(2,1)} %copy-done, bf16[2,256,768]{2,1,0:T(8,128)(2,1)} %copy-done.5, bf16[256,768]{1,0:T(8,128)(2,1)} %copy-done.27, f32[256,768]{1,0:T(8,128)} %get-tuple-element.150.resid_ref, ...), custom_call_target="tpu_custom_call" | custom-call | bytes 3943952 | tf_op jit(solution)/shard_map/stream_back/pallas_call | solution.py:75
  253.4 10.6 %collective-permute-done.53.pair = bf16[2,2,104,576]{3,2,1,0:T(8,128)(2,1)} collective-permute-done((bf16[2,2,104,576]{3,2,1,0:T(8,128)(2,1)S(1)}, bf16[2,2,104,576]{3,2,1,0:T(8,128)(2,1)}, u32[]{:S(2)}, u32[]{:S(2)}) %collective-permute-start.53) | collective-permute-done | bytes 479264 | tf_op jit(solution)/shard_map/ppermute | solution.py:569
  264.1 3.1 %heads_out.1 = (f32[192,2304]{1,0:T(8,128)}, f32[192,1]{1,0:T(8,128)}, f32[1,384]{1,0:T(1,128)}) custom-call(s32[4]{0:T(128)} %pad_add_fusion.place, bf16[2,104,576]{2,1,0:T(8,128)(2,1)} %copy-done.16, bf16[2,104,576]{2,1,0:T(8,128)(2,1)} %copy-done.17, bf16[2,2,104,576]{3,2,1,0:T(8,128)(2,1)} %collective-permute-done.53.pair, bf16[192,2304]{1,0:T(8,128)(2,1)} %weight_ref.1), custom_call_target="tpu_custom_call" | custom-call | bytes 3614992 | tf_op jit(solution)/shard_map/heads_out/pallas_call | solution.py:75
  273.7 3.1 %up_out.1 = (f32[192,3072]{1,0:T(8,128)}, f32[192,768]{1,0:T(8,128)}) custom-call(s32[4]{0:T(128)} %pad_add_fusion.place, bf16[2,120,768]{2,1,0:T(8,128)(2,1)} %copy-done.4, bf16[2,120,768]{2,1,0:T(8,128)(2,1)} %copy-done.9, bf16[2,2,120,768]{3,2,1,0:T(8,128)(2,1)} %copy-done.22), custom_call_target="tpu_custom_call" | custom-call | bytes 4423696 | tf_op jit(solution)/shard_map/up_out/pallas_call | solution.py:75
  (284 shorter events, 92.3 us)
Async XLA Ops:
  0.7 15.3 %collective-permute-start.6 = (bf16[256,767]{1,0:T(8,128)(2,1)}, bf16[256,767]{1,0:T(8,128)(2,1)S(1)}, u32[]{:S(2)}, u32[]{:S(2)}) collective-permute-start(bf16[256,767]{1,0:T(8,128)(2,1)} %param.12), channel_id=1, source_target_pairs={{0,0},{1,1},{2,2},{3,3},{4,8},{5,9},{6,10},{7,11},{8,4},{9,5},{10,... | collective-permute-start | bytes 1178120 | tf_op jit(solution)/shard_map/ppermute | solution.py:569
  9.2 13.2 %collective-permute-start.4 = (f32[1,1920]{1,0:T(1,128)S(1)}, f32[1,1920]{1,0:T(1,128)S(1)}, u32[]{:S(2)}, u32[]{:S(2)}) collective-permute-start(f32[1,1920]{1,0:T(1,128)S(1)} %concatenate.9), channel_id=1, source_target_pairs={{0,8},{1,9},{2,10},{3,11},{4,12},{5,13},{6,14},{7,15},{8,0},{9,1},... | collective-permute-start | bytes 23048 | tf_op jit(solution)/shard_map/ppermute | solution.py:569
  16.0 25.5 %collective-permute-start = (bf16[192,576]{1,0:T(8,128)(2,1)}, bf16[192,576]{1,0:T(8,128)(2,1)}, u32[]{:S(2)}, u32[]{:S(2)}) collective-permute-start(bf16[192,576]{1,0:T(8,128)(2,1)} %get-tuple-element.133.refs_0_.slab0), channel_id=1, source_target_pairs={{0,8},{1,9},{2,10},{3,11},{4,12},{5,13},{6,14},{7,15},{8,0},{9,1},... | collective-permute-start | bytes 663560 | tf_op jit(solution)/shard_map/ppermute | solution.py:569
  18.9 13.3 %collective-permute-start.9 = (bf16[1,256,768]{2,1,0:T(8,128)(2,1)}, bf16[1,256,768]{2,1,0:T(8,128)(2,1)S(1)}, u32[]{:S(2)}, u32[]{:S(2)}) collective-permute-start(bf16[1,256,768]{2,1,0:T(8,128)(2,1)} %get-tuple-element.155.refs_6_.refs_0_), channel_id=1, source_target_pairs={{0,3},{1,2},{2,1},{3,0},{4,7},{5,6},{6,5},{7,4},{8,11},{9,10},{10,... | collective-permute-start | bytes 1179656 | tf_op jit(solution)/shard_map/ppermute | solution.py:569
  22.0 18.6 %collective-permute-start.8 = (bf16[1,256,768]{2,1,0:T(8,128)(2,1)}, bf16[1,256,768]{2,1,0:T(8,128)(2,1)S(1)}, u32[]{:S(2)}, u32[]{:S(2)}) collective-permute-start(bf16[1,256,768]{2,1,0:T(8,128)(2,1)} %get-tuple-element.155.refs_6_.refs_0_), channel_id=1, source_target_pairs={{0,2},{1,3},{2,0},{3,1},{4,6},{5,7},{6,4},{7,5},{8,10},{9,11},{10,... | collective-permute-start | bytes 1179656 | tf_op jit(solution)/shard_map/ppermute | solution.py:569
  22.4 18.1 %collective-permute-start.7 = (bf16[1,256,768]{2,1,0:T(8,128)(2,1)}, bf16[1,256,768]{2,1,0:T(8,128)(2,1)S(1)}, u32[]{:S(2)}, u32[]{:S(2)}) collective-permute-start(bf16[1,256,768]{2,1,0:T(8,128)(2,1)} %get-tuple-element.155.refs_6_.refs_0_), channel_id=1, source_target_pairs={{0,1},{1,0},{2,3},{3,2},{4,5},{5,4},{6,7},{7,6},{8,9},{9,8},{10,11... | collective-permute-start | bytes 1179656 | tf_op jit(solution)/shard_map/ppermute | solution.py:569
  43.6 20.7 %collective-permute-start.15 = (bf16[192,768]{1,0:T(8,128)(2,1)}, bf16[192,768]{1,0:T(8,128)(2,1)}, u32[]{:S(2)}, u32[]{:S(2)}) collective-permute-start(bf16[192,768]{1,0:T(8,128)(2,1)} %get-tuple-element.146), channel_id=1, source_target_pairs={{0,8},{1,9},{2,10},{3,11},{4,12},{5,13},{6,14},{7,15},{8,0},{9,1},... | collective-permute-start | bytes 884744 | tf_op jit(solution)/shard_map/ppermute | solution.py:569
  43.9 20.4 %collective-permute-start.16 = (bf16[192,768]{1,0:T(8,128)(2,1)}, bf16[192,768]{1,0:T(8,128)(2,1)}, u32[]{:S(2)}, u32[]{:S(2)}) collective-permute-start(bf16[192,768]{1,0:T(8,128)(2,1)} %get-tuple-element.147), channel_id=1, source_target_pairs={{0,16},{1,17},{2,18},{3,19},{4,20},{5,21},{6,22},{7,23},{8,24},{9,... | collective-permute-start | bytes 884744 | tf_op jit(solution)/shard_map/ppermute | solution.py:569
  45.4 18.9 %collective-permute-start.17 = (bf16[192,768]{1,0:T(8,128)(2,1)}, bf16[192,768]{1,0:T(8,128)(2,1)}, u32[]{:S(2)}, u32[]{:S(2)}) collective-permute-start(bf16[192,768]{1,0:T(8,128)(2,1)} %get-tuple-element.148), channel_id=1, source_target_pairs={{0,24},{1,25},{2,26},{3,27},{4,28},{5,29},{6,30},{7,31},{8,16},{9,... | collective-permute-start | bytes 884744 | tf_op jit(solution)/shard_map/ppermute | solution.py:569
  46.8 24.6 %collective-permute-start.23 = (bf16[256,767]{1,0:T(8,128)(2,1)}, bf16[256,767]{1,0:T(8,128)(2,1)S(1)}, u32[]{:S(2)}, u32[]{:S(2)}) collective-permute-start(bf16[256,767]{1,0:T(8,128)(2,1)} %param.23), channel_id=1, source_target_pairs={{0,0},{1,1},{2,2},{3,3},{4,8},{5,9},{6,10},{7,11},{8,4},{9,5},{10,... | collective-permute-start | bytes 1178120 | tf_op jit(solution)/shard_map/ppermute | solution.py:569
  64.3 13.2 %all-to-all-start = ((bf16[8,192,128]{2,1,0:T(8,128)(2,1)}), bf16[8,192,128]{2,1,0:T(8,128)(2,1)S(1)}, u32[]{:S(2)}, u32[]{:S(2)}) async-start(bf16[8,192,128]{2,1,0:T(8,128)(2,1)} %get-tuple-element.149.out_ref), calls=%async_computation | async-start | bytes 786432 | tf_op jit(solution)/shard_map/all_to_all | solution.py:592
  132.5 33.3 %collective-permute-start.31 = (bf16[2,192,768]{2,1,0:T(8,128)(2,1)}, bf16[2,192,768]{2,1,0:T(8,128)(2,1)S(1)}, u32[]{:S(2)}, u32[]{:S(2)}) collective-permute-start(bf16[2,192,768]{2,1,0:T(8,128)(2,1)} %get-tuple-element.206), channel_id=1, source_target_pairs={{0,1},{1,0},{2,3},{3,2},{4,5},{5,4},{6,7},{7,6},{8,9},{9,8},{10,11... | collective-permute-start | bytes 1769480 | tf_op jit(solution)/shard_map/ppermute | solution.py:569
  134.4 31.4 %collective-permute-start.32 = (bf16[2,192,768]{2,1,0:T(8,128)(2,1)}, bf16[2,192,768]{2,1,0:T(8,128)(2,1)S(1)}, u32[]{:S(2)}, u32[]{:S(2)}) collective-permute-start(bf16[2,192,768]{2,1,0:T(8,128)(2,1)} %get-tuple-element.207), channel_id=1, source_target_pairs={{0,2},{1,3},{2,0},{3,1},{4,6},{5,7},{6,4},{7,5},{8,10},{9,11},{10,... | collective-permute-start | bytes 1769480 | tf_op jit(solution)/shard_map/ppermute | solution.py:569
  135.8 30.2 %collective-permute-start.33 = (bf16[2,192,768]{2,1,0:T(8,128)(2,1)}, bf16[2,192,768]{2,1,0:T(8,128)(2,1)S(1)}, u32[]{:S(2)}, u32[]{:S(2)}) collective-permute-start(bf16[2,192,768]{2,1,0:T(8,128)(2,1)} %get-tuple-element.208), channel_id=1, source_target_pairs={{0,3},{1,2},{2,1},{3,0},{4,7},{5,6},{6,5},{7,4},{8,11},{9,10},{10,... | collective-permute-start | bytes 1769480 | tf_op jit(solution)/shard_map/ppermute | solution.py:569
  140.5 18.4 %collective-permute-start.30 = (bf16[8,32,768]{2,1,0:T(8,128)(2,1)S(1)}, bf16[8,32,768]{2,1,0:T(8,128)(2,1)S(1)}, u32[]{:S(2)}, u32[]{:S(2)}) collective-permute-start(bf16[8,32,768]{2,1,0:T(8,128)(2,1)S(1)} %slice_bitcast_fusion.3), channel_id=1, source_target_pairs={{0,16},{1,17},{2,18},{3,19},{4,20},{5,21},{6,22},{7,23},{8,24},{9,... | collective-permute-start | bytes 1179656 | tf_op jit(solution)/shard_map/ppermute | solution.py:569
  171.5 29.2 %collective-permute-start.36 = (bf16[2,192,768]{2,1,0:T(8,128)(2,1)S(1)}, bf16[2,192,768]{2,1,0:T(8,128)(2,1)S(1)}, u32[]{:S(2)}, u32[]{:S(2)}) collective-permute-start(bf16[2,192,768]{2,1,0:T(8,128)(2,1)S(1)} %copy-done.3), channel_id=1, source_target_pairs={{0,4},{1,5},{2,6},{3,7},{4,0},{5,1},{6,2},{7,3},{8,12},{9,13},{10,... | collective-permute-start | bytes 1769480 | tf_op jit(solution)/shard_map/ppermute | solution.py:569
  173.1 17.6 %collective-permute-start.35 = (bf16[2,104,576]{2,1,0:T(8,128)(2,1)S(1)}, bf16[2,104,576]{2,1,0:T(8,128)(2,1)S(1)}, u32[]{:S(2)}, u32[]{:S(2)}) collective-permute-start(bf16[2,104,576]{2,1,0:T(8,128)(2,1)S(1)} %get-tuple-element.219), channel_id=1, source_target_pairs={{0,16},{1,17},{2,18},{3,19},{4,20},{5,21},{6,22},{7,23},{8,24},{9,... | collective-permute-start | bytes 718856 | tf_op jit(solution)/shard_map/ppermute | solution.py:569
  175.1 14.0 %collective-permute-start.38 = (bf16[2,32,768]{2,1,0:T(8,128)(2,1)}, bf16[2,32,768]{2,1,0:T(8,128)(2,1)S(1)}, u32[]{:S(2)}, u32[]{:S(2)}) collective-permute-start(bf16[2,32,768]{2,1,0:T(8,128)(2,1)} %get-tuple-element.222), channel_id=1, source_target_pairs={{0,2},{1,3},{2,0},{3,1},{4,6},{5,7},{6,4},{7,5},{8,10},{9,11},{10,... | collective-permute-start | bytes 294920 | tf_op jit(solution)/shard_map/ppermute | solution.py:569
  175.4 15.2 %collective-permute-start.39 = (bf16[2,32,768]{2,1,0:T(8,128)(2,1)}, bf16[2,32,768]{2,1,0:T(8,128)(2,1)S(1)}, u32[]{:S(2)}, u32[]{:S(2)}) collective-permute-start(bf16[2,32,768]{2,1,0:T(8,128)(2,1)} %get-tuple-element.223), channel_id=1, source_target_pairs={{0,3},{1,2},{2,1},{3,0},{4,7},{5,6},{6,5},{7,4},{8,11},{9,10},{10,... | collective-permute-start | bytes 294920 | tf_op jit(solution)/shard_map/ppermute | solution.py:569
  206.8 12.7 %collective-permute-start.51 = (bf16[2,32,768]{2,1,0:T(8,128)(2,1)S(1)}, bf16[2,32,768]{2,1,0:T(8,128)(2,1)S(1)}, u32[]{:S(2)}, u32[]{:S(2)}) collective-permute-start(bf16[2,32,768]{2,1,0:T(8,128)(2,1)S(1)} %add_add_fusion), channel_id=1, source_target_pairs={{0,4},{1,5},{2,6},{3,7},{4,0},{5,1},{6,2},{7,3},{8,12},{9,13},{10,... | collective-permute-start | bytes 294920 | tf_op jit(solution)/shard_map/ppermute | solution.py:569
  206.8 18.3 %collective-permute-start.50 = (bf16[2,104,576]{2,1,0:T(8,128)(2,1)S(1)}, bf16[2,104,576]{2,1,0:T(8,128)(2,1)S(1)}, u32[]{:S(2)}, u32[]{:S(2)}) collective-permute-start(bf16[2,104,576]{2,1,0:T(8,128)(2,1)S(1)} %add.131), channel_id=1, source_target_pairs={{0,4},{1,5},{2,6},{3,7},{4,0},{5,1},{6,2},{7,3},{8,12},{9,13},{10,... | collective-permute-start | bytes 718856 | tf_op jit(solution)/shard_map/ppermute | solution.py:569
  210.9 26.0 %collective-permute-start.56 = (bf16[2,96,768]{2,1,0:T(8,128)(2,1)S(1)}, bf16[2,96,768]{2,1,0:T(8,128)(2,1)S(1)}, u32[]{:S(2)}, u32[]{:S(2)}) collective-permute-start(bf16[2,96,768]{2,1,0:T(8,128)(2,1)S(1)} %get-tuple-element.271.own), channel_id=1, source_target_pairs={{0,2},{1,3},{2,0},{3,1},{4,6},{5,7},{6,4},{7,5},{8,10},{9,11},{10,... | collective-permute-start | bytes 884744 | tf_op jit(solution)/shard_map/ppermute | solution.py:569
  212.7 20.5 %collective-permute-start.47 = (bf16[2,256,768]{2,1,0:T(8,128)(2,1)S(1)}, bf16[2,256,768]{2,1,0:T(8,128)(2,1)S(1)}, u32[]{:S(2)}, u32[]{:S(2)}) collective-permute-start(bf16[2,256,768]{2,1,0:T(8,128)(2,1)S(1)} %get-tuple-element.256), channel_id=1, source_target_pairs={{0,1},{1,0},{2,3},{3,2},{4,5},{5,4},{6,7},{7,6},{8,9},{9,8},{10,11... | collective-permute-start | bytes 2359304 | tf_op jit(solution)/shard_map/ppermute | solution.py:569
  212.8 22.6 %collective-permute-start.44 = (bf16[2,256,768]{2,1,0:T(8,128)(2,1)S(1)}, bf16[2,256,768]{2,1,0:T(8,128)(2,1)S(1)}, u32[]{:S(2)}, u32[]{:S(2)}) collective-permute-start(bf16[2,256,768]{2,1,0:T(8,128)(2,1)S(1)} %copy-done.46), channel_id=1, source_target_pairs={{0,8},{1,9},{2,10},{3,11},{4,12},{5,13},{6,14},{7,15},{8,0},{9,1},... | collective-permute-start | bytes 2359304 | tf_op jit(solution)/shard_map/ppermute | solution.py:569
  225.2 13.2 %collective-permute-start.52 = (bf16[2,104,576]{2,1,0:T(8,128)(2,1)S(1)}, bf16[2,104,576]{2,1,0:T(8,128)(2,1)S(1)}, u32[]{:S(2)}, u32[]{:S(2)}) collective-permute-start(bf16[2,104,576]{2,1,0:T(8,128)(2,1)S(1)} %get-tuple-element.277.own), channel_id=1, source_target_pairs={{0,2},{1,3},{2,0},{3,1},{4,6},{5,7},{6,4},{7,5},{8,10},{9,11},{10,... | collective-permute-start | bytes 718856 | tf_op jit(solution)/shard_map/ppermute | solution.py:569
  225.3 15.8 %collective-permute-start.54 = (bf16[2,120,768]{2,1,0:T(8,128)(2,1)S(1)}, bf16[2,120,768]{2,1,0:T(8,128)(2,1)S(1)}, u32[]{:S(2)}, u32[]{:S(2)}) collective-permute-start(bf16[2,120,768]{2,1,0:T(8,128)(2,1)S(1)} %fusion.10.own), channel_id=1, source_target_pairs={{0,1},{1,0},{2,3},{3,2},{4,5},{5,4},{6,7},{7,6},{8,9},{9,8},{10,11... | collective-permute-start | bytes 1105928 | tf_op jit(solution)/shard_map/ppermute | solution.py:569
  236.3 13.8 %collective-permute-start.45 = (bf16[256,768]{1,0:T(8,128)(2,1)}, bf16[256,768]{1,0:T(8,128)(2,1)}, u32[]{:S(2)}, u32[]{:S(2)}) collective-permute-start(bf16[256,768]{1,0:T(8,128)(2,1)} %fusion.2), channel_id=1, source_target_pairs={{0,16},{1,17},{2,18},{3,19},{4,20},{5,21},{6,22},{7,23},{8,24},{9,... | collective-permute-start | bytes 1179656 | tf_op jit(solution)/shard_map/ppermute | solution.py:569
  237.9 31.6 %collective-permute-start.57 = (bf16[2,2,96,768]{3,2,1,0:T(8,128)(2,1)}, bf16[2,2,96,768]{3,2,1,0:T(8,128)(2,1)}, u32[]{:S(2)}, u32[]{:S(2)}) collective-permute-start(bf16[2,2,96,768]{3,2,1,0:T(8,128)(2,1)} %pad_maximum_fusion.1), channel_id=1, source_target_pairs={{0,1},{1,0},{2,3},{3,2},{4,5},{5,4},{6,7},{7,6},{8,9},{9,8},{10,11... | collective-permute-start | bytes 1769480 | tf_op jit(solution)/shard_map/ppermute | solution.py:569
  238.5 25.6 %collective-permute-start.53 = (bf16[2,2,104,576]{3,2,1,0:T(8,128)(2,1)S(1)}, bf16[2,2,104,576]{3,2,1,0:T(8,128)(2,1)}, u32[]{:S(2)}, u32[]{:S(2)}) collective-permute-start(bf16[2,2,104,576]{3,2,1,0:T(8,128)(2,1)S(1)} %pad_maximum_fusion.2), channel_id=1, source_target_pairs={{0,1},{1,0},{2,3},{3,2},{4,5},{5,4},{6,7},{7,6},{8,9},{9,8},{10,11... | collective-permute-start | bytes 1437704 | tf_op jit(solution)/shard_map/ppermute | solution.py:569
  242.1 30.8 %collective-permute-start.55 = (bf16[2,2,120,768]{3,2,1,0:T(8,128)(2,1)}, bf16[2,2,120,768]{3,2,1,0:T(8,128)(2,1)S(1)}, u32[]{:S(2)}, u32[]{:S(2)}) collective-permute-start(bf16[2,2,120,768]{3,2,1,0:T(8,128)(2,1)} %pad_maximum_fusion), channel_id=1, source_target_pairs={{0,2},{1,3},{2,0},{3,1},{4,6},{5,7},{6,4},{7,5},{8,10},{9,11},{10,... | collective-permute-start | bytes 2211848 | tf_op jit(solution)/shard_map/ppermute | solution.py:569
  248.3 28.6 %collective-permute-start.49 = (bf16[256,767]{1,0:T(8,128)(2,1)}, bf16[256,767]{1,0:T(8,128)(2,1)S(1)}, u32[]{:S(2)}, u32[]{:S(2)}) collective-permute-start(bf16[256,767]{1,0:T(8,128)(2,1)} %stream_back.1), channel_id=1, source_target_pairs={{0,0},{1,1},{2,2},{3,3},{4,8},{5,9},{6,10},{7,11},{8,4},{9,5},{10,... | collective-permute-start | bytes 1178120 | tf_op jit(solution)/shard_map/ppermute | solution.py:569
  251.5 26.3 %collective-permute-start.46 = (bf16[256,767]{1,0:T(8,128)(2,1)S(1)}, bf16[256,767]{1,0:T(8,128)(2,1)S(1)}, u32[]{:S(2)}, u32[]{:S(2)}) collective-permute-start(bf16[256,767]{1,0:T(8,128)(2,1)S(1)} %fusion.1), channel_id=1, source_target_pairs={{0,0},{1,1},{2,2},{3,3},{4,8},{5,9},{6,10},{7,11},{8,4},{9,5},{10,... | collective-permute-start | bytes 1178120 | tf_op jit(solution)/shard_map/ppermute | solution.py:569
  (86 other events, 723.7 us)

commit v3 on v2

--- a/solution.py
+++ b/solution.py
@@ -144,7 +144,7 @@
     pieces = refs[6:-7]
     k_ref, v_ref, q_ref, qt_ref, wq, wkv, normed_ref = refs[-7:]
     load_heads(place, slabs, wq, wkv)
-    gain = gain_ref[...]
+    gain = gain_ref[0:1, :]
     slot = 0
     for ref in pieces:
         for at in range(ref.shape[0]):
@@ -170,7 +170,7 @@
     blocks, rows, _ = normed_ref.shape
     query_rows = query_t_ref.shape[1] // blocks
     own = pl.ds(pl.multiple_of(place[2] * query_rows, query_rows), query_rows)
-    gain, slot = gain_ref[...], 0
+    gain, slot = gain_ref[0:1, :], 0
     for ref in pieces:
         for at in range(ref.shape[0]):
             normed_ref[slot] = (ref[at].astype(f32) * gain).astype(bf16)
@@ -688,7 +688,6 @@
         bias_heads = vectors[:, D : D + 2 * shard].reshape(2, HEAD_GROUPS, GROUP_COLS)
         bias_heads = lax.dynamic_index_in_dim(bias_heads, head_group, 1, keepdims=False)
         bias_hidden = lax.dynamic_slice_in_dim(vectors[:, D + 2 * shard :], fsdp_at, 1)
-        gain = vec[0:1]
 
         head_weights = [pltpu.VMEM((D, GROUP_COLS), bf16), pltpu.VMEM((D, 2 * GROUP_COLS), bf16)]
         tokens = ctx_count * rows
@@ -704,12 +703,12 @@
                 project_kernel,
                 "project",
                 projected,
-                (place, *w_heads, gain, bias_heads, *pieces),
+                (place, *w_heads, vec, bias_heads, *pieces),
                 flops=work,
                 scratch=head_weights + [pltpu.VMEM((ctx_count, rows, D), bf16)],
             )
         else:
-            normed = (jnp.concatenate(pieces).astype(f32) * gain).astype(bf16)
+            normed = (jnp.concatenate(pieces).astype(f32) * vec[0:1]).astype(bf16)
             block = lambda *dims: pl.BlockSpec((1,) + dims, lambda at: (at, 0, 0))
             whole = lambda *dims: pl.BlockSpec(dims, lambda at: (0,) * len(dims))
             keys, values, queries, queries_t = call(
@@ -772,11 +771,11 @@
                     shape((D, tokens), bf16),
                     shape((D, ctx_count * query_rows), bf16),
                 ),
-                (place, gain, *late_pieces),
+                (place, vec, *late_pieces),
                 scratch=[pltpu.VMEM((ctx_count, rows, D), bf16)],
             )
         else:
-            normed = (jnp.concatenate(late_pieces).astype(f32) * gain).astype(bf16)
+            normed = (jnp.concatenate(late_pieces).astype(f32) * vec[0:1]).astype(bf16)
             normed_query = lax.dynamic_index_in_dim(
                 normed.reshape(ctx_count, splits, query_rows, D), place[2], 1, keepdims=False
             )
@@ -840,6 +839,7 @@
             flops=2 * rows * D * D,
             scratch=[pltpu.VMEM((D + 8, D), f32)],
         )
+        grads, out_near = together((grads, out_near))
         out_sum = out_near + to_core(out_give)
         grads, out_sum = together((grads, out_sum))
         out_got = to_chip_row(out_sum[1])
@@ -974,12 +974,7 @@
         )
         grad_stream = swap_sequences(grad_stream)
         (grad_w_down,) = call(down_out_kernel, "down_out", (shape((hidden, D), f32),), (place, *downs))
-        grad_w_up, grad_w_out = call(
-            up_out_kernel,
-            "up_out",
-            (shape((shard, fsdp_count * hidden), f32), shape((shard, D), f32)),
-            (place, *ups),
-        )
+        grad_w_down, *heads = together((grad_w_down, *heads))
         grad_w_qkv, grad_gain_attn, grad_bias_qv = call(
             heads_out_kernel,
             "heads_out",
@@ -991,6 +986,13 @@
             (place, *heads, w_qkv),
             scratch=[pltpu.VMEM((4, 2, shard // 2 + EXTRA, 3 * GROUP_COLS), bf16)],
         )
+        grad_w_up, grad_w_out = call(
+            up_out_kernel,
+            "up_out",
+            (shape((shard, fsdp_count * hidden), f32), shape((shard, D), f32)),
+            (place, *ups),
+        )
+
         return (
             stream_out,
             grad_stream.astype(f32),

time: 282 us -> 277 us (0.982)
  waiting for transfers between devices: 85.1 us -> 82.1 us
    ppermute x58, waiting for transfers between devices: 77.9 us -> 72.9 us  [send(): return lax.ppermute(value, AXES, pairs)]
    unnamed x122 -> x124, local copies, waits for them, and re-layouts: 9.59 us -> 9.72 us
  transfers between devices with their start and end apart: 60 -> 60, of which waited for: 23 -> 20; matrix products, arithmetic and copies ran while one was open for 7% -> 7% of each run, Pallas kernels for 30% -> 30%
where the time goes in v3:
time: 277 us; the launch traced here: 274 us
  Pallas kernels  100 us (36%)
  waiting for transfers between devices  82.1 us (30%)
  starting transfers between devices  61.3 us (22%)
  other arithmetic  15.9 us (6%)
  local copies, waits for them, and re-layouts  12.8 us (5%)
    pallas_call x18, Pallas kernels, call(): pl.pallas_call(body, out_shape=tuple(outs), scratch_shapes=list(scratch),...  100 us
    ppermute x58, waiting for transfers between devices, send(): return lax.ppermute(value, AXES, pairs)  72.9 us
    ppermute x58, starting transfers between devices, send(): return lax.ppermute(value, AXES, pairs)  52.6 us
    unnamed x124, local copies, waits for them, and re-layouts  9.72 us
    all_to_all x2, waiting for transfers between devices, group_all_to_all(): lax.all_to_all(value, AXES, 0, 0, axis_index_groups=groups, tiled=True)  9.28 us
    all_to_all x2, starting transfers between devices, group_all_to_all(): lax.all_to_all(value, AXES, 0, 0, axis_index_groups=groups, tiled=True)  8.73 us
  transfers between devices with their start and end apart: 60, of which 20 were waited for; matrix products, arithmetic and copies ran while one was open for 7% of the time, Pallas kernels for 30%

profile of v3, /device:TPU:0, one launch (start us, length us, event | category | flops | bytes accessed | tf_op | source)
XLA Modules:
  0.0 273.8 jit_solution(4721476666949313478)
XLA Ops:
  6.0 3.0 %collective-permute-start.1 = (bf16[192,576]{1,0:T(8,128)(2,1)}, bf16[192,576]{1,0:T(8,128)(2,1)S(1)}, u32[]{:S(2)}, u32[]{:S(2)}) collective-permute-start(bf16[192,576]{1,0:T(8,128)(2,1)} %get-tuple-element.139.refs_0_.slab0), channel_id=1, source_target_pairs={{0,16},{1,17},{2,18},{3,19},{4,20},{5,21},{6,22},{7,23},{8,24},{9,... | collective-permute-start | bytes 663560 | tf_op jit(solution)/shard_map/ppermute | solution.py:569
  9.2 4.4 %collective-permute-done.2 = f32[1,1920]{1,0:T(1,128)S(1)} collective-permute-done((f32[1,1920]{1,0:T(1,128)S(1)}, f32[1,1920]{1,0:T(1,128)S(1)}, u32[]{:S(2)}, u32[]{:S(2)}) %collective-permute-start.2) | collective-permute-done | bytes 7712 | tf_op jit(solution)/shard_map/ppermute | solution.py:569
  16.5 3.5 %collective-permute-start.9 = (bf16[1,256,768]{2,1,0:T(8,128)(2,1)}, bf16[1,256,768]{2,1,0:T(8,128)(2,1)S(1)}, u32[]{:S(2)}, u32[]{:S(2)}) collective-permute-start(bf16[1,256,768]{2,1,0:T(8,128)(2,1)} %get-tuple-element.161.refs_6_.refs_0_), channel_id=1, source_target_pairs={{0,3},{1,2},{2,1},{3,0},{4,7},{5,6},{6,5},{7,4},{8,11},{9,10},{10,... | collective-permute-start | bytes 1179656 | tf_op jit(solution)/shard_map/ppermute | solution.py:569
  23.6 6.2 %collective-permute-done.10.slab2 = bf16[192,768]{1,0:T(8,128)(2,1)S(1)} collective-permute-done((bf16[192,768]{1,0:T(8,128)(2,1)S(1)}, bf16[192,768]{1,0:T(8,128)(2,1)S(1)}, u32[]{:S(2)}, u32[]{:S(2)}) %collective-permute-start.10) | collective-permute-done | bytes 294944 | tf_op jit(solution)/shard_map/ppermute | solution.py:569
  31.8 6.2 %collective-permute-done.8.refs_8_.refs_2_ = bf16[1,256,768]{2,1,0:T(8,128)(2,1)S(1)} collective-permute-done((bf16[1,256,768]{2,1,0:T(8,128)(2,1)}, bf16[1,256,768]{2,1,0:T(8,128)(2,1)S(1)}, u32[]{:S(2)}, u32[]{:S(2)}) %collective-permute-start.8) | collective-permute-done | bytes 393248 | tf_op jit(solution)/shard_map/ppermute | solution.py:569
  46.2 6.9 %project.1 = (bf16[8,256,192]{2,1,0:T(8,128)(2,1)}, bf16[8,256,192]{2,1,0:T(8,128)(2,1)}, bf16[8,128,192]{2,1,0:T(8,128)(2,1)}, bf16[8,192,128]{2,1,0:T(8,128)(2,1)}) custom-call(s32[4]{0:T(128)} %pad_add_fusion.place, bf16[192,576]{1,0:T(8,128)(2,1)} %get-tuple-element.139.refs_0_.slab0, bf16[192,576]{1,0:T(8,128)(2,1)} %copy-done.55, ...), custom_call_target="tpu_custom_call" | custom-call | flops 1509949440 | bytes 6403600 | tf_op jit(solution)/shard_map/project/pallas_call | solution.py:75
  53.2 8.6 %attend.1 = (bf16[8,192,128]{2,1,0:T(8,128)(2,1)}, f32[8,1,384]{2,1,0:T(1,128)}) custom-call(s32[4]{0:T(128)} %pad_add_fusion.place, bf16[8,128,192]{2,1,0:T(8,128)(2,1)} %get-tuple-element.148.q_ref, bf16[8,256,192]{2,1,0:T(8,128)(2,1)} %get-tuple-element.149.k_ref, bf16[8,256,192]{2,1,0:T(8,128)(2,1)} %get-tuple-element.150.v_ref), custom_call_target="tpu_custom_call" | custom-call | flops 905969664 | bytes 2371600 | tf_op jit(solution)/shard_map/attend/pallas_call | solution.py:75
  61.8 5.3 %all-to-all-start = ((bf16[8,192,128]{2,1,0:T(8,128)(2,1)}), bf16[8,192,128]{2,1,0:T(8,128)(2,1)S(1)}, u32[]{:S(2)}, u32[]{:S(2)}) async-start(bf16[8,192,128]{2,1,0:T(8,128)(2,1)} %get-tuple-element.155.out_ref), calls=%async_computation | async-start | bytes 786432 | tf_op jit(solution)/shard_map/all_to_all | solution.py:592
  69.5 4.9 %all-to-all-done.att_ref = bf16[8,192,128]{2,1,0:T(8,128)(2,1)S(1)} async-done(((bf16[8,192,128]{2,1,0:T(8,128)(2,1)}), bf16[8,192,128]{2,1,0:T(8,128)(2,1)S(1)}, u32[]{:S(2)}, u32[]{:S(2)}) %all-to-all-start) | async-done | bytes 393248 | tf_op jit(solution)/shard_map/all_to_all | solution.py:592
  75.2 3.4 %middle.1 = (f32[256,768]{1,0:T(8,128)}, bf16[256,768]{1,0:T(8,128)(2,1)}) custom-call(s32[4]{0:T(128)} %pad_add_fusion.place, bf16[8,192,128]{2,1,0:T(8,128)(2,1)} %copy-done.8, f32[256,768]{1,0:T(8,128)} %get-tuple-element.156.resid_ref, f32[4,768]{1,0:T(4,128)} %reshape.104.refs_4_.vec_ref.gain_ref, bf16[192,768]{1,0:T(8,128)(2,1)} %slab0.3, ...), custom_call_target="tpu_custom_call" | custom-call | flops 301989888 | bytes 3551248 | tf_op jit(solution)/shard_map/middle/pallas_call | solution.py:75
  80.6 5.6 %collect.1 = (bf16[768,2048]{1,0:T(8,128)(2,1)}, bf16[768,1024]{1,0:T(8,128)(2,1)}) custom-call(s32[4]{0:T(128)} %pad_add_fusion.place, f32[4,768]{1,0:T(4,128)} %reshape.104.refs_4_.vec_ref.gain_ref, bf16[1,256,768]{2,1,0:T(8,128)(2,1)} %get-tuple-element.161.refs_6_.refs_0_, bf16[1,256,768]{2,1,0:T(8,128)(2,1)} %copy-done.33, ...), custom_call_target="tpu_custom_call" | custom-call | bytes 7876624 | tf_op jit(solution)/shard_map/collect/pallas_call | solution.py:75
  86.2 4.0 %collective-permute-done.21.refs_2_ = bf16[256,768]{1,0:T(8,128)(2,1)S(1)} collective-permute-done((bf16[256,768]{1,0:T(8,128)(2,1)}, bf16[256,768]{1,0:T(8,128)(2,1)S(1)}, u32[]{:S(2)}, u32[]{:S(2)}) %collective-permute-start.21) | collective-permute-done | bytes 393248 | tf_op jit(solution)/shard_map/ppermute | solution.py:569
  92.7 8.8 %mlp.1 = (f32[256,768]{1,0:T(8,128)}, f32[256,768]{1,0:T(8,128)}, bf16[2,256,768]{2,1,0:T(8,128)(2,1)}, bf16[2,512,768]{2,1,0:T(8,128)(2,1)}, bf16[2,512,768]{2,1,0:T(8,128)(2,1)}, /*index=5*/f32[1,768]{1,0:T(1,128)}) custom-call(s32[4]{0:T(128)} %pad_add_fusion.place, bf16[256,768]{1,0:T(8,128)(2,1)} %get-tuple-element.160.refs_0_, ...), custom_call_target="tpu_custom_call" | custom-call | flops 3623878656 | bytes 11016208 | tf_op jit(solution)/shard_map/mlp/pallas_call | solution.py:75
  106.9 9.1 %mlp_back.1 = (f32[256,768]{1,0:T(8,128)}, f32[256,768]{1,0:T(8,128)}, bf16[2,256,768]{2,1,0:T(8,128)(2,1)}, bf16[2,192,768]{2,1,0:T(8,128)(2,1)}, bf16[2,192,76...) custom-call(s32[4]{0:T(128)} %pad_add_fusion.place, ...), custom_call_target="tpu_custom_call" | custom-call | flops 99999997952 | bytes 12189712 | tf_op jit(solution)/shard_map/mlp_back/pallas_call | solution.py:75
  117.5 4.2 %branch_back.1 = (f32[256,768]{1,0:T(8,128)}, bf16[256,768]{1,0:T(8,128)(2,1)}, bf16[8,192,128]{2,1,0:T(8,128)(2,1)}, f32[8,768]{1,0:T(8,128)}) custom-call(s32[4]{0:T(128)} %pad_add_fusion.place, f32[256,768]{1,0:T(8,128)} %get-tuple-element.191.own_ref, bf16[2,256,768]{2,1,0:T(8,128)(2,1)} %copy-done.6, bf16[256,768]{1,0:T(8,128)(2,1)} %copy-done.37, ...), custom_call_target="tpu_custom_call" | custom-call | flops 603979776 | bytes 5934608 | tf_op jit(solution)/shard_map/branch_back/pallas_call | solution.py:75
  121.7 3.6 %out_back.1 = (bf16[2,8,32,768]{3,2,1,0:T(8,128)(2,1)}, bf16[2,8,32,768]{3,2,1,0:T(8,128)(2,1)}) custom-call(s32[4]{0:T(128)} %pad_add_fusion.place, bf16[8,192,128]{2,1,0:T(8,128)(2,1)} %copy-done.8, bf16[256,768]{1,0:T(8,128)(2,1)} %get-tuple-element.194.grad_ref, f32[8,768]{1,0:T(8,128)} %get-tuple-element.195.sum_ref, ...), custom_call_target="tpu_custom_call" | custom-call | flops 301989888 | bytes 2386960 | tf_op jit(solution)/shard_map/out_back/pallas_call | solution.py:75
  125.3 3.5 %all-to-all-start.1 = ((bf16[8,192,128]{2,1,0:T(8,128)(2,1)}), bf16[8,192,128]{2,1,0:T(8,128)(2,1)S(1)}, u32[]{:S(2)}, u32[]{:S(2)}) async-start(bf16[8,192,128]{2,1,0:T(8,128)(2,1)} %get-tuple-element.193), calls=%async_computation.1 | async-start | bytes 786432 | tf_op jit(solution)/shard_map/all_to_all | solution.py:592
  132.3 4.3 %all-to-all-done.1.gt_ref = bf16[8,192,128]{2,1,0:T(8,128)(2,1)S(1)} async-done(((bf16[8,192,128]{2,1,0:T(8,128)(2,1)}), bf16[8,192,128]{2,1,0:T(8,128)(2,1)S(1)}, u32[]{:S(2)}, u32[]{:S(2)}) %all-to-all-start.1) | async-done | bytes 393248 | tf_op jit(solution)/shard_map/all_to_all | solution.py:592
  140.2 16.9 %attend_back.1 = (bf16[8,128,192]{2,1,0:T(8,128)(2,1)}, bf16[8,256,384]{2,1,0:T(8,128)(2,1)}, f32[8,192]{1,0:T(8,128)}) custom-call(s32[4]{0:T(128)} %pad_add_fusion.place, bf16[8,192,128]{2,1,0:T(8,128)(2,1)} %get-tuple-element.190.qt_ref, bf16[8,256,192]{2,1,0:T(8,128)(2,1)} %get-tuple-element.149.k_ref, bf16[8,256,192]{2,1,0:T(8,128)(2,1)} %get-tuple-element.150.v_ref, ...), custom_call_target="tpu_custom_call" | custom-call | flops 2264924160 | bytes 4737040 | tf_op jit(solution)/shard_map/attend_back/pallas_call | solution.py:75
  157.0 6.8 %heads_back.1 = (bf16[2,2,104,576]{3,2,1,0:T(8,128)(2,1)}, bf16[2,2,104,576]{3,2,1,0:T(8,128)(2,1)}) custom-call(s32[4]{0:T(128)} %pad_add_fusion.place, bf16[768,2048]{1,0:T(8,128)(2,1)} %get-tuple-element.207.normed_t_ref, bf16[768,1024]{1,0:T(8,128)(2,1)} %get-tuple-element.208.query_t_ref, bf16[8,128,192]{2,1,0:T(8,128)(2,1)} %get-tuple-element.224.dq_ref, ...), custom_call_target="tpu_custom_call" | custom-call | flops 1509949440 | bytes 7649296 | tf_op jit(solution)/shard_map/heads_back/pallas_call | solution.py:75
  175.5 6.0 %rows_back.1 = (bf16[4,256,768]{2,1,0:T(8,128)(2,1)}, bf16[4,256,768]{2,1,0:T(8,128)(2,1)}) custom-call(s32[4]{0:T(128)} %pad_add_fusion.place, bf16[8,128,192]{2,1,0:T(8,128)(2,1)} %get-tuple-element.224.dq_ref, bf16[8,256,384]{2,1,0:T(8,128)(2,1)} %get-tuple-element.209.dkv_ref, bf16[192,576]{1,0:T(8,128)(2,1)} %get-tuple-element.139.refs_0_.slab0, ...), custom_call_target="tpu_custom_call" | custom-call | flops 1509949440 | bytes 5996560 | tf_op jit(solution)/shard_map/rows_back/pallas_call | solution.py:75
  181.6 5.8 %collective-permute-done.38 = bf16[2,32,768]{2,1,0:T(8,128)(2,1)S(1)} collective-permute-done((bf16[2,32,768]{2,1,0:T(8,128)(2,1)S(1)}, bf16[2,32,768]{2,1,0:T(8,128)(2,1)S(1)}, u32[]{:S(2)}, u32[]{:S(2)}) %collective-permute-start.38) | collective-permute-done | bytes 98336 | tf_op jit(solution)/shard_map/ppermute | solution.py:569
  189.0 9.5 %collective-permute-done.36 = bf16[2,192,768]{2,1,0:T(8,128)(2,1)S(1)} collective-permute-done((bf16[2,192,768]{2,1,0:T(8,128)(2,1)S(1)}, bf16[2,192,768]{2,1,0:T(8,128)(2,1)S(1)}, u32[]{:S(2)}, u32[]{:S(2)}) %collective-permute-start.36) | collective-permute-done | bytes 589856 | tf_op jit(solution)/shard_map/ppermute | solution.py:569
  198.6 3.6 %collective-permute-done.40 = bf16[4,256,768]{2,1,0:T(8,128)(2,1)} collective-permute-done((bf16[4,256,768]{2,1,0:T(8,128)(2,1)}, bf16[4,256,768]{2,1,0:T(8,128)(2,1)}, u32[]{:S(2)}, u32[]{:S(2)}) %collective-permute-start.40) | collective-permute-done | bytes 1572896 | tf_op jit(solution)/shard_map/ppermute | solution.py:569
  205.3 2.9 %collective-permute-start.52 = (bf16[2,104,576]{2,1,0:T(8,128)(2,1)S(1)}, bf16[2,104,576]{2,1,0:T(8,128)(2,1)S(1)}, u32[]{:S(2)}, u32[]{:S(2)}) collective-permute-start(bf16[2,104,576]{2,1,0:T(8,128)(2,1)S(1)} %add.131), channel_id=1, source_target_pairs={{0,4},{1,5},{2,6},{3,7},{4,0},{5,1},{6,2},{7,3},{8,12},{9,13},{10,... | collective-permute-start | bytes 718856 | tf_op jit(solution)/shard_map/ppermute | solution.py:569
  212.6 6.0 %collective-permute-done.53 = bf16[2,32,768]{2,1,0:T(8,128)(2,1)S(1)} collective-permute-done((bf16[2,32,768]{2,1,0:T(8,128)(2,1)S(1)}, bf16[2,32,768]{2,1,0:T(8,128)(2,1)S(1)}, u32[]{:S(2)}, u32[]{:S(2)}) %collective-permute-start.53) | collective-permute-done | bytes 98336 | tf_op jit(solution)/shard_map/ppermute | solution.py:569
  218.5 5.6 %collective-permute-done.52 = bf16[2,104,576]{2,1,0:T(8,128)(2,1)S(1)} collective-permute-done((bf16[2,104,576]{2,1,0:T(8,128)(2,1)S(1)}, bf16[2,104,576]{2,1,0:T(8,128)(2,1)S(1)}, u32[]{:S(2)}, u32[]{:S(2)}) %collective-permute-start.52) | collective-permute-done | bytes 239648 | tf_op jit(solution)/shard_map/ppermute | solution.py:569
  224.5 6.5 %collective-permute-done.47.far_ref = bf16[2,256,768]{2,1,0:T(8,128)(2,1)S(1)} collective-permute-done((bf16[2,256,768]{2,1,0:T(8,128)(2,1)S(1)}, bf16[2,256,768]{2,1,0:T(8,128)(2,1)S(1)}, u32[]{:S(2)}, u32[]{:S(2)}) %collective-permute-start.47) | collective-permute-done | bytes 786464 | tf_op jit(solution)/shard_map/ppermute | solution.py:569
  242.8 3.3 %stream_back.1 = bf16[256,767]{1,0:T(8,128)(2,1)} custom-call(s32[4]{0:T(128)} %pad_add_fusion.place, bf16[2,256,768]{2,1,0:T(8,128)(2,1)} %copy-done, bf16[2,256,768]{2,1,0:T(8,128)(2,1)} %copy-done.5, bf16[256,768]{1,0:T(8,128)(2,1)} %copy-done.27, f32[256,768]{1,0:T(8,128)} %get-tuple-element.156.resid_ref, ...), custom_call_target="tpu_custom_call" | custom-call | bytes 3943952 | tf_op jit(solution)/shard_map/stream_back/pallas_call | solution.py:75
  255.1 6.8 %collective-permute-done.55.pair = bf16[2,2,104,576]{3,2,1,0:T(8,128)(2,1)} collective-permute-done((bf16[2,2,104,576]{3,2,1,0:T(8,128)(2,1)S(1)}, bf16[2,2,104,576]{3,2,1,0:T(8,128)(2,1)}, u32[]{:S(2)}, u32[]{:S(2)}) %collective-permute-start.55) | collective-permute-done | bytes 479264 | tf_op jit(solution)/shard_map/ppermute | solution.py:569
  261.9 3.1 %heads_out.1 = (f32[192,2304]{1,0:T(8,128)}, f32[192,1]{1,0:T(8,128)}, f32[1,384]{1,0:T(1,128)}) custom-call(s32[4]{0:T(128)} %pad_add_fusion.place, bf16[2,104,576]{2,1,0:T(8,128)(2,1)} %copy-done.16, bf16[2,104,576]{2,1,0:T(8,128)(2,1)} %copy-done.17, bf16[2,2,104,576]{3,2,1,0:T(8,128)(2,1)} %collective-permute-done.55.pair, bf16[192,2304]{1,0:T(8,128)(2,1)} %weight_ref.1), custom_call_target="tpu_custom_call" | custom-call | bytes 3614992 | tf_op jit(solution)/shard_map/heads_out/pallas_call | solution.py:75
  268.7 3.1 %up_out.1 = (f32[192,3072]{1,0:T(8,128)}, f32[192,768]{1,0:T(8,128)}) custom-call(s32[4]{0:T(128)} %pad_add_fusion.place, bf16[2,120,768]{2,1,0:T(8,128)(2,1)} %copy-done.4, bf16[2,120,768]{2,1,0:T(8,128)(2,1)} %copy-done.9, bf16[2,2,120,768]{3,2,1,0:T(8,128)(2,1)} %copy-done.22), custom_call_target="tpu_custom_call" | custom-call | bytes 4423696 | tf_op jit(solution)/shard_map/up_out/pallas_call | solution.py:75
  (285 shorter events, 90.6 us)
Async XLA Ops:
  0.7 12.9 %collective-permute-start.6 = (bf16[256,767]{1,0:T(8,128)(2,1)}, bf16[256,767]{1,0:T(8,128)(2,1)S(1)}, u32[]{:S(2)}, u32[]{:S(2)}) collective-permute-start(bf16[256,767]{1,0:T(8,128)(2,1)} %param.12), channel_id=1, source_target_pairs={{0,0},{1,1},{2,2},{3,3},{4,8},{5,9},{6,10},{7,11},{8,4},{9,5},{10,... | collective-permute-start | bytes 1178120 | tf_op jit(solution)/shard_map/ppermute | solution.py:569
  16.5 14.1 %collective-permute-start.9 = (bf16[1,256,768]{2,1,0:T(8,128)(2,1)}, bf16[1,256,768]{2,1,0:T(8,128)(2,1)S(1)}, u32[]{:S(2)}, u32[]{:S(2)}) collective-permute-start(bf16[1,256,768]{2,1,0:T(8,128)(2,1)} %get-tuple-element.161.refs_6_.refs_0_), channel_id=1, source_target_pairs={{0,3},{1,2},{2,1},{3,0},{4,7},{5,6},{6,5},{7,4},{8,11},{9,10},{10,... | collective-permute-start | bytes 1179656 | tf_op jit(solution)/shard_map/ppermute | solution.py:569
  20.0 17.9 %collective-permute-start.8 = (bf16[1,256,768]{2,1,0:T(8,128)(2,1)}, bf16[1,256,768]{2,1,0:T(8,128)(2,1)S(1)}, u32[]{:S(2)}, u32[]{:S(2)}) collective-permute-start(bf16[1,256,768]{2,1,0:T(8,128)(2,1)} %get-tuple-element.161.refs_6_.refs_0_), channel_id=1, source_target_pairs={{0,2},{1,3},{2,0},{3,1},{4,6},{5,7},{6,4},{7,5},{8,10},{9,11},{10,... | collective-permute-start | bytes 1179656 | tf_op jit(solution)/shard_map/ppermute | solution.py:569
  20.5 18.5 %collective-permute-start.7 = (bf16[1,256,768]{2,1,0:T(8,128)(2,1)}, bf16[1,256,768]{2,1,0:T(8,128)(2,1)S(1)}, u32[]{:S(2)}, u32[]{:S(2)}) collective-permute-start(bf16[1,256,768]{2,1,0:T(8,128)(2,1)} %get-tuple-element.161.refs_6_.refs_0_), channel_id=1, source_target_pairs={{0,1},{1,0},{2,3},{3,2},{4,5},{5,4},{6,7},{7,6},{8,9},{9,8},{10,11... | collective-permute-start | bytes 1179656 | tf_op jit(solution)/shard_map/ppermute | solution.py:569
  22.5 16.5 %collective-permute-start.4 = (f32[1,1920]{1,0:T(1,128)S(1)}, f32[1,1920]{1,0:T(1,128)S(1)}, u32[]{:S(2)}, u32[]{:S(2)}) collective-permute-start(f32[1,1920]{1,0:T(1,128)S(1)} %concatenate.9), channel_id=1, source_target_pairs={{0,8},{1,9},{2,10},{3,11},{4,12},{5,13},{6,14},{7,15},{8,0},{9,1},... | collective-permute-start | bytes 23048 | tf_op jit(solution)/shard_map/ppermute | solution.py:569
  40.5 21.3 %collective-permute-start.15 = (bf16[192,768]{1,0:T(8,128)(2,1)}, bf16[192,768]{1,0:T(8,128)(2,1)}, u32[]{:S(2)}, u32[]{:S(2)}) collective-permute-start(bf16[192,768]{1,0:T(8,128)(2,1)} %get-tuple-element.152), channel_id=1, source_target_pairs={{0,8},{1,9},{2,10},{3,11},{4,12},{5,13},{6,14},{7,15},{8,0},{9,1},... | collective-permute-start | bytes 884744 | tf_op jit(solution)/shard_map/ppermute | solution.py:569
  40.9 20.8 %collective-permute-start.16 = (bf16[192,768]{1,0:T(8,128)(2,1)}, bf16[192,768]{1,0:T(8,128)(2,1)}, u32[]{:S(2)}, u32[]{:S(2)}) collective-permute-start(bf16[192,768]{1,0:T(8,128)(2,1)} %get-tuple-element.153), channel_id=1, source_target_pairs={{0,16},{1,17},{2,18},{3,19},{4,20},{5,21},{6,22},{7,23},{8,24},{9,... | collective-permute-start | bytes 884744 | tf_op jit(solution)/shard_map/ppermute | solution.py:569
  42.6 19.2 %collective-permute-start.17 = (bf16[192,768]{1,0:T(8,128)(2,1)}, bf16[192,768]{1,0:T(8,128)(2,1)}, u32[]{:S(2)}, u32[]{:S(2)}) collective-permute-start(bf16[192,768]{1,0:T(8,128)(2,1)} %get-tuple-element.154), channel_id=1, source_target_pairs={{0,24},{1,25},{2,26},{3,27},{4,28},{5,29},{6,30},{7,31},{8,16},{9,... | collective-permute-start | bytes 884744 | tf_op jit(solution)/shard_map/ppermute | solution.py:569
  44.2 23.4 %collective-permute-start.23 = (bf16[256,767]{1,0:T(8,128)(2,1)}, bf16[256,767]{1,0:T(8,128)(2,1)S(1)}, u32[]{:S(2)}, u32[]{:S(2)}) collective-permute-start(bf16[256,767]{1,0:T(8,128)(2,1)} %param.23), channel_id=1, source_target_pairs={{0,0},{1,1},{2,2},{3,3},{4,8},{5,9},{6,10},{7,11},{8,4},{9,5},{10,... | collective-permute-start | bytes 1178120 | tf_op jit(solution)/shard_map/ppermute | solution.py:569
  61.8 12.6 %all-to-all-start = ((bf16[8,192,128]{2,1,0:T(8,128)(2,1)}), bf16[8,192,128]{2,1,0:T(8,128)(2,1)S(1)}, u32[]{:S(2)}, u32[]{:S(2)}) async-start(bf16[8,192,128]{2,1,0:T(8,128)(2,1)} %get-tuple-element.155.out_ref), calls=%async_computation | async-start | bytes 786432 | tf_op jit(solution)/shard_map/all_to_all | solution.py:592
  68.0 12.0 %collective-permute-start.25 = (bf16[256,768]{1,0:T(8,128)(2,1)S(1)}, bf16[256,768]{1,0:T(8,128)(2,1)S(1)}, u32[]{:S(2)}, u32[]{:S(2)}) collective-permute-start(bf16[256,768]{1,0:T(8,128)(2,1)S(1)} %fusion.refs_4_), channel_id=1, source_target_pairs={{0,16},{1,17},{2,18},{3,19},{4,20},{5,21},{6,22},{7,23},{8,24},{9,... | collective-permute-start | bytes 1179656 | tf_op jit(solution)/shard_map/ppermute | solution.py:569
  125.3 12.1 %collective-permute-start.29 = (bf16[2,8,32,768]{3,2,1,0:T(8,128)(2,1)}, bf16[2,8,32,768]{3,2,1,0:T(8,128)(2,1)S(1)}, u32[]{:S(2)}, u32[]{:S(2)}) collective-permute-start(bf16[2,8,32,768]{3,2,1,0:T(8,128)(2,1)} %get-tuple-element.200), channel_id=1, source_target_pairs={{0,8},{1,9},{2,10},{3,11},{4,12},{5,13},{6,14},{7,15},{8,0},{9,1},... | collective-permute-start | bytes 2359304 | tf_op jit(solution)/shard_map/ppermute | solution.py:569
  128.7 35.1 %collective-permute-start.31 = (bf16[2,192,768]{2,1,0:T(8,128)(2,1)}, bf16[2,192,768]{2,1,0:T(8,128)(2,1)S(1)}, u32[]{:S(2)}, u32[]{:S(2)}) collective-permute-start(bf16[2,192,768]{2,1,0:T(8,128)(2,1)} %get-tuple-element.214), channel_id=1, source_target_pairs={{0,1},{1,0},{2,3},{3,2},{4,5},{5,4},{6,7},{7,6},{8,9},{9,8},{10,11... | collective-permute-start | bytes 1769480 | tf_op jit(solution)/shard_map/ppermute | solution.py:569
  130.6 33.2 %collective-permute-start.32 = (bf16[2,192,768]{2,1,0:T(8,128)(2,1)}, bf16[2,192,768]{2,1,0:T(8,128)(2,1)S(1)}, u32[]{:S(2)}, u32[]{:S(2)}) collective-permute-start(bf16[2,192,768]{2,1,0:T(8,128)(2,1)} %get-tuple-element.215), channel_id=1, source_target_pairs={{0,2},{1,3},{2,0},{3,1},{4,6},{5,7},{6,4},{7,5},{8,10},{9,11},{10,... | collective-permute-start | bytes 1769480 | tf_op jit(solution)/shard_map/ppermute | solution.py:569
  132.1 31.8 %collective-permute-start.33 = (bf16[2,192,768]{2,1,0:T(8,128)(2,1)}, bf16[2,192,768]{2,1,0:T(8,128)(2,1)S(1)}, u32[]{:S(2)}, u32[]{:S(2)}) collective-permute-start(bf16[2,192,768]{2,1,0:T(8,128)(2,1)} %get-tuple-element.216), channel_id=1, source_target_pairs={{0,3},{1,2},{2,1},{3,0},{4,7},{5,6},{6,5},{7,4},{8,11},{9,10},{10,... | collective-permute-start | bytes 1769480 | tf_op jit(solution)/shard_map/ppermute | solution.py:569
  138.7 18.3 %collective-permute-start.30 = (bf16[8,32,768]{2,1,0:T(8,128)(2,1)S(1)}, bf16[8,32,768]{2,1,0:T(8,128)(2,1)S(1)}, u32[]{:S(2)}, u32[]{:S(2)}) collective-permute-start(bf16[8,32,768]{2,1,0:T(8,128)(2,1)S(1)} %slice_bitcast_fusion.3), channel_id=1, source_target_pairs={{0,16},{1,17},{2,18},{3,19},{4,20},{5,21},{6,22},{7,23},{8,24},{9,... | collective-permute-start | bytes 1179656 | tf_op jit(solution)/shard_map/ppermute | solution.py:569
  169.2 29.3 %collective-permute-start.36 = (bf16[2,192,768]{2,1,0:T(8,128)(2,1)S(1)}, bf16[2,192,768]{2,1,0:T(8,128)(2,1)S(1)}, u32[]{:S(2)}, u32[]{:S(2)}) collective-permute-start(bf16[2,192,768]{2,1,0:T(8,128)(2,1)S(1)} %copy-done.3), channel_id=1, source_target_pairs={{0,4},{1,5},{2,6},{3,7},{4,0},{5,1},{6,2},{7,3},{8,12},{9,13},{10,... | collective-permute-start | bytes 1769480 | tf_op jit(solution)/shard_map/ppermute | solution.py:569
  171.5 17.4 %collective-permute-start.35 = (bf16[2,104,576]{2,1,0:T(8,128)(2,1)S(1)}, bf16[2,104,576]{2,1,0:T(8,128)(2,1)S(1)}, u32[]{:S(2)}, u32[]{:S(2)}) collective-permute-start(bf16[2,104,576]{2,1,0:T(8,128)(2,1)S(1)} %get-tuple-element.227), channel_id=1, source_target_pairs={{0,16},{1,17},{2,18},{3,19},{4,20},{5,21},{6,22},{7,23},{8,24},{9,... | collective-permute-start | bytes 718856 | tf_op jit(solution)/shard_map/ppermute | solution.py:569
  172.1 15.2 %collective-permute-start.38 = (bf16[2,32,768]{2,1,0:T(8,128)(2,1)S(1)}, bf16[2,32,768]{2,1,0:T(8,128)(2,1)S(1)}, u32[]{:S(2)}, u32[]{:S(2)}) collective-permute-start(bf16[2,32,768]{2,1,0:T(8,128)(2,1)S(1)} %get-tuple-element.230), channel_id=1, source_target_pairs={{0,2},{1,3},{2,0},{3,1},{4,6},{5,7},{6,4},{7,5},{8,10},{9,11},{10,... | collective-permute-start | bytes 294920 | tf_op jit(solution)/shard_map/ppermute | solution.py:569
  173.5 15.5 %collective-permute-start.39 = (bf16[2,32,768]{2,1,0:T(8,128)(2,1)S(1)}, bf16[2,32,768]{2,1,0:T(8,128)(2,1)S(1)}, u32[]{:S(2)}, u32[]{:S(2)}) collective-permute-start(bf16[2,32,768]{2,1,0:T(8,128)(2,1)S(1)} %get-tuple-element.231), channel_id=1, source_target_pairs={{0,3},{1,2},{2,1},{3,0},{4,7},{5,6},{6,5},{7,4},{8,11},{9,10},{10,... | collective-permute-start | bytes 294920 | tf_op jit(solution)/shard_map/ppermute | solution.py:569
  205.3 13.3 %collective-permute-start.53 = (bf16[2,32,768]{2,1,0:T(8,128)(2,1)S(1)}, bf16[2,32,768]{2,1,0:T(8,128)(2,1)S(1)}, u32[]{:S(2)}, u32[]{:S(2)}) collective-permute-start(bf16[2,32,768]{2,1,0:T(8,128)(2,1)S(1)} %add_add_fusion), channel_id=1, source_target_pairs={{0,4},{1,5},{2,6},{3,7},{4,0},{5,1},{6,2},{7,3},{8,12},{9,13},{10,... | collective-permute-start | bytes 294920 | tf_op jit(solution)/shard_map/ppermute | solution.py:569
  205.3 18.9 %collective-permute-start.52 = (bf16[2,104,576]{2,1,0:T(8,128)(2,1)S(1)}, bf16[2,104,576]{2,1,0:T(8,128)(2,1)S(1)}, u32[]{:S(2)}, u32[]{:S(2)}) collective-permute-start(bf16[2,104,576]{2,1,0:T(8,128)(2,1)S(1)} %add.131), channel_id=1, source_target_pairs={{0,4},{1,5},{2,6},{3,7},{4,0},{5,1},{6,2},{7,3},{8,12},{9,13},{10,... | collective-permute-start | bytes 718856 | tf_op jit(solution)/shard_map/ppermute | solution.py:569
  208.7 26.0 %collective-permute-start.50 = (bf16[2,96,768]{2,1,0:T(8,128)(2,1)S(1)}, bf16[2,96,768]{2,1,0:T(8,128)(2,1)S(1)}, u32[]{:S(2)}, u32[]{:S(2)}) collective-permute-start(bf16[2,96,768]{2,1,0:T(8,128)(2,1)S(1)} %get-tuple-element.283.own), channel_id=1, source_target_pairs={{0,2},{1,3},{2,0},{3,1},{4,6},{5,7},{6,4},{7,5},{8,10},{9,11},{10,... | collective-permute-start | bytes 884744 | tf_op jit(solution)/shard_map/ppermute | solution.py:569
  210.5 20.5 %collective-permute-start.47 = (bf16[2,256,768]{2,1,0:T(8,128)(2,1)S(1)}, bf16[2,256,768]{2,1,0:T(8,128)(2,1)S(1)}, u32[]{:S(2)}, u32[]{:S(2)}) collective-permute-start(bf16[2,256,768]{2,1,0:T(8,128)(2,1)S(1)} %get-tuple-element.268), channel_id=1, source_target_pairs={{0,1},{1,0},{2,3},{3,2},{4,5},{5,4},{6,7},{7,6},{8,9},{9,8},{10,11... | collective-permute-start | bytes 2359304 | tf_op jit(solution)/shard_map/ppermute | solution.py:569
  210.6 22.6 %collective-permute-start.44 = (bf16[2,256,768]{2,1,0:T(8,128)(2,1)S(1)}, bf16[2,256,768]{2,1,0:T(8,128)(2,1)S(1)}, u32[]{:S(2)}, u32[]{:S(2)}) collective-permute-start(bf16[2,256,768]{2,1,0:T(8,128)(2,1)S(1)} %copy-done.47), channel_id=1, source_target_pairs={{0,8},{1,9},{2,10},{3,11},{4,12},{5,13},{6,14},{7,15},{8,0},{9,1},... | collective-permute-start | bytes 2359304 | tf_op jit(solution)/shard_map/ppermute | solution.py:569
  224.4 14.5 %collective-permute-start.56 = (bf16[2,120,768]{2,1,0:T(8,128)(2,1)S(1)}, bf16[2,120,768]{2,1,0:T(8,128)(2,1)S(1)}, u32[]{:S(2)}, u32[]{:S(2)}) collective-permute-start(bf16[2,120,768]{2,1,0:T(8,128)(2,1)S(1)} %fusion.10.own), channel_id=1, source_target_pairs={{0,1},{1,0},{2,3},{3,2},{4,5},{5,4},{6,7},{7,6},{8,9},{9,8},{10,11... | collective-permute-start | bytes 1105928 | tf_op jit(solution)/shard_map/ppermute | solution.py:569
  234.1 13.8 %collective-permute-start.45 = (bf16[256,768]{1,0:T(8,128)(2,1)}, bf16[256,768]{1,0:T(8,128)(2,1)}, u32[]{:S(2)}, u32[]{:S(2)}) collective-permute-start(bf16[256,768]{1,0:T(8,128)(2,1)} %fusion.2), channel_id=1, source_target_pairs={{0,16},{1,17},{2,18},{3,19},{4,20},{5,21},{6,22},{7,23},{8,24},{9,... | collective-permute-start | bytes 1179656 | tf_op jit(solution)/shard_map/ppermute | solution.py:569
  235.7 16.6 %collective-permute-start.51 = (bf16[2,2,96,768]{3,2,1,0:T(8,128)(2,1)}, bf16[2,2,96,768]{3,2,1,0:T(8,128)(2,1)}, u32[]{:S(2)}, u32[]{:S(2)}) collective-permute-start(bf16[2,2,96,768]{3,2,1,0:T(8,128)(2,1)} %pad_maximum_fusion.1), channel_id=1, source_target_pairs={{0,1},{1,0},{2,3},{3,2},{4,5},{5,4},{6,7},{7,6},{8,9},{9,8},{10,11... | collective-permute-start | bytes 1769480 | tf_op jit(solution)/shard_map/ppermute | solution.py:569
  235.8 26.1 %collective-permute-start.55 = (bf16[2,2,104,576]{3,2,1,0:T(8,128)(2,1)S(1)}, bf16[2,2,104,576]{3,2,1,0:T(8,128)(2,1)}, u32[]{:S(2)}, u32[]{:S(2)}) collective-permute-start(bf16[2,2,104,576]{3,2,1,0:T(8,128)(2,1)S(1)} %pad_maximum_fusion.2), channel_id=1, source_target_pairs={{0,1},{1,0},{2,3},{3,2},{4,5},{5,4},{6,7},{7,6},{8,9},{9,8},{10,11... | collective-permute-start | bytes 1437704 | tf_op jit(solution)/shard_map/ppermute | solution.py:569
  239.9 28.0 %collective-permute-start.57 = (bf16[2,2,120,768]{3,2,1,0:T(8,128)(2,1)}, bf16[2,2,120,768]{3,2,1,0:T(8,128)(2,1)S(1)}, u32[]{:S(2)}, u32[]{:S(2)}) collective-permute-start(bf16[2,2,120,768]{3,2,1,0:T(8,128)(2,1)} %pad_maximum_fusion), channel_id=1, source_target_pairs={{0,2},{1,3},{2,0},{3,1},{4,6},{5,7},{6,4},{7,5},{8,10},{9,11},{10,... | collective-permute-start | bytes 2211848 | tf_op jit(solution)/shard_map/ppermute | solution.py:569
  246.1 25.8 %collective-permute-start.49 = (bf16[256,767]{1,0:T(8,128)(2,1)}, bf16[256,767]{1,0:T(8,128)(2,1)S(1)}, u32[]{:S(2)}, u32[]{:S(2)}) collective-permute-start(bf16[256,767]{1,0:T(8,128)(2,1)} %stream_back.1), channel_id=1, source_target_pairs={{0,0},{1,1},{2,2},{3,3},{4,8},{5,9},{6,10},{7,11},{8,4},{9,5},{10,... | collective-permute-start | bytes 1178120 | tf_op jit(solution)/shard_map/ppermute | solution.py:569
  249.3 23.5 %collective-permute-start.46 = (bf16[256,767]{1,0:T(8,128)(2,1)S(1)}, bf16[256,767]{1,0:T(8,128)(2,1)S(1)}, u32[]{:S(2)}, u32[]{:S(2)}) collective-permute-start(bf16[256,767]{1,0:T(8,128)(2,1)S(1)} %fusion.1), channel_id=1, source_target_pairs={{0,0},{1,1},{2,2},{3,3},{4,8},{5,9},{6,10},{7,11},{8,4},{9,5},{10,... | collective-permute-start | bytes 1178120 | tf_op jit(solution)/shard_map/ppermute | solution.py:569
  (87 other events, 647.7 us)

commit v4 on v3

--- a/solution.py
+++ b/solution.py
@@ -974,7 +974,13 @@
         )
         grad_stream = swap_sequences(grad_stream)
         (grad_w_down,) = call(down_out_kernel, "down_out", (shape((hidden, D), f32),), (place, *downs))
-        grad_w_down, *heads = together((grad_w_down, *heads))
+        grad_w_up, grad_w_out = call(
+            up_out_kernel,
+            "up_out",
+            (shape((shard, fsdp_count * hidden), f32), shape((shard, D), f32)),
+            (place, *ups),
+        )
+        grad_w_down, grad_w_up, *heads = together((grad_w_down, grad_w_up, *heads))
         grad_w_qkv, grad_gain_attn, grad_bias_qv = call(
             heads_out_kernel,
             "heads_out",
@@ -985,12 +991,6 @@
             ),
             (place, *heads, w_qkv),
             scratch=[pltpu.VMEM((4, 2, shard // 2 + EXTRA, 3 * GROUP_COLS), bf16)],
-        )
-        grad_w_up, grad_w_out = call(
-            up_out_kernel,
-            "up_out",
-            (shape((shard, fsdp_count * hidden), f32), shape((shard, D), f32)),
-            (place, *ups),
         )
 
         return (

time: 277 us -> 278 us (level)
  no operation moved by 1% of the time
where the time goes in v4:
time: 278 us; the launch traced here: 274 us
  Pallas kernels  100 us (36%)
  waiting for transfers between devices  82.6 us (30%)
  starting transfers between devices  61.3 us (22%)
  other arithmetic  15.9 us (6%)
  local copies, waits for them, and re-layouts  12.8 us (5%)
    pallas_call x18, Pallas kernels, call(): pl.pallas_call(body, out_shape=tuple(outs), scratch_shapes=list(scratch),...  100 us
    ppermute x58, waiting for transfers between devices, send(): return lax.ppermute(value, AXES, pairs)  73.3 us
    ppermute x58, starting transfers between devices, send(): return lax.ppermute(value, AXES, pairs)  52.6 us
    unnamed x124, local copies, waits for them, and re-layouts  9.72 us
    all_to_all x2, waiting for transfers between devices, group_all_to_all(): lax.all_to_all(value, AXES, 0, 0, axis_index_groups=groups, tiled=True)  9.28 us
    all_to_all x2, starting transfers between devices, group_all_to_all(): lax.all_to_all(value, AXES, 0, 0, axis_index_groups=groups, tiled=True)  8.73 us
  transfers between devices with their start and end apart: 60, of which 20 were waited for; matrix products, arithmetic and copies ran while one was open for 7% of the time, Pallas kernels for 30%

profile of v4, /device:TPU:0, one launch (start us, length us, event | category | flops | bytes accessed | tf_op | source)
XLA Modules:
  0.0 274.4 jit_solution(3722081637065877624)
XLA Ops:
  6.0 3.0 %collective-permute-start.1 = (bf16[192,576]{1,0:T(8,128)(2,1)}, bf16[192,576]{1,0:T(8,128)(2,1)S(1)}, u32[]{:S(2)}, u32[]{:S(2)}) collective-permute-start(bf16[192,576]{1,0:T(8,128)(2,1)} %get-tuple-element.140.refs_0_.slab0), channel_id=1, source_target_pairs={{0,16},{1,17},{2,18},{3,19},{4,20},{5,21},{6,22},{7,23},{8,24},{9,... | collective-permute-start | bytes 663560 | tf_op jit(solution)/shard_map/ppermute | solution.py:569
  9.2 4.4 %collective-permute-done.2 = f32[1,1920]{1,0:T(1,128)S(1)} collective-permute-done((f32[1,1920]{1,0:T(1,128)S(1)}, f32[1,1920]{1,0:T(1,128)S(1)}, u32[]{:S(2)}, u32[]{:S(2)}) %collective-permute-start.2) | collective-permute-done | bytes 7712 | tf_op jit(solution)/shard_map/ppermute | solution.py:569
  16.5 3.5 %collective-permute-start.9 = (bf16[1,256,768]{2,1,0:T(8,128)(2,1)}, bf16[1,256,768]{2,1,0:T(8,128)(2,1)S(1)}, u32[]{:S(2)}, u32[]{:S(2)}) collective-permute-start(bf16[1,256,768]{2,1,0:T(8,128)(2,1)} %get-tuple-element.162.refs_6_.refs_0_), channel_id=1, source_target_pairs={{0,3},{1,2},{2,1},{3,0},{4,7},{5,6},{6,5},{7,4},{8,11},{9,10},{10,... | collective-permute-start | bytes 1179656 | tf_op jit(solution)/shard_map/ppermute | solution.py:569
  23.6 6.2 %collective-permute-done.10.slab2 = bf16[192,768]{1,0:T(8,128)(2,1)S(1)} collective-permute-done((bf16[192,768]{1,0:T(8,128)(2,1)S(1)}, bf16[192,768]{1,0:T(8,128)(2,1)S(1)}, u32[]{:S(2)}, u32[]{:S(2)}) %collective-permute-start.10) | collective-permute-done | bytes 294944 | tf_op jit(solution)/shard_map/ppermute | solution.py:569
  31.8 6.2 %collective-permute-done.8.refs_8_.refs_2_ = bf16[1,256,768]{2,1,0:T(8,128)(2,1)S(1)} collective-permute-done((bf16[1,256,768]{2,1,0:T(8,128)(2,1)}, bf16[1,256,768]{2,1,0:T(8,128)(2,1)S(1)}, u32[]{:S(2)}, u32[]{:S(2)}) %collective-permute-start.8) | collective-permute-done | bytes 393248 | tf_op jit(solution)/shard_map/ppermute | solution.py:569
  46.2 6.9 %project.1 = (bf16[8,256,192]{2,1,0:T(8,128)(2,1)}, bf16[8,256,192]{2,1,0:T(8,128)(2,1)}, bf16[8,128,192]{2,1,0:T(8,128)(2,1)}, bf16[8,192,128]{2,1,0:T(8,128)(2,1)}) custom-call(s32[4]{0:T(128)} %pad_add_fusion.place, bf16[192,576]{1,0:T(8,128)(2,1)} %get-tuple-element.140.refs_0_.slab0, bf16[192,576]{1,0:T(8,128)(2,1)} %copy-done.55, ...), custom_call_target="tpu_custom_call" | custom-call | flops 1509949440 | bytes 6403600 | tf_op jit(solution)/shard_map/project/pallas_call | solution.py:75
  53.2 8.6 %attend.1 = (bf16[8,192,128]{2,1,0:T(8,128)(2,1)}, f32[8,1,384]{2,1,0:T(1,128)}) custom-call(s32[4]{0:T(128)} %pad_add_fusion.place, bf16[8,128,192]{2,1,0:T(8,128)(2,1)} %get-tuple-element.149.q_ref, bf16[8,256,192]{2,1,0:T(8,128)(2,1)} %get-tuple-element.150.k_ref, bf16[8,256,192]{2,1,0:T(8,128)(2,1)} %get-tuple-element.151.v_ref), custom_call_target="tpu_custom_call" | custom-call | flops 905969664 | bytes 2371600 | tf_op jit(solution)/shard_map/attend/pallas_call | solution.py:75
  61.8 5.3 %all-to-all-start = ((bf16[8,192,128]{2,1,0:T(8,128)(2,1)}), bf16[8,192,128]{2,1,0:T(8,128)(2,1)S(1)}, u32[]{:S(2)}, u32[]{:S(2)}) async-start(bf16[8,192,128]{2,1,0:T(8,128)(2,1)} %get-tuple-element.156.out_ref), calls=%async_computation | async-start | bytes 786432 | tf_op jit(solution)/shard_map/all_to_all | solution.py:592
  69.5 4.9 %all-to-all-done.att_ref = bf16[8,192,128]{2,1,0:T(8,128)(2,1)S(1)} async-done(((bf16[8,192,128]{2,1,0:T(8,128)(2,1)}), bf16[8,192,128]{2,1,0:T(8,128)(2,1)S(1)}, u32[]{:S(2)}, u32[]{:S(2)}) %all-to-all-start) | async-done | bytes 393248 | tf_op jit(solution)/shard_map/all_to_all | solution.py:592
  75.2 3.4 %middle.1 = (f32[256,768]{1,0:T(8,128)}, bf16[256,768]{1,0:T(8,128)(2,1)}) custom-call(s32[4]{0:T(128)} %pad_add_fusion.place, bf16[8,192,128]{2,1,0:T(8,128)(2,1)} %copy-done.8, f32[256,768]{1,0:T(8,128)} %get-tuple-element.157.resid_ref, f32[4,768]{1,0:T(4,128)} %reshape.104.refs_4_.vec_ref.gain_ref, bf16[192,768]{1,0:T(8,128)(2,1)} %slab0.3, ...), custom_call_target="tpu_custom_call" | custom-call | flops 301989888 | bytes 3551248 | tf_op jit(solution)/shard_map/middle/pallas_call | solution.py:75
  80.6 5.6 %collect.1 = (bf16[768,2048]{1,0:T(8,128)(2,1)}, bf16[768,1024]{1,0:T(8,128)(2,1)}) custom-call(s32[4]{0:T(128)} %pad_add_fusion.place, f32[4,768]{1,0:T(4,128)} %reshape.104.refs_4_.vec_ref.gain_ref, bf16[1,256,768]{2,1,0:T(8,128)(2,1)} %get-tuple-element.162.refs_6_.refs_0_, bf16[1,256,768]{2,1,0:T(8,128)(2,1)} %copy-done.33, ...), custom_call_target="tpu_custom_call" | custom-call | bytes 7876624 | tf_op jit(solution)/shard_map/collect/pallas_call | solution.py:75
  86.2 4.0 %collective-permute-done.21.refs_2_ = bf16[256,768]{1,0:T(8,128)(2,1)S(1)} collective-permute-done((bf16[256,768]{1,0:T(8,128)(2,1)}, bf16[256,768]{1,0:T(8,128)(2,1)S(1)}, u32[]{:S(2)}, u32[]{:S(2)}) %collective-permute-start.21) | collective-permute-done | bytes 393248 | tf_op jit(solution)/shard_map/ppermute | solution.py:569
  92.7 8.8 %mlp.1 = (f32[256,768]{1,0:T(8,128)}, f32[256,768]{1,0:T(8,128)}, bf16[2,256,768]{2,1,0:T(8,128)(2,1)}, bf16[2,512,768]{2,1,0:T(8,128)(2,1)}, bf16[2,512,768]{2,1,0:T(8,128)(2,1)}, /*index=5*/f32[1,768]{1,0:T(1,128)}) custom-call(s32[4]{0:T(128)} %pad_add_fusion.place, bf16[256,768]{1,0:T(8,128)(2,1)} %get-tuple-element.161.refs_0_, ...), custom_call_target="tpu_custom_call" | custom-call | flops 3623878656 | bytes 11016208 | tf_op jit(solution)/shard_map/mlp/pallas_call | solution.py:75
  106.9 9.1 %mlp_back.1 = (f32[256,768]{1,0:T(8,128)}, f32[256,768]{1,0:T(8,128)}, bf16[2,256,768]{2,1,0:T(8,128)(2,1)}, bf16[2,192,768]{2,1,0:T(8,128)(2,1)}, bf16[2,192,76...) custom-call(s32[4]{0:T(128)} %pad_add_fusion.place, ...), custom_call_target="tpu_custom_call" | custom-call | flops 99999997952 | bytes 12189712 | tf_op jit(solution)/shard_map/mlp_back/pallas_call | solution.py:75
  117.5 4.2 %branch_back.1 = (f32[256,768]{1,0:T(8,128)}, bf16[256,768]{1,0:T(8,128)(2,1)}, bf16[8,192,128]{2,1,0:T(8,128)(2,1)}, f32[8,768]{1,0:T(8,128)}) custom-call(s32[4]{0:T(128)} %pad_add_fusion.place, f32[256,768]{1,0:T(8,128)} %get-tuple-element.192.own_ref, bf16[2,256,768]{2,1,0:T(8,128)(2,1)} %copy-done.6, bf16[256,768]{1,0:T(8,128)(2,1)} %copy-done.37, ...), custom_call_target="tpu_custom_call" | custom-call | flops 603979776 | bytes 5934608 | tf_op jit(solution)/shard_map/branch_back/pallas_call | solution.py:75
  121.7 3.6 %out_back.1 = (bf16[2,8,32,768]{3,2,1,0:T(8,128)(2,1)}, bf16[2,8,32,768]{3,2,1,0:T(8,128)(2,1)}) custom-call(s32[4]{0:T(128)} %pad_add_fusion.place, bf16[8,192,128]{2,1,0:T(8,128)(2,1)} %copy-done.8, bf16[256,768]{1,0:T(8,128)(2,1)} %get-tuple-element.195.grad_ref, f32[8,768]{1,0:T(8,128)} %get-tuple-element.196.sum_ref, ...), custom_call_target="tpu_custom_call" | custom-call | flops 301989888 | bytes 2386960 | tf_op jit(solution)/shard_map/out_back/pallas_call | solution.py:75
  125.3 3.5 %all-to-all-start.1 = ((bf16[8,192,128]{2,1,0:T(8,128)(2,1)}), bf16[8,192,128]{2,1,0:T(8,128)(2,1)S(1)}, u32[]{:S(2)}, u32[]{:S(2)}) async-start(bf16[8,192,128]{2,1,0:T(8,128)(2,1)} %get-tuple-element.194), calls=%async_computation.1 | async-start | bytes 786432 | tf_op jit(solution)/shard_map/all_to_all | solution.py:592
  132.3 4.3 %all-to-all-done.1.gt_ref = bf16[8,192,128]{2,1,0:T(8,128)(2,1)S(1)} async-done(((bf16[8,192,128]{2,1,0:T(8,128)(2,1)}), bf16[8,192,128]{2,1,0:T(8,128)(2,1)S(1)}, u32[]{:S(2)}, u32[]{:S(2)}) %all-to-all-start.1) | async-done | bytes 393248 | tf_op jit(solution)/shard_map/all_to_all | solution.py:592
  140.2 16.9 %attend_back.1 = (bf16[8,128,192]{2,1,0:T(8,128)(2,1)}, bf16[8,256,384]{2,1,0:T(8,128)(2,1)}, f32[8,192]{1,0:T(8,128)}) custom-call(s32[4]{0:T(128)} %pad_add_fusion.place, bf16[8,192,128]{2,1,0:T(8,128)(2,1)} %get-tuple-element.191.qt_ref, bf16[8,256,192]{2,1,0:T(8,128)(2,1)} %get-tuple-element.150.k_ref, bf16[8,256,192]{2,1,0:T(8,128)(2,1)} %get-tuple-element.151.v_ref, ...), custom_call_target="tpu_custom_call" | custom-call | flops 2264924160 | bytes 4737040 | tf_op jit(solution)/shard_map/attend_back/pallas_call | solution.py:75
  157.0 6.8 %heads_back.1 = (bf16[2,2,104,576]{3,2,1,0:T(8,128)(2,1)}, bf16[2,2,104,576]{3,2,1,0:T(8,128)(2,1)}) custom-call(s32[4]{0:T(128)} %pad_add_fusion.place, bf16[768,2048]{1,0:T(8,128)(2,1)} %get-tuple-element.208.normed_t_ref, bf16[768,1024]{1,0:T(8,128)(2,1)} %get-tuple-element.209.query_t_ref, bf16[8,128,192]{2,1,0:T(8,128)(2,1)} %get-tuple-element.225.dq_ref, ...), custom_call_target="tpu_custom_call" | custom-call | flops 1509949440 | bytes 7649296 | tf_op jit(solution)/shard_map/heads_back/pallas_call | solution.py:75
  175.5 6.0 %rows_back.1 = (bf16[4,256,768]{2,1,0:T(8,128)(2,1)}, bf16[4,256,768]{2,1,0:T(8,128)(2,1)}) custom-call(s32[4]{0:T(128)} %pad_add_fusion.place, bf16[8,128,192]{2,1,0:T(8,128)(2,1)} %get-tuple-element.225.dq_ref, bf16[8,256,384]{2,1,0:T(8,128)(2,1)} %get-tuple-element.210.dkv_ref, bf16[192,576]{1,0:T(8,128)(2,1)} %get-tuple-element.140.refs_0_.slab0, ...), custom_call_target="tpu_custom_call" | custom-call | flops 1509949440 | bytes 5996560 | tf_op jit(solution)/shard_map/rows_back/pallas_call | solution.py:75
  181.6 5.8 %collective-permute-done.38 = bf16[2,32,768]{2,1,0:T(8,128)(2,1)S(1)} collective-permute-done((bf16[2,32,768]{2,1,0:T(8,128)(2,1)S(1)}, bf16[2,32,768]{2,1,0:T(8,128)(2,1)S(1)}, u32[]{:S(2)}, u32[]{:S(2)}) %collective-permute-start.38) | collective-permute-done | bytes 98336 | tf_op jit(solution)/shard_map/ppermute | solution.py:569
  189.0 9.5 %collective-permute-done.36 = bf16[2,192,768]{2,1,0:T(8,128)(2,1)S(1)} collective-permute-done((bf16[2,192,768]{2,1,0:T(8,128)(2,1)S(1)}, bf16[2,192,768]{2,1,0:T(8,128)(2,1)S(1)}, u32[]{:S(2)}, u32[]{:S(2)}) %collective-permute-start.36) | collective-permute-done | bytes 589856 | tf_op jit(solution)/shard_map/ppermute | solution.py:569
  198.6 3.6 %collective-permute-done.40 = bf16[4,256,768]{2,1,0:T(8,128)(2,1)} collective-permute-done((bf16[4,256,768]{2,1,0:T(8,128)(2,1)}, bf16[4,256,768]{2,1,0:T(8,128)(2,1)}, u32[]{:S(2)}, u32[]{:S(2)}) %collective-permute-start.40) | collective-permute-done | bytes 1572896 | tf_op jit(solution)/shard_map/ppermute | solution.py:569
  205.3 2.9 %collective-permute-start.52 = (bf16[2,104,576]{2,1,0:T(8,128)(2,1)S(1)}, bf16[2,104,576]{2,1,0:T(8,128)(2,1)S(1)}, u32[]{:S(2)}, u32[]{:S(2)}) collective-permute-start(bf16[2,104,576]{2,1,0:T(8,128)(2,1)S(1)} %add.131), channel_id=1, source_target_pairs={{0,4},{1,5},{2,6},{3,7},{4,0},{5,1},{6,2},{7,3},{8,12},{9,13},{10,... | collective-permute-start | bytes 718856 | tf_op jit(solution)/shard_map/ppermute | solution.py:569
  212.6 6.0 %collective-permute-done.53 = bf16[2,32,768]{2,1,0:T(8,128)(2,1)S(1)} collective-permute-done((bf16[2,32,768]{2,1,0:T(8,128)(2,1)S(1)}, bf16[2,32,768]{2,1,0:T(8,128)(2,1)S(1)}, u32[]{:S(2)}, u32[]{:S(2)}) %collective-permute-start.53) | collective-permute-done | bytes 98336 | tf_op jit(solution)/shard_map/ppermute | solution.py:569
  218.5 5.6 %collective-permute-done.52 = bf16[2,104,576]{2,1,0:T(8,128)(2,1)S(1)} collective-permute-done((bf16[2,104,576]{2,1,0:T(8,128)(2,1)S(1)}, bf16[2,104,576]{2,1,0:T(8,128)(2,1)S(1)}, u32[]{:S(2)}, u32[]{:S(2)}) %collective-permute-start.52) | collective-permute-done | bytes 239648 | tf_op jit(solution)/shard_map/ppermute | solution.py:569
  224.5 6.5 %collective-permute-done.47.far_ref = bf16[2,256,768]{2,1,0:T(8,128)(2,1)S(1)} collective-permute-done((bf16[2,256,768]{2,1,0:T(8,128)(2,1)S(1)}, bf16[2,256,768]{2,1,0:T(8,128)(2,1)S(1)}, u32[]{:S(2)}, u32[]{:S(2)}) %collective-permute-start.47) | collective-permute-done | bytes 786464 | tf_op jit(solution)/shard_map/ppermute | solution.py:569
  242.8 3.3 %stream_back.1 = bf16[256,767]{1,0:T(8,128)(2,1)} custom-call(s32[4]{0:T(128)} %pad_add_fusion.place, bf16[2,256,768]{2,1,0:T(8,128)(2,1)} %copy-done, bf16[2,256,768]{2,1,0:T(8,128)(2,1)} %copy-done.5, bf16[256,768]{1,0:T(8,128)(2,1)} %copy-done.27, f32[256,768]{1,0:T(8,128)} %get-tuple-element.157.resid_ref, ...), custom_call_target="tpu_custom_call" | custom-call | bytes 3943952 | tf_op jit(solution)/shard_map/stream_back/pallas_call | solution.py:75
  255.1 7.4 %collective-permute-done.55.pair = bf16[2,2,120,768]{3,2,1,0:T(8,128)(2,1)S(1)} collective-permute-done((bf16[2,2,120,768]{3,2,1,0:T(8,128)(2,1)}, bf16[2,2,120,768]{3,2,1,0:T(8,128)(2,1)S(1)}, u32[]{:S(2)}, u32[]{:S(2)}) %collective-permute-start.55) | collective-permute-done | bytes 737312 | tf_op jit(solution)/shard_map/ppermute | solution.py:569
  263.3 3.1 %up_out.1 = (f32[192,3072]{1,0:T(8,128)}, f32[192,768]{1,0:T(8,128)}) custom-call(s32[4]{0:T(128)} %pad_add_fusion.place, bf16[2,120,768]{2,1,0:T(8,128)(2,1)} %copy-done.4, bf16[2,120,768]{2,1,0:T(8,128)(2,1)} %copy-done.9, bf16[2,2,120,768]{3,2,1,0:T(8,128)(2,1)} %copy-done.22), custom_call_target="tpu_custom_call" | custom-call | bytes 4423696 | tf_op jit(solution)/shard_map/up_out/pallas_call | solution.py:75
  266.5 3.1 %heads_out.1 = (f32[192,2304]{1,0:T(8,128)}, f32[192,1]{1,0:T(8,128)}, f32[1,384]{1,0:T(1,128)}) custom-call(s32[4]{0:T(128)} %pad_add_fusion.place, bf16[2,104,576]{2,1,0:T(8,128)(2,1)} %copy-done.16, bf16[2,104,576]{2,1,0:T(8,128)(2,1)} %copy-done.17, bf16[2,2,104,576]{3,2,1,0:T(8,128)(2,1)} %collective-permute-done.57.pair, bf16[192,2304]{1,0:T(8,128)(2,1)} %weight_ref.1), custom_call_target="tpu_custom_call" | custom-call | bytes 3614992 | tf_op jit(solution)/shard_map/heads_out/pallas_call | solution.py:75
  (285 shorter events, 90.6 us)
Async XLA Ops:
  0.7 12.9 %collective-permute-start.6 = (bf16[256,767]{1,0:T(8,128)(2,1)}, bf16[256,767]{1,0:T(8,128)(2,1)S(1)}, u32[]{:S(2)}, u32[]{:S(2)}) collective-permute-start(bf16[256,767]{1,0:T(8,128)(2,1)} %param.12), channel_id=1, source_target_pairs={{0,0},{1,1},{2,2},{3,3},{4,8},{5,9},{6,10},{7,11},{8,4},{9,5},{10,... | collective-permute-start | bytes 1178120 | tf_op jit(solution)/shard_map/ppermute | solution.py:569
  16.5 14.1 %collective-permute-start.9 = (bf16[1,256,768]{2,1,0:T(8,128)(2,1)}, bf16[1,256,768]{2,1,0:T(8,128)(2,1)S(1)}, u32[]{:S(2)}, u32[]{:S(2)}) collective-permute-start(bf16[1,256,768]{2,1,0:T(8,128)(2,1)} %get-tuple-element.162.refs_6_.refs_0_), channel_id=1, source_target_pairs={{0,3},{1,2},{2,1},{3,0},{4,7},{5,6},{6,5},{7,4},{8,11},{9,10},{10,... | collective-permute-start | bytes 1179656 | tf_op jit(solution)/shard_map/ppermute | solution.py:569
  20.0 17.9 %collective-permute-start.8 = (bf16[1,256,768]{2,1,0:T(8,128)(2,1)}, bf16[1,256,768]{2,1,0:T(8,128)(2,1)S(1)}, u32[]{:S(2)}, u32[]{:S(2)}) collective-permute-start(bf16[1,256,768]{2,1,0:T(8,128)(2,1)} %get-tuple-element.162.refs_6_.refs_0_), channel_id=1, source_target_pairs={{0,2},{1,3},{2,0},{3,1},{4,6},{5,7},{6,4},{7,5},{8,10},{9,11},{10,... | collective-permute-start | bytes 1179656 | tf_op jit(solution)/shard_map/ppermute | solution.py:569
  20.5 18.5 %collective-permute-start.7 = (bf16[1,256,768]{2,1,0:T(8,128)(2,1)}, bf16[1,256,768]{2,1,0:T(8,128)(2,1)S(1)}, u32[]{:S(2)}, u32[]{:S(2)}) collective-permute-start(bf16[1,256,768]{2,1,0:T(8,128)(2,1)} %get-tuple-element.162.refs_6_.refs_0_), channel_id=1, source_target_pairs={{0,1},{1,0},{2,3},{3,2},{4,5},{5,4},{6,7},{7,6},{8,9},{9,8},{10,11... | collective-permute-start | bytes 1179656 | tf_op jit(solution)/shard_map/ppermute | solution.py:569
  22.5 16.5 %collective-permute-start.4 = (f32[1,1920]{1,0:T(1,128)S(1)}, f32[1,1920]{1,0:T(1,128)S(1)}, u32[]{:S(2)}, u32[]{:S(2)}) collective-permute-start(f32[1,1920]{1,0:T(1,128)S(1)} %concatenate.9), channel_id=1, source_target_pairs={{0,8},{1,9},{2,10},{3,11},{4,12},{5,13},{6,14},{7,15},{8,0},{9,1},... | collective-permute-start | bytes 23048 | tf_op jit(solution)/shard_map/ppermute | solution.py:569
  40.5 21.3 %collective-permute-start.15 = (bf16[192,768]{1,0:T(8,128)(2,1)}, bf16[192,768]{1,0:T(8,128)(2,1)}, u32[]{:S(2)}, u32[]{:S(2)}) collective-permute-start(bf16[192,768]{1,0:T(8,128)(2,1)} %get-tuple-element.153), channel_id=1, source_target_pairs={{0,8},{1,9},{2,10},{3,11},{4,12},{5,13},{6,14},{7,15},{8,0},{9,1},... | collective-permute-start | bytes 884744 | tf_op jit(solution)/shard_map/ppermute | solution.py:569
  40.9 20.8 %collective-permute-start.16 = (bf16[192,768]{1,0:T(8,128)(2,1)}, bf16[192,768]{1,0:T(8,128)(2,1)}, u32[]{:S(2)}, u32[]{:S(2)}) collective-permute-start(bf16[192,768]{1,0:T(8,128)(2,1)} %get-tuple-element.154), channel_id=1, source_target_pairs={{0,16},{1,17},{2,18},{3,19},{4,20},{5,21},{6,22},{7,23},{8,24},{9,... | collective-permute-start | bytes 884744 | tf_op jit(solution)/shard_map/ppermute | solution.py:569
  42.6 19.2 %collective-permute-start.17 = (bf16[192,768]{1,0:T(8,128)(2,1)}, bf16[192,768]{1,0:T(8,128)(2,1)}, u32[]{:S(2)}, u32[]{:S(2)}) collective-permute-start(bf16[192,768]{1,0:T(8,128)(2,1)} %get-tuple-element.155), channel_id=1, source_target_pairs={{0,24},{1,25},{2,26},{3,27},{4,28},{5,29},{6,30},{7,31},{8,16},{9,... | collective-permute-start | bytes 884744 | tf_op jit(solution)/shard_map/ppermute | solution.py:569
  44.2 23.4 %collective-permute-start.23 = (bf16[256,767]{1,0:T(8,128)(2,1)}, bf16[256,767]{1,0:T(8,128)(2,1)S(1)}, u32[]{:S(2)}, u32[]{:S(2)}) collective-permute-start(bf16[256,767]{1,0:T(8,128)(2,1)} %param.23), channel_id=1, source_target_pairs={{0,0},{1,1},{2,2},{3,3},{4,8},{5,9},{6,10},{7,11},{8,4},{9,5},{10,... | collective-permute-start | bytes 1178120 | tf_op jit(solution)/shard_map/ppermute | solution.py:569
  61.8 12.6 %all-to-all-start = ((bf16[8,192,128]{2,1,0:T(8,128)(2,1)}), bf16[8,192,128]{2,1,0:T(8,128)(2,1)S(1)}, u32[]{:S(2)}, u32[]{:S(2)}) async-start(bf16[8,192,128]{2,1,0:T(8,128)(2,1)} %get-tuple-element.156.out_ref), calls=%async_computation | async-start | bytes 786432 | tf_op jit(solution)/shard_map/all_to_all | solution.py:592
  68.0 12.0 %collective-permute-start.25 = (bf16[256,768]{1,0:T(8,128)(2,1)S(1)}, bf16[256,768]{1,0:T(8,128)(2,1)S(1)}, u32[]{:S(2)}, u32[]{:S(2)}) collective-permute-start(bf16[256,768]{1,0:T(8,128)(2,1)S(1)} %fusion.refs_4_), channel_id=1, source_target_pairs={{0,16},{1,17},{2,18},{3,19},{4,20},{5,21},{6,22},{7,23},{8,24},{9,... | collective-permute-start | bytes 1179656 | tf_op jit(solution)/shard_map/ppermute | solution.py:569
  125.3 12.1 %collective-permute-start.29 = (bf16[2,8,32,768]{3,2,1,0:T(8,128)(2,1)}, bf16[2,8,32,768]{3,2,1,0:T(8,128)(2,1)S(1)}, u32[]{:S(2)}, u32[]{:S(2)}) collective-permute-start(bf16[2,8,32,768]{3,2,1,0:T(8,128)(2,1)} %get-tuple-element.201), channel_id=1, source_target_pairs={{0,8},{1,9},{2,10},{3,11},{4,12},{5,13},{6,14},{7,15},{8,0},{9,1},... | collective-permute-start | bytes 2359304 | tf_op jit(solution)/shard_map/ppermute | solution.py:569
  128.7 35.1 %collective-permute-start.31 = (bf16[2,192,768]{2,1,0:T(8,128)(2,1)}, bf16[2,192,768]{2,1,0:T(8,128)(2,1)S(1)}, u32[]{:S(2)}, u32[]{:S(2)}) collective-permute-start(bf16[2,192,768]{2,1,0:T(8,128)(2,1)} %get-tuple-element.215), channel_id=1, source_target_pairs={{0,1},{1,0},{2,3},{3,2},{4,5},{5,4},{6,7},{7,6},{8,9},{9,8},{10,11... | collective-permute-start | bytes 1769480 | tf_op jit(solution)/shard_map/ppermute | solution.py:569
  130.6 33.2 %collective-permute-start.32 = (bf16[2,192,768]{2,1,0:T(8,128)(2,1)}, bf16[2,192,768]{2,1,0:T(8,128)(2,1)S(1)}, u32[]{:S(2)}, u32[]{:S(2)}) collective-permute-start(bf16[2,192,768]{2,1,0:T(8,128)(2,1)} %get-tuple-element.216), channel_id=1, source_target_pairs={{0,2},{1,3},{2,0},{3,1},{4,6},{5,7},{6,4},{7,5},{8,10},{9,11},{10,... | collective-permute-start | bytes 1769480 | tf_op jit(solution)/shard_map/ppermute | solution.py:569
  132.1 31.8 %collective-permute-start.33 = (bf16[2,192,768]{2,1,0:T(8,128)(2,1)}, bf16[2,192,768]{2,1,0:T(8,128)(2,1)S(1)}, u32[]{:S(2)}, u32[]{:S(2)}) collective-permute-start(bf16[2,192,768]{2,1,0:T(8,128)(2,1)} %get-tuple-element.217), channel_id=1, source_target_pairs={{0,3},{1,2},{2,1},{3,0},{4,7},{5,6},{6,5},{7,4},{8,11},{9,10},{10,... | collective-permute-start | bytes 1769480 | tf_op jit(solution)/shard_map/ppermute | solution.py:569
  138.7 18.3 %collective-permute-start.30 = (bf16[8,32,768]{2,1,0:T(8,128)(2,1)S(1)}, bf16[8,32,768]{2,1,0:T(8,128)(2,1)S(1)}, u32[]{:S(2)}, u32[]{:S(2)}) collective-permute-start(bf16[8,32,768]{2,1,0:T(8,128)(2,1)S(1)} %slice_bitcast_fusion.3), channel_id=1, source_target_pairs={{0,16},{1,17},{2,18},{3,19},{4,20},{5,21},{6,22},{7,23},{8,24},{9,... | collective-permute-start | bytes 1179656 | tf_op jit(solution)/shard_map/ppermute | solution.py:569
  169.2 29.3 %collective-permute-start.36 = (bf16[2,192,768]{2,1,0:T(8,128)(2,1)S(1)}, bf16[2,192,768]{2,1,0:T(8,128)(2,1)S(1)}, u32[]{:S(2)}, u32[]{:S(2)}) collective-permute-start(bf16[2,192,768]{2,1,0:T(8,128)(2,1)S(1)} %copy-done.3), channel_id=1, source_target_pairs={{0,4},{1,5},{2,6},{3,7},{4,0},{5,1},{6,2},{7,3},{8,12},{9,13},{10,... | collective-permute-start | bytes 1769480 | tf_op jit(solution)/shard_map/ppermute | solution.py:569
  171.5 17.4 %collective-permute-start.35 = (bf16[2,104,576]{2,1,0:T(8,128)(2,1)S(1)}, bf16[2,104,576]{2,1,0:T(8,128)(2,1)S(1)}, u32[]{:S(2)}, u32[]{:S(2)}) collective-permute-start(bf16[2,104,576]{2,1,0:T(8,128)(2,1)S(1)} %get-tuple-element.228), channel_id=1, source_target_pairs={{0,16},{1,17},{2,18},{3,19},{4,20},{5,21},{6,22},{7,23},{8,24},{9,... | collective-permute-start | bytes 718856 | tf_op jit(solution)/shard_map/ppermute | solution.py:569
  172.1 15.2 %collective-permute-start.38 = (bf16[2,32,768]{2,1,0:T(8,128)(2,1)S(1)}, bf16[2,32,768]{2,1,0:T(8,128)(2,1)S(1)}, u32[]{:S(2)}, u32[]{:S(2)}) collective-permute-start(bf16[2,32,768]{2,1,0:T(8,128)(2,1)S(1)} %get-tuple-element.231), channel_id=1, source_target_pairs={{0,2},{1,3},{2,0},{3,1},{4,6},{5,7},{6,4},{7,5},{8,10},{9,11},{10,... | collective-permute-start | bytes 294920 | tf_op jit(solution)/shard_map/ppermute | solution.py:569
  173.5 15.5 %collective-permute-start.39 = (bf16[2,32,768]{2,1,0:T(8,128)(2,1)S(1)}, bf16[2,32,768]{2,1,0:T(8,128)(2,1)S(1)}, u32[]{:S(2)}, u32[]{:S(2)}) collective-permute-start(bf16[2,32,768]{2,1,0:T(8,128)(2,1)S(1)} %get-tuple-element.232), channel_id=1, source_target_pairs={{0,3},{1,2},{2,1},{3,0},{4,7},{5,6},{6,5},{7,4},{8,11},{9,10},{10,... | collective-permute-start | bytes 294920 | tf_op jit(solution)/shard_map/ppermute | solution.py:569
  205.3 13.3 %collective-permute-start.53 = (bf16[2,32,768]{2,1,0:T(8,128)(2,1)S(1)}, bf16[2,32,768]{2,1,0:T(8,128)(2,1)S(1)}, u32[]{:S(2)}, u32[]{:S(2)}) collective-permute-start(bf16[2,32,768]{2,1,0:T(8,128)(2,1)S(1)} %add_add_fusion), channel_id=1, source_target_pairs={{0,4},{1,5},{2,6},{3,7},{4,0},{5,1},{6,2},{7,3},{8,12},{9,13},{10,... | collective-permute-start | bytes 294920 | tf_op jit(solution)/shard_map/ppermute | solution.py:569
  205.3 18.9 %collective-permute-start.52 = (bf16[2,104,576]{2,1,0:T(8,128)(2,1)S(1)}, bf16[2,104,576]{2,1,0:T(8,128)(2,1)S(1)}, u32[]{:S(2)}, u32[]{:S(2)}) collective-permute-start(bf16[2,104,576]{2,1,0:T(8,128)(2,1)S(1)} %add.131), channel_id=1, source_target_pairs={{0,4},{1,5},{2,6},{3,7},{4,0},{5,1},{6,2},{7,3},{8,12},{9,13},{10,... | collective-permute-start | bytes 718856 | tf_op jit(solution)/shard_map/ppermute | solution.py:569
  208.7 26.1 %collective-permute-start.50 = (bf16[2,96,768]{2,1,0:T(8,128)(2,1)S(1)}, bf16[2,96,768]{2,1,0:T(8,128)(2,1)S(1)}, u32[]{:S(2)}, u32[]{:S(2)}) collective-permute-start(bf16[2,96,768]{2,1,0:T(8,128)(2,1)S(1)} %get-tuple-element.285.own), channel_id=1, source_target_pairs={{0,2},{1,3},{2,0},{3,1},{4,6},{5,7},{6,4},{7,5},{8,10},{9,11},{10,... | collective-permute-start | bytes 884744 | tf_op jit(solution)/shard_map/ppermute | solution.py:569
  210.5 20.5 %collective-permute-start.47 = (bf16[2,256,768]{2,1,0:T(8,128)(2,1)S(1)}, bf16[2,256,768]{2,1,0:T(8,128)(2,1)S(1)}, u32[]{:S(2)}, u32[]{:S(2)}) collective-permute-start(bf16[2,256,768]{2,1,0:T(8,128)(2,1)S(1)} %get-tuple-element.270), channel_id=1, source_target_pairs={{0,1},{1,0},{2,3},{3,2},{4,5},{5,4},{6,7},{7,6},{8,9},{9,8},{10,11... | collective-permute-start | bytes 2359304 | tf_op jit(solution)/shard_map/ppermute | solution.py:569
  210.6 22.6 %collective-permute-start.44 = (bf16[2,256,768]{2,1,0:T(8,128)(2,1)S(1)}, bf16[2,256,768]{2,1,0:T(8,128)(2,1)S(1)}, u32[]{:S(2)}, u32[]{:S(2)}) collective-permute-start(bf16[2,256,768]{2,1,0:T(8,128)(2,1)S(1)} %copy-done.47), channel_id=1, source_target_pairs={{0,8},{1,9},{2,10},{3,11},{4,12},{5,13},{6,14},{7,15},{8,0},{9,1},... | collective-permute-start | bytes 2359304 | tf_op jit(solution)/shard_map/ppermute | solution.py:569
  224.4 14.5 %collective-permute-start.54 = (bf16[2,120,768]{2,1,0:T(8,128)(2,1)S(1)}, bf16[2,120,768]{2,1,0:T(8,128)(2,1)S(1)}, u32[]{:S(2)}, u32[]{:S(2)}) collective-permute-start(bf16[2,120,768]{2,1,0:T(8,128)(2,1)S(1)} %fusion.10.own), channel_id=1, source_target_pairs={{0,1},{1,0},{2,3},{3,2},{4,5},{5,4},{6,7},{7,6},{8,9},{9,8},{10,11... | collective-permute-start | bytes 1105928 | tf_op jit(solution)/shard_map/ppermute | solution.py:569
  234.1 13.8 %collective-permute-start.45 = (bf16[256,768]{1,0:T(8,128)(2,1)}, bf16[256,768]{1,0:T(8,128)(2,1)}, u32[]{:S(2)}, u32[]{:S(2)}) collective-permute-start(bf16[256,768]{1,0:T(8,128)(2,1)} %fusion.2), channel_id=1, source_target_pairs={{0,16},{1,17},{2,18},{3,19},{4,20},{5,21},{6,22},{7,23},{8,24},{9,... | collective-permute-start | bytes 1179656 | tf_op jit(solution)/shard_map/ppermute | solution.py:569
  235.7 16.6 %collective-permute-start.51 = (bf16[2,2,96,768]{3,2,1,0:T(8,128)(2,1)}, bf16[2,2,96,768]{3,2,1,0:T(8,128)(2,1)}, u32[]{:S(2)}, u32[]{:S(2)}) collective-permute-start(bf16[2,2,96,768]{3,2,1,0:T(8,128)(2,1)} %pad_maximum_fusion.1), channel_id=1, source_target_pairs={{0,1},{1,0},{2,3},{3,2},{4,5},{5,4},{6,7},{7,6},{8,9},{9,8},{10,11... | collective-permute-start | bytes 1769480 | tf_op jit(solution)/shard_map/ppermute | solution.py:569
  235.8 30.6 %collective-permute-start.57 = (bf16[2,2,104,576]{3,2,1,0:T(8,128)(2,1)S(1)}, bf16[2,2,104,576]{3,2,1,0:T(8,128)(2,1)}, u32[]{:S(2)}, u32[]{:S(2)}) collective-permute-start(bf16[2,2,104,576]{3,2,1,0:T(8,128)(2,1)S(1)} %pad_maximum_fusion.2), channel_id=1, source_target_pairs={{0,1},{1,0},{2,3},{3,2},{4,5},{5,4},{6,7},{7,6},{8,9},{9,8},{10,11... | collective-permute-start | bytes 1437704 | tf_op jit(solution)/shard_map/ppermute | solution.py:569
  239.9 22.5 %collective-permute-start.55 = (bf16[2,2,120,768]{3,2,1,0:T(8,128)(2,1)}, bf16[2,2,120,768]{3,2,1,0:T(8,128)(2,1)S(1)}, u32[]{:S(2)}, u32[]{:S(2)}) collective-permute-start(bf16[2,2,120,768]{3,2,1,0:T(8,128)(2,1)} %pad_maximum_fusion), channel_id=1, source_target_pairs={{0,2},{1,3},{2,0},{3,1},{4,6},{5,7},{6,4},{7,5},{8,10},{9,11},{10,... | collective-permute-start | bytes 2211848 | tf_op jit(solution)/shard_map/ppermute | solution.py:569
  246.2 26.3 %collective-permute-start.49 = (bf16[256,767]{1,0:T(8,128)(2,1)}, bf16[256,767]{1,0:T(8,128)(2,1)S(1)}, u32[]{:S(2)}, u32[]{:S(2)}) collective-permute-start(bf16[256,767]{1,0:T(8,128)(2,1)} %stream_back.1), channel_id=1, source_target_pairs={{0,0},{1,1},{2,2},{3,3},{4,8},{5,9},{6,10},{7,11},{8,4},{9,5},{10,... | collective-permute-start | bytes 1178120 | tf_op jit(solution)/shard_map/ppermute | solution.py:569
  249.4 24.0 %collective-permute-start.46 = (bf16[256,767]{1,0:T(8,128)(2,1)S(1)}, bf16[256,767]{1,0:T(8,128)(2,1)S(1)}, u32[]{:S(2)}, u32[]{:S(2)}) collective-permute-start(bf16[256,767]{1,0:T(8,128)(2,1)S(1)} %fusion.1), channel_id=1, source_target_pairs={{0,0},{1,1},{2,2},{3,3},{4,8},{5,9},{6,10},{7,11},{8,4},{9,5},{10,... | collective-permute-start | bytes 1178120 | tf_op jit(solution)/shard_map/ppermute | solution.py:569
  (87 other events, 652.6 us)
